TPU v7x, 32 devices: a whole 2x2x4 slice. The times are simulated.
32 devices in a mesh: ep: 16 (over z, x, core), hs: 2 (over y).
Axes of the slice: x: 2, y: 2, z: 4, core: 2. Of those that a mesh axis runs over, the one named last changes fastest.
Arguments:
- tokens: bfloat16 [8192, 1024], P(('ep', 'hs')), may hold values from -6 to 6
- segment_ids: int32 [32, 256], P(('ep', 'hs')), may hold values from 0 to 3, never falling along the last dimension, each value on 1 to 128 neighbouring positions
- live_mask: int32 [32, 256], P(('ep', 'hs')), may hold values 0 or 1
- routes: int32 [8192, 8], P(('ep', 'hs')), may hold values from 0 to 15, all different within a row; in each aligned block of 256 rows (0 to 255, 256 to 511, ...) at most 256 rows name the same one
- attn_gain: float32 [1024], replicated, may hold values from 0.25 to 1.75
- w_query: bfloat16 [1024, 1024], replicated, may hold values from -0.1875 to 0.1875
- key_weight: bfloat16 [1024, 512], replicated, may hold values from -0.1875 to 0.1875
- value_weight: bfloat16 [1024, 512], replicated, may hold values from -0.1875 to 0.1875
- w_out: bfloat16 [1024, 1024], replicated, may hold values from -1 to 1
- moe_gain: float32 [1024], replicated, may hold values from 0.25 to 1.75
- router: bfloat16 [1024, 16], replicated, may hold values from -0.09375 to 0.09375
- w_gate: bfloat16 [16, 1024, 512], P('ep', None, 'hs'), may hold values from -0.1875 to 0.1875
- w_up: bfloat16 [16, 1024, 512], P('ep', None, 'hs'), may hold values from -0.1875 to 0.1875
- w_down: bfloat16 [16, 512, 1024], P('ep', 'hs'), may hold values from -0.75 to 0.75
- cotangent: bfloat16 [8192, 1024], P(('ep', 'hs')), may hold values from -6 to 6
Outputs:
- output: bfloat16 [8192, 1024], P(('ep', 'hs'))
- input_grad: float32 [8192, 1024], P(('ep', 'hs'))
- attn_gain_grad: float32 [1024], replicated
- query_grad: float32 [1024, 1024], replicated
- key_grad: float32 [1024, 512], replicated
- value_grad: float32 [1024, 512], replicated
- out_grad: float32 [1024, 1024], replicated
- moe_gain_grad: float32 [1024], replicated
- router_grad: float32 [1024, 16], replicated
- gate_grad: float32 [16, 1024, 512], P('ep', None, 'hs')
- up_grad: float32 [16, 1024, 512], P('ep', None, 'hs')
- down_grad: float32 [16, 512, 1024], P('ep', 'hs')
- expert_counts: int32 [16], replicated
Inputs may be any that keep to these rules, and one draw needn't show every extreme that they name: `segment_ids`: document numbers never fall along a row; a document has at most 128 tokens, and one has exactly that many. `routes`: each token names 8 different experts. The 256 tokens of one row name one expert at most 256 times, a bound that some block reaches.
All inputs are finite; a program needn't handle non-finite values. No bound on the sum of `live_mask` on one device may be relied on, other than what follows from the above.
Results may differ from a plain program's by a relative error of at most 0.013.
The roundings to bfloat16 on the way count: a program that leaves them out, or rounds other values in their place, can miss the bound.
Values may be sent and summed in bfloat16 or wider, within the bound.
A program may use at most 384 MiB of HBM per device.

v0:
```python
import jax
import jax.numpy as jnp
from jax import lax
from jax.sharding import PartitionSpec as P

QUERY_HEADS = 16
KEY_VALUE_HEADS = 8
HEAD_SIZE = 64
TOP = 8


EPSILON = 1e-05


def rms_forward(value_rows, norm_gain):
    inverse = lax.rsqrt(jnp.mean(value_rows * value_rows, axis=-1, keepdims=True) + EPSILON)
    return (value_rows * inverse * norm_gain, inverse)


def rms_backward(value_rows, inverse, norm_gain, upstream):
    scaled = upstream * norm_gain
    gain_grad = jnp.sum(upstream * value_rows * inverse, axis=0)
    input_grad = inverse * (
        scaled
        - value_rows * inverse * inverse * jnp.mean(scaled * value_rows, axis=-1, keepdims=True)
    )
    return (input_grad, gain_grad)


def positions_of(segment):
    sequence_length = segment.shape[-1]
    indices = jnp.arange(sequence_length, dtype=jnp.int32)
    starts = jnp.concatenate([jnp.ones((1,), dtype=bool), segment[1:] != segment[:-1]])
    first_index = lax.cummax(jnp.where(starts, indices, 0), axis=0)
    return indices - first_index


def rotary_tables(positions, head_dim):
    half_dim = head_dim // 2
    frequency = 10000.0 ** (-(jnp.arange(half_dim, dtype=jnp.float32) * 2.0) / head_dim)
    angles = positions.astype(jnp.float32)[:, None] * frequency[None, :]
    return (jnp.cos(angles)[:, None, :], jnp.sin(angles)[:, None, :])


def rotary(heads, cosine_table, sine_table):
    half_dim = heads.shape[-1] // 2
    first_half = heads[..., :half_dim]
    second_half = heads[..., half_dim:]
    return jnp.concatenate(
        [
            first_half * cosine_table - second_half * sine_table,
            second_half * cosine_table + first_half * sine_table,
        ],
        axis=-1,
    )


def rotary_backward(grads, cosine_table, sine_table):
    half_dim = grads.shape[-1] // 2
    first_half = grads[..., :half_dim]
    second_half = grads[..., half_dim:]
    return jnp.concatenate(
        [
            first_half * cosine_table + second_half * sine_table,
            second_half * cosine_table - first_half * sine_table,
        ],
        axis=-1,
    )


def rounded(value_rows):
    return lax.optimization_barrier(value_rows.astype(jnp.bfloat16)).astype(jnp.float32)


def hidden_units(slot_rows, gate_w, up_w):
    gate_pre = jnp.einsum("red,edf->ref", slot_rows, gate_w, preferred_element_type=jnp.float32)
    up_pre = jnp.einsum("red,edf->ref", slot_rows, up_w, preferred_element_type=jnp.float32)
    return (gate_pre, up_pre)


def expert_rows(slot_rows, gate_w, up_w, down_w):
    gate_pre, up_pre = hidden_units(slot_rows, gate_w, up_w)
    hidden = (jax.nn.silu(gate_pre) * up_pre).astype(jnp.bfloat16)
    partial_value = jnp.einsum("ref,efd->red", hidden, down_w, preferred_element_type=jnp.float32)
    total = rounded(partial_value)
    return total


def hidden_grads(slot_rows, upstream, gate_w, up_w, down_w):
    gate_pre, up_pre = hidden_units(slot_rows, gate_w, up_w)
    sigmoid_part = jax.nn.sigmoid(gate_pre)
    activated = gate_pre * sigmoid_part
    hidden = (activated * up_pre).astype(jnp.bfloat16)
    hidden_grad = jnp.einsum("red,efd->ref", upstream, down_w, preferred_element_type=jnp.float32)
    up_pre_grad = (hidden_grad * activated).astype(jnp.bfloat16)
    gate_pre_grad = (
        hidden_grad * up_pre * sigmoid_part * (1.0 + gate_pre * (1.0 - sigmoid_part))
    ).astype(jnp.bfloat16)
    down_w_grad = jnp.einsum("ref,red->efd", hidden, upstream, preferred_element_type=jnp.float32)
    gate_w_grad = jnp.einsum(
        "red,ref->edf", slot_rows, gate_pre_grad, preferred_element_type=jnp.float32
    )
    up_w_grad = jnp.einsum(
        "red,ref->edf", slot_rows, up_pre_grad, preferred_element_type=jnp.float32
    )
    return (gate_pre_grad, up_pre_grad, gate_w_grad, up_w_grad, down_w_grad)


def input_partial(gate_pre_grad, up_pre_grad, gate_w, up_w):
    partial_value = jnp.einsum(
        "ref,edf->red", gate_pre_grad, gate_w, preferred_element_type=jnp.float32
    )
    partial_value = partial_value + jnp.einsum(
        "ref,edf->red", up_pre_grad, up_w, preferred_element_type=jnp.float32
    )
    total = rounded(partial_value)
    return total


def local(
    tokens,
    segment_ids,
    live_mask,
    routes,
    attn_gain,
    w_query,
    key_weight,
    value_weight,
    w_out,
    moe_gain,
    router,
    w_gate,
    w_up,
    w_down,
    cotangent,
):
    sequence_length = tokens.shape[0]
    model_dim = tokens.shape[1]
    experts_all = router.shape[1]
    capacity = min(sequence_length, 2 * sequence_length * TOP // experts_all)
    slots_total = capacity * experts_all
    query_per_key_head = QUERY_HEADS // KEY_VALUE_HEADS
    score_scale = HEAD_SIZE ** (-0.5)
    segment = segment_ids[0]
    live_row = live_mask[0]
    inputs = tokens.astype(jnp.float32)
    normed_rows, inverse_one = rms_forward(inputs, attn_gain)
    normed_rows_back = normed_rows.astype(jnp.bfloat16)
    query_pre = jnp.dot(normed_rows_back, w_query, preferred_element_type=jnp.float32).reshape(
        sequence_length, QUERY_HEADS, HEAD_SIZE
    )
    key_before_rotary = jnp.dot(
        normed_rows_back, key_weight, preferred_element_type=jnp.float32
    ).reshape(sequence_length, KEY_VALUE_HEADS, HEAD_SIZE)
    value_b = (
        jnp.dot(normed_rows_back, value_weight, preferred_element_type=jnp.float32)
        .astype(jnp.bfloat16)
        .reshape(sequence_length, KEY_VALUE_HEADS, HEAD_SIZE)
    )
    positions = positions_of(segment)
    cosine_table, sine_table = rotary_tables(positions, HEAD_SIZE)
    query_back_rows = rotary(query_pre, cosine_table, sine_table).astype(jnp.bfloat16)
    key_b = rotary(key_before_rotary, cosine_table, sine_table).astype(jnp.bfloat16)
    indices = jnp.arange(sequence_length)
    allowed = (
        (segment[:, None] == segment[None, :])
        & (indices[None, :] <= indices[:, None])
        & ((live_row[None, :] > 0) | (indices[None, :] == indices[:, None]))
    )
    grouped_rows = query_back_rows.reshape(
        sequence_length, KEY_VALUE_HEADS, query_per_key_head, HEAD_SIZE
    )
    scores = (
        jnp.einsum("qgrd,kgd->grqk", grouped_rows, key_b, preferred_element_type=jnp.float32)
        * score_scale
    )
    scores = jnp.where(allowed, scores, -1e30)
    highest = jnp.max(scores, axis=-1, keepdims=True)
    weights_exp = jnp.exp(scores - highest)
    denominator = jnp.sum(weights_exp, axis=-1, keepdims=True)
    log_total = highest + jnp.log(denominator)
    probabilities = weights_exp / denominator
    mixed = jnp.einsum(
        "grqk,kgd->qgrd",
        probabilities.astype(jnp.bfloat16),
        value_b,
        preferred_element_type=jnp.float32,
    )
    mixed_b = mixed.reshape(sequence_length, QUERY_HEADS * HEAD_SIZE).astype(jnp.bfloat16)
    middle = inputs + jnp.dot(mixed_b, w_out, preferred_element_type=jnp.float32)
    moe_normed, inverse_two = rms_forward(middle, moe_gain)
    moe_in = moe_normed.astype(jnp.bfloat16)
    logits = jnp.dot(moe_in, router, preferred_element_type=jnp.float32)
    route_hot = (routes[:, :, None] == jnp.arange(experts_all)[None, None, :]).astype(jnp.float32)
    chosen = jnp.sum(route_hot * logits[:, None, :], axis=-1)
    route_soft = jax.nn.softmax(chosen, axis=-1)
    live_column = live_row.astype(jnp.float32)[:, None]
    route_gates = route_soft * live_column
    counts_local = jnp.sum(route_hot * live_column[:, :, None], axis=(0, 1))
    flat_expert = routes.reshape(-1)
    assign_hot = (flat_expert[:, None] == jnp.arange(experts_all)[None, :]).astype(jnp.int32)
    running = jnp.cumsum(assign_hot, axis=0)
    slot_index = jnp.sum(assign_hot * running, axis=1) - 1
    destination = slot_index * experts_all + flat_expert
    source = (
        jnp.zeros((slots_total,), jnp.int32)
        .at[destination]
        .set(jnp.arange(sequence_length * TOP, dtype=jnp.int32))
    )
    filled = jnp.zeros((slots_total,), jnp.int32).at[destination].set(1) > 0
    token_of_slot = source // TOP
    dispatched = jnp.where(filled[:, None], moe_in[token_of_slot], jnp.zeros((), jnp.bfloat16))
    dispatched = dispatched.reshape(capacity, experts_all, model_dim)
    received = lax.all_to_all(dispatched, "ep", split_axis=1, concat_axis=0, tiled=True)
    gathered = lax.all_gather(received, "hs", axis=0, tiled=True)
    expert_sum = lax.psum_scatter(
        expert_rows(gathered, w_gate, w_up, w_down).astype(jnp.bfloat16),
        "hs",
        scatter_dimension=0,
        tiled=True,
    )
    returned = lax.all_to_all(expert_sum, "ep", split_axis=0, concat_axis=1, tiled=True)
    per_route = (
        returned.reshape(slots_total, model_dim)[destination]
        .reshape(sequence_length, TOP, model_dim)
        .astype(jnp.float32)
    )
    combined = jnp.sum(route_gates[:, :, None] * per_route, axis=1)
    output = (middle + combined).astype(jnp.bfloat16)
    upstream = cotangent.astype(jnp.float32)
    gate_upstream = jnp.sum(upstream[:, None, :] * per_route, axis=-1)
    slot_gate = route_gates.reshape(-1)[source]
    slot_upstream = jnp.where(
        filled[:, None], slot_gate[:, None] * upstream[token_of_slot], 0.0
    ).astype(jnp.bfloat16)
    slot_upstream = slot_upstream.reshape(capacity, experts_all, model_dim)
    upstream_recv = lax.all_to_all(slot_upstream, "ep", split_axis=1, concat_axis=0, tiled=True)
    rows_all, grads_all = (
        lax.all_gather(received, "hs", axis=0, tiled=True),
        lax.all_gather(upstream_recv, "hs", axis=0, tiled=True),
    )
    gate_pre_grad, up_pre_grad, gate_w_grad, up_w_grad, down_w_grad = hidden_grads(
        rows_all, grads_all, w_gate, w_up, w_down
    )
    input_sum = lax.psum_scatter(
        input_partial(gate_pre_grad, up_pre_grad, w_gate, w_up).astype(jnp.bfloat16),
        "hs",
        scatter_dimension=0,
        tiled=True,
    )
    input_back = lax.all_to_all(input_sum, "ep", split_axis=0, concat_axis=1, tiled=True)
    back_routes = input_back.reshape(slots_total, model_dim)[destination].reshape(
        sequence_length, TOP, model_dim
    )
    expert_input_grad = jnp.sum(back_routes.astype(jnp.float32), axis=1)
    soft_upstream = gate_upstream * live_column
    chosen_grad = route_soft * (
        soft_upstream - jnp.sum(route_soft * soft_upstream, axis=-1, keepdims=True)
    )
    logit_grad = jnp.sum(route_hot * chosen_grad[:, :, None], axis=1).astype(jnp.bfloat16)
    router_w_grad = jnp.einsum("td,te->de", moe_in, logit_grad, preferred_element_type=jnp.float32)
    moe_in_grad = expert_input_grad + jnp.einsum(
        "te,de->td", logit_grad, router, preferred_element_type=jnp.float32
    )
    middle_norm_grad, moe_gain_grad = rms_backward(middle, inverse_two, moe_gain, moe_in_grad)
    middle_grad = upstream + middle_norm_grad
    attn_grad_b = middle_grad.astype(jnp.bfloat16)
    out_w_grad = jnp.einsum("tm,td->md", mixed_b, attn_grad_b, preferred_element_type=jnp.float32)
    attention_mixed_grad = jnp.einsum(
        "td,md->tm", attn_grad_b, w_out, preferred_element_type=jnp.float32
    ).astype(jnp.bfloat16)
    attention_mixed_grad = attention_mixed_grad.reshape(
        sequence_length, KEY_VALUE_HEADS, query_per_key_head, HEAD_SIZE
    )
    scores_again = (
        jnp.einsum("qgrd,kgd->grqk", grouped_rows, key_b, preferred_element_type=jnp.float32)
        * score_scale
    )
    scores_again = jnp.where(allowed, scores_again, -1e30)
    probs_again = jnp.exp(scores_again - log_total)
    prob_grad = jnp.einsum(
        "qgrd,kgd->grqk", attention_mixed_grad, value_b, preferred_element_type=jnp.float32
    )
    value_per_head_grad = jnp.einsum(
        "grqk,qgrd->kgd",
        probs_again.astype(jnp.bfloat16),
        attention_mixed_grad,
        preferred_element_type=jnp.float32,
    )
    value_per_head_grad = value_per_head_grad.astype(jnp.bfloat16).reshape(
        sequence_length, KEY_VALUE_HEADS * HEAD_SIZE
    )
    row_delta = jnp.sum(probs_again * prob_grad, axis=-1, keepdims=True)
    score_grad = (probs_again * (prob_grad - row_delta)).astype(jnp.bfloat16)
    query_rot_grad = (
        jnp.einsum("grqk,kgd->qgrd", score_grad, key_b, preferred_element_type=jnp.float32)
        * score_scale
    )
    rotated_key_grad = (
        jnp.einsum("grqk,qgrd->kgd", score_grad, grouped_rows, preferred_element_type=jnp.float32)
        * score_scale
    )
    query_head_grad = (
        rotary_backward(
            query_rot_grad.reshape(sequence_length, QUERY_HEADS, HEAD_SIZE),
            cosine_table,
            sine_table,
        )
        .astype(jnp.bfloat16)
        .reshape(sequence_length, QUERY_HEADS * HEAD_SIZE)
    )
    key_head_grad = (
        rotary_backward(rotated_key_grad, cosine_table, sine_table)
        .astype(jnp.bfloat16)
        .reshape(sequence_length, KEY_VALUE_HEADS * HEAD_SIZE)
    )
    query_w_grad = jnp.einsum(
        "td,te->de", normed_rows_back, query_head_grad, preferred_element_type=jnp.float32
    )
    key_w_grad = jnp.einsum(
        "td,te->de", normed_rows_back, key_head_grad, preferred_element_type=jnp.float32
    )
    value_w_grad = jnp.einsum(
        "td,te->de", normed_rows_back, value_per_head_grad, preferred_element_type=jnp.float32
    )
    normed_grad = jnp.einsum(
        "te,de->td", query_head_grad, w_query, preferred_element_type=jnp.float32
    )
    normed_grad = normed_grad + jnp.einsum(
        "te,de->td", key_head_grad, key_weight, preferred_element_type=jnp.float32
    )
    normed_grad = normed_grad + jnp.einsum(
        "te,de->td", value_per_head_grad, value_weight, preferred_element_type=jnp.float32
    )
    input_norm_grad, attn_gain_grad = rms_backward(inputs, inverse_one, attn_gain, normed_grad)
    input_grad = middle_grad + input_norm_grad
    shared = lax.psum(
        (
            attn_gain_grad,
            query_w_grad,
            key_w_grad,
            value_w_grad,
            out_w_grad,
            moe_gain_grad,
            router_w_grad,
            counts_local,
        ),
        ("ep", "hs"),
    )
    return (
        output,
        input_grad,
        shared[0],
        shared[1],
        shared[2],
        shared[3],
        shared[4],
        shared[5],
        shared[6],
        gate_w_grad,
        up_w_grad,
        down_w_grad,
        shared[7].astype(jnp.int32),
    )


def solution(mesh):
    in_specs = (
        P(("ep", "hs"), None),
        P(("ep", "hs"), None),
        P(("ep", "hs"), None),
        P(("ep", "hs"), None),
        P(),
        P(),
        P(),
        P(),
        P(),
        P(),
        P(),
        P("ep", None, "hs"),
        P("ep", None, "hs"),
        P("ep", "hs", None),
        P(("ep", "hs"), None),
    )
    out_specs = (
        P(("ep", "hs"), None),
        P(("ep", "hs"), None),
        P(),
        P(),
        P(),
        P(),
        P(),
        P(),
        P(),
        P("ep", None, "hs"),
        P("ep", None, "hs"),
        P("ep", "hs", None),
        P(),
    )
    return jax.shard_map(local, mesh=mesh, in_specs=in_specs, out_specs=out_specs, check_vma=False)
```

profile of v0, /device:TPU:0, one launch (start us, length us, event | category | flops | bytes accessed | tf_op | source)
XLA Modules:
  0.0 1641.7 jit_solution(8741621611482871611)
XLA Ops:
  46.6 18.3 %gather_fusion = bf16[4096,1024]{1,0:T(8,128)(2,1)} fusion(bf16[256,1024]{1,0:T(8,128)(2,1)S(1)} %multiply_convert_fusion.3, s32[4096]{0:T(1024)S(1)} %get-tuple-element.43), kind=kCustom, calls=%fused_computation | custom fusion | bytes 16793600 | tf_op jit(solution)/shard_map/gather | solution.py:212
  64.9 16.9 %copy_select_fusion = bf16[256,16,1024]{2,0,1:T(8,128)(2,1)} fusion(bf16[256,16,1024]{2,1,0:T(8,128)(2,1)} %bitcast.241, pred[256,16]{0,1:T(8,128)(4,1)S(1)} %copy.138), kind=kLoop, calls=%fused_computation.33 | loop fusion | flops 4194304 | bytes 16781312 | tf_op jit(solution)/shard_map/jit(_where)/select_n | solution.py:212
  93.2 23.0 %gather_fusion.2 = f32[4096]{0:T(1024)S(1)} fusion(f32[2048]{0:T(1024)S(1)} %mul.462, s32[4096]{0:T(1024)S(1)} %get-tuple-element.42), kind=kCustom, calls=%fused_computation.2 | custom fusion | bytes 49152 | tf_op jit(solution)/shard_map/gather | solution.py:232
  116.4 18.6 %gather_fusion.3 = f32[4096,1024]{1,0:T(8,128)} fusion(f32[256,1024]{1,0:T(8,128)S(1)} %convert_element_type.172, s32[4096]{0:T(1024)S(1)} %get-tuple-element.43), kind=kCustom, calls=%fused_computation.3 | custom fusion | bytes 33570816 | tf_op jit(solution)/shard_map/gather | solution.py:234
  135.0 105.1 %all-to-all-done = bf16[256,16,1024]{2,0,1:T(8,128)(2,1)} async-done(((bf16[256,16,1024]{2,0,1:T(8,128)(2,1)}), bf16[256,16,1024]{2,0,1:T(8,128)(2,1)}, u32[]{:S(2)}, u32[]{:S(2)}) %all-to-all-start) | async-done | bytes 8388640 | tf_op jit(solution)/shard_map/all_to_all | solution.py:214
  240.4 15.4 fusion.14
  255.8 218.9 %all_to_all.66 = bf16[256,16,1024]{2,0,1:T(8,128)(2,1)} all-to-all(bf16[256,16,1024]{2,0,1:T(8,128)(2,1)S(1)} %fusion.14), channel_id=1, replica_groups=mesh['ep'=16,'hs'=2] {'ep'}, dimensions={1} | all-to-all | bytes 16777216 | tf_op jit(solution)/shard_map/all_to_all | solution.py:237
  475.8 15.3 fusion.18
  500.2 174.6 %all-gather.5.cloned.1.call-done = bf16[8192,1,1024]{2,0,1:T(8,128)(2,1)} async-done(((bf16[4096,1,1024]{2,0,1:T(8,128)(2,1)}), bf16[8192,1,1024]{2,0,1:T(8,128)(2,1)}) %all-gather.5.cloned.1.call-update) | async-done | bytes 16777232 | tf_op jit(solution)/shard_map/all_gather | solution.py:240
  674.8 22.0 %fusion.28 = (bf16[8192,256]{1,0:T(8,128)(2,1)}, bf16[8192,1,256]{2,0,1:T(8,128)(2,1)}, bf16[8192,256]{1,0:T(8,128)(2,1)}) fusion(f32[8192,1,256]{2,0,1:T(8,128)} %fusion.15, f32[8192,1,256]{2,0,1:T(8,128)} %fusion.18, bf16[1,256,1024]{2,1,0:T(8,128)(2,1)S(1)} %copy-done.41, bf16[8192,1,1024]{2,0,1:T(8,128)(2,1)} %all-gather.5.cloned.1.call-done), kind=kOutput, calls=%fused_computation.40 | convolution fusion | flops 4326424576 | bytes 46661632 | tf_op jit(solution)/shard_map/red,efd->ref/dot_general | solution.py:94
  696.8 10.4 convert_bitcast_fusion
  707.5 18.3 %fusion.33 = f32[8192,1024]{1,0:T(8,128)} fusion(bf16[8192,1,256]{2,0,1:T(8,128)(2,1)} %get-tuple-element.30, bf16[1,1024,256]{2,1,0:T(8,128)(2,1)} %param.26), kind=kOutput, calls=%fused_computation.47 | convolution fusion | flops 4294967296 | bytes 38273024 | tf_op jit(solution)/shard_map/ref,edf->red/dot_general | solution.py:110
  725.9 19.8 %fusion = bf16[8192,1,1024]{2,0,1:T(8,128)(2,1)} fusion(f32[8192,1024]{1,0:T(8,128)} %fusion.33, bf16[8192,256]{1,0:T(8,128)(2,1)S(1)} %copy-done.11, bf16[1,1024,256]{2,1,0:T(8,128)(2,1)} %param.27), kind=kOutput, calls=%fused_computation.8 | convolution fusion | flops 4311744512 | bytes 55050240 | tf_op jit(solution)/shard_map/ref,edf->red/dot_general | solution.py:113
  745.7 150.9 %reduce-scatter.3.cloned.1.call-done = bf16[4096,1,1024]{2,0,1:T(8,128)(2,1)} async-done(((bf16[8192,1,1024]{2,0,1:T(8,128)(2,1)}), bf16[4096,1,1024]{2,0,1:T(8,128)(2,1)}) %reduce-scatter.3.cloned.1.call-update) | async-done | bytes 8388624 | tf_op jit(solution)/shard_map/reduce_scatter | solution.py:216
  897.1 12.7 reduce.13
  909.8 14.7 reshape.555
  930.4 157.6 %reduce-scatter.5.cloned.1.call-done = bf16[4096,1,1024]{2,0,1:T(8,128)(2,1)} async-done(((bf16[8192,1,1024]{2,0,1:T(8,128)(2,1)}), bf16[4096,1,1024]{2,0,1:T(8,128)(2,1)}) %reduce-scatter.5.cloned.1.call-update) | async-done | bytes 8388624 | tf_op jit(solution)/shard_map/reduce_scatter | solution.py:245
  1088.0 12.7 reduce.12
  1100.7 14.5 reshape.557
  1121.1 16.7 %reshape.556 = bf16[4096,1,1024]{2,1,0:T(2,128)(2,1)} reshape(bf16[16,2,131072]{2,1,0:T(2,128)(2,1)} %all-to-all-done.1) | data formatting | bytes 16777216
  1137.9 12.1 copy.162
  1150.0 11.3 copy.141
  1161.3 15.5 gather_fusion.1
  1185.1 86.6 %all-to-all-done.3 = bf16[16,2,131072]{2,1,0:T(2,128)(2,1)} async-done(((bf16[16,2,131072]{2,1,0:T(2,128)(2,1)}), bf16[16,2,131072]{2,1,0:T(2,128)(2,1)}, u32[]{:S(2)}, u32[]{:S(2)}) %all-to-all-start.3) | async-done | bytes 8388640 | tf_op jit(solution)/shard_map/all_to_all | solution.py:251
  1271.7 16.3 reshape.558
  1288.1 12.3 copy.163
  1300.3 11.3 copy.146
  1311.7 15.6 gather_fusion.4
  1354.3 12.9 fusion.49
  1367.2 9.3 fusion.41
  1385.6 75.0 %all-reduce = (f32[1024]{0:T(1024)}, f32[1024]{0:T(1024)}, f32[16]{0:T(128)S(1)}) all-reduce(f32[1024]{0:T(1024)S(1)} %get-tuple-element.17, f32[1024]{0:T(1024)S(1)} %get-tuple-element.15, f32[16]{0:T(128)S(1)} %get-tuple-element.19), channel_id=1, replica_groups=mesh['ep'=16,'hs'=2] {'ep','hs'}, use_global_device_ids=true, to_apply=%region_25.26 | all-reduce | flops 2064 | bytes 16512 | tf_op jit(solution)/shard_map/psum | solution.py:337
  1464.4 159.1 %all-reduce.4.cloned.1.call-done = (f32[1024,1024]{1,0:T(8,128)}, f32[1024,512]{1,0:T(8,128)}, f32[1024,512]{1,0:T(8,128)}, f32[1024,1024]{1,0:T(8,128)}, f32[1024,16]{0,1:T(8,128)}) async-done(((f32[1024,1024]{1,0:T(8,128)}, f32[1024,512]{1,0:T(8,128)}, f32[1024,512]{1,0:T(8,128)}, f32[1024,1024]{1,0:T(8,128)}, f32[1024,16]{0,1:T(8,128)}), (f32[1024,1024]{1,0:T(8,128)}, f32[1024,512]{1,0:T(8,128)}, ...) | async-done | bytes 12648464 | tf_op jit(solution)/shard_map/psum | solution.py:337
  (271 shorter events, 132.5 us)
Async XLA Ops:
  7.2 37.5 %copy-start = (bf16[1024,1024]{1,0:T(8,128)(2,1)S(1)}, bf16[1024,1024]{1,0:T(8,128)(2,1)}, u32[]{:S(2)}) copy-start(bf16[1024,1024]{1,0:T(8,128)(2,1)} %param.23) | copy-start | bytes 6291460
  7.2 28.9 %copy-start.7 = (bf16[256,1024]{1,0:T(8,128)(2,1)S(1)}, bf16[256,1024]{1,0:T(8,128)(2,1)}, u32[]{:S(2)}) copy-start(bf16[256,1024]{1,0:T(8,128)(2,1)} %param.15) | copy-start | bytes 1572868
  7.2 28.9 %copy-start.48 = (f32[1024]{0:T(1024)S(1)}, f32[1024]{0:T(1024)}, u32[]{:S(2)}) copy-start(f32[1024]{0:T(1024)} %param.19) | copy-start | bytes 12292
  12.0 28.6 %copy-start.59 = (f32[256]{0:T(256)}, f32[256]{0:T(256)S(1)}, u32[]{:S(2)}) copy-start(f32[256]{0:T(256)S(1)} %add_rsqrt_fusion.1) | copy-start | bytes 3076
  17.4 16.4 copy-start.63
  45.5 19.4 %copy-start.72 = (f32[256]{0:T(256)}, f32[256]{0:T(256)S(1)}, u32[]{:S(2)}) copy-start(f32[256]{0:T(256)S(1)} %add_rsqrt_fusion) | copy-start | bytes 3076
  46.6 18.3 %copy-start.3 = (bf16[256,1024]{1,0:T(8,128)(2,1)}, bf16[256,1024]{1,0:T(8,128)(2,1)S(1)}, u32[]{:S(2)}) copy-start(bf16[256,1024]{1,0:T(8,128)(2,1)S(1)} %multiply_convert_fusion.3) | copy-start | bytes 1572868
  81.8 7.6 copy-start.74
  81.8 8.8 copy-start.50
  81.8 10.5 copy-start.52
  81.8 158.3 %all-to-all-start = ((bf16[256,16,1024]{2,0,1:T(8,128)(2,1)}), bf16[256,16,1024]{2,0,1:T(8,128)(2,1)}, u32[]{:S(2)}, u32[]{:S(2)}) async-start(bf16[256,16,1024]{2,0,1:T(8,128)(2,1)} %copy_select_fusion), calls=%async_computation | async-start | bytes 16777216 | tf_op jit(solution)/shard_map/all_to_all | solution.py:214
  89.4 385.4 %all-gather.3.cloned.1.call-start = ((), (), s32[]{:S(2)}) async-start(), calls=%async_computation.6 | async-start | bytes 25165824 | tf_op jit(solution)/shard_map/all_gather | solution.py:215
  90.6 25.8 %copy-start.1 = (f32[256,1024]{1,0:T(8,128)}, f32[256,1024]{1,0:T(8,128)S(1)}, u32[]{:S(2)}) copy-start(f32[256,1024]{1,0:T(8,128)S(1)} %convert_element_type.172) | copy-start | bytes 3145732
  93.1 23.2 %copy-start.26 = (f32[256,8]{1,0:T(8,128)}, f32[256,8]{1,0:T(8,128)S(1)}, u32[]{:S(2)}) copy-start(f32[256,8]{1,0:T(8,128)S(1)} %copy.134) | copy-start | bytes 24580
  240.1 434.7 %all-gather.5.cloned.1.call-start = ((), (), s32[]{:S(2)}) async-start(), calls=%async_computation.8 | async-start | bytes 25165824 | tf_op jit(solution)/shard_map/all_gather | solution.py:240
  474.7 16.3 copy-start.39
  474.8 421.8 %reduce-scatter.3.cloned.1.call-start = ((), (), s32[]{:S(2)}) async-start(), calls=%async_computation.7 | async-start | bytes 25165824 | tf_op jit(solution)/shard_map/reduce_scatter | solution.py:216
  475.8 17.3 %copy-start.4 = (bf16[8192,1,1024]{2,0,1:T(8,128)(2,1)S(1)}, bf16[8192,1,1024]{2,0,1:T(8,128)(2,1)}, u32[]{:S(2)}) copy-start(bf16[8192,1,1024]{2,0,1:T(8,128)(2,1)} %all-gather.3.cloned.1.call-done) | copy-start | bytes 50331652
  493.1 181.8 %copy-start.41 = (bf16[1,256,1024]{2,1,0:T(8,128)(2,1)S(1)}, bf16[1,256,1024]{2,1,0:T(8,128)(2,1)}, u32[]{:S(2)}) copy-start(bf16[1,256,1024]{2,1,0:T(8,128)(2,1)} %param.28) | copy-start | bytes 1572868
  707.3 380.7 %reduce-scatter.5.cloned.1.call-start = ((), (), s32[]{:S(2)}) async-start(), calls=%async_computation.9 | async-start | bytes 25165824 | tf_op jit(solution)/shard_map/reduce_scatter | solution.py:245
  707.5 18.4 %copy-start.11 = (bf16[8192,256]{1,0:T(8,128)(2,1)S(1)}, bf16[8192,256]{1,0:T(8,128)(2,1)}, u32[]{:S(2)}) copy-start(bf16[8192,256]{1,0:T(8,128)(2,1)} %get-tuple-element.29) | copy-start | bytes 12582916
  924.5 190.7 %all-to-all-start.1 = ((bf16[16,2,131072]{2,1,0:T(2,128)(2,1)}), bf16[16,2,131072]{2,1,0:T(2,128)(2,1)}, u32[]{:S(2)}, u32[]{:S(2)}) async-start(bf16[16,2,131072]{2,1,0:T(2,128)(2,1)} %reshape.555), calls=%async_computation.2 | async-start | bytes 16777216 | tf_op jit(solution)/shard_map/all_to_all | solution.py:222
  1115.2 156.5 %all-to-all-start.3 = ((bf16[16,2,131072]{2,1,0:T(2,128)(2,1)}), bf16[16,2,131072]{2,1,0:T(2,128)(2,1)}, u32[]{:S(2)}, u32[]{:S(2)}) async-start(bf16[16,2,131072]{2,1,0:T(2,128)(2,1)} %reshape.557), calls=%async_computation.5 | async-start | bytes 16777216 | tf_op jit(solution)/shard_map/all_to_all | solution.py:251
  1121.0 502.4 %all-reduce.4.cloned.1.call-start = ((), (), s32[]{:S(2)}) async-start(), calls=%async_computation.10 | async-start | bytes 25296896 | tf_op jit(solution)/shard_map/psum | solution.py:337
  1161.3 15.5 copy-start.2
  1161.3 15.5 copy-start.27
  1354.3 12.9 copy-start.9
  1354.3 22.2 %slice-start = ((s8[16777216]{0:T(1024)(128)(4,1)}), s8[4194304]{0:T(1024)(128)(4,1)S(1)}, s32[]{:S(2)}) async-start(s8[16777216]{0:T(1024)(128)(4,1)} %bitcast.245), calls=%async_computation.11 | async-start | bytes 8388608
  1354.3 22.2 %slice-start.1 = ((s8[16777216]{0:T(1024)(128)(4,1)}), s8[4194304]{0:T(1024)(128)(4,1)S(1)}, s32[]{:S(2)}) async-start(s8[16777216]{0:T(1024)(128)(4,1)} %bitcast.245), calls=%async_computation.12 | async-start | bytes 8388608
  1367.2 9.3 slice-start.2
  1367.2 9.3 slice-start.3
  1367.2 9.6 copy-start.10
  (55 other events, 188.2 us)
Sparse Core Ops, SparseCore 0:
  240.2 230.6 all-gather.2
  474.9 199.8 all-gather.4
  707.4 189.1 reduce-scatter.2
  898.8 189.1 reduce-scatter.4
  1354.4 269.0 all-reduce.3
where the time goes:
time: 1650 us; the launch traced here: 1640 us
  waiting for transfers between devices  834 us (51%)
  blocking collectives  294 us (18%)
  local copies, waits for them, and re-layouts  239 us (14%)
  matrix products  153 us (9%)
  other arithmetic  86.7 us (5%)
  starting transfers between devices  19.9 us (1%)
    all_to_all x1, blocking collectives, local(): lax.all_to_all(slot_upstream, 'ep', split_axis=1, concat_axis=0, tiled=True)  219 us
    all_gather x1, waiting for transfers between devices, local(): lax.all_gather(upstream_recv, 'hs', axis=0, tiled=True)  175 us
    psum x1, waiting for transfers between devices, local(): lax.psum((attn_gain_grad, query_w_grad, key_w_grad, value_w_grad, out_w_g...  159 us
    reduce_scatter x1, waiting for transfers between devices, local(): lax.psum_scatter(input_partial(gate_pre_grad, up_pre_grad, w_gate, w_up)....  158 us
    reduce_scatter x1, waiting for transfers between devices, local(): lax.psum_scatter(expert_rows(gathered, w_gate, w_up, w_down).astype(jnp.b...  151 us
    unnamed x170, local copies, waits for them, and re-layouts  107 us
    all_to_all x1, waiting for transfers between devices, local(): lax.all_to_all(dispatched, 'ep', split_axis=1, concat_axis=0, tiled=True)  105 us
    all_to_all x1, waiting for transfers between devices, local(): lax.all_to_all(input_sum, 'ep', split_axis=0, concat_axis=1, tiled=True)  86.6 us
  transfers between devices with their start and end apart: 8, of which 6 were waited for; matrix products, arithmetic and copies ran while one was open for 17% of the time, Pallas kernels for 0%

commit v1 on v0

--- a/solution.py
+++ b/solution.py
@@ -28,11 +28,8 @@
 
 
 def positions_of(segment):
-    sequence_length = segment.shape[-1]
-    indices = jnp.arange(sequence_length, dtype=jnp.int32)
-    starts = jnp.concatenate([jnp.ones((1,), dtype=bool), segment[1:] != segment[:-1]])
-    first_index = lax.cummax(jnp.where(starts, indices, 0), axis=0)
-    return indices - first_index
+    before = (segment[None, :] < segment[:, None]).astype(jnp.int32)
+    return jnp.arange(segment.shape[-1], dtype=jnp.int32) - jnp.sum(before, axis=1)
 
 
 def rotary_tables(positions, head_dim):
@@ -68,53 +65,46 @@
     )
 
 
-def rounded(value_rows):
-    return lax.optimization_barrier(value_rows.astype(jnp.bfloat16)).astype(jnp.float32)
-
-
-def hidden_units(slot_rows, gate_w, up_w):
-    gate_pre = jnp.einsum("red,edf->ref", slot_rows, gate_w, preferred_element_type=jnp.float32)
-    up_pre = jnp.einsum("red,edf->ref", slot_rows, up_w, preferred_element_type=jnp.float32)
-    return (gate_pre, up_pre)
-
-
-def expert_rows(slot_rows, gate_w, up_w, down_w):
-    gate_pre, up_pre = hidden_units(slot_rows, gate_w, up_w)
-    hidden = (jax.nn.silu(gate_pre) * up_pre).astype(jnp.bfloat16)
-    partial_value = jnp.einsum("ref,efd->red", hidden, down_w, preferred_element_type=jnp.float32)
-    total = rounded(partial_value)
-    return total
-
-
-def hidden_grads(slot_rows, upstream, gate_w, up_w, down_w):
-    gate_pre, up_pre = hidden_units(slot_rows, gate_w, up_w)
+def to_bf16(value):
+    return lax.reduce_precision(value, 8, 7)
+
+
+def expert_pass(rows, upstream, gates, gate_w, up_w, down_w):
+    groups, model_dim, width = gate_w.shape
+    gate_all = jnp.concatenate([gate_w[j] for j in range(groups)], axis=1)
+    up_all = jnp.concatenate([up_w[j] for j in range(groups)], axis=1)
+    down_all = down_w.reshape(groups * width, model_dim)
+    gate_pre = jnp.dot(rows, gate_all, preferred_element_type=jnp.float32)
+    up_pre = jnp.dot(rows, up_all, preferred_element_type=jnp.float32)
     sigmoid_part = jax.nn.sigmoid(gate_pre)
     activated = gate_pre * sigmoid_part
     hidden = (activated * up_pre).astype(jnp.bfloat16)
-    hidden_grad = jnp.einsum("red,efd->ref", upstream, down_w, preferred_element_type=jnp.float32)
+    total = jnp.zeros(rows.shape, jnp.float32)
+    for j in range(groups):
+        total = total + to_bf16(
+            jnp.dot(hidden[:, j * width : (j + 1) * width], down_w[j], preferred_element_type=jnp.float32)
+        )
+    total = to_bf16(total)
+    upstream_f = upstream.astype(jnp.float32)
+    gate_upstream = jnp.sum(upstream_f * total, axis=-1)
+    weighted = (gates[:, None] * total).astype(jnp.bfloat16)
+    upstream_e = (gates[:, None] * upstream_f).astype(jnp.bfloat16)
+    hidden_grad = jnp.einsum("td,fd->tf", upstream_e, down_all, preferred_element_type=jnp.float32)
     up_pre_grad = (hidden_grad * activated).astype(jnp.bfloat16)
     gate_pre_grad = (
         hidden_grad * up_pre * sigmoid_part * (1.0 + gate_pre * (1.0 - sigmoid_part))
     ).astype(jnp.bfloat16)
-    down_w_grad = jnp.einsum("ref,red->efd", hidden, upstream, preferred_element_type=jnp.float32)
-    gate_w_grad = jnp.einsum(
-        "red,ref->edf", slot_rows, gate_pre_grad, preferred_element_type=jnp.float32
-    )
-    up_w_grad = jnp.einsum(
-        "red,ref->edf", slot_rows, up_pre_grad, preferred_element_type=jnp.float32
-    )
-    return (gate_pre_grad, up_pre_grad, gate_w_grad, up_w_grad, down_w_grad)
-
-
-def input_partial(gate_pre_grad, up_pre_grad, gate_w, up_w):
-    partial_value = jnp.einsum(
-        "ref,edf->red", gate_pre_grad, gate_w, preferred_element_type=jnp.float32
-    )
-    partial_value = partial_value + jnp.einsum(
-        "ref,edf->red", up_pre_grad, up_w, preferred_element_type=jnp.float32
-    )
-    total = rounded(partial_value)
-    return total
+    down_grad = jnp.einsum("tf,td->fd", hidden, upstream_e, preferred_element_type=jnp.float32)
+    gate_grad = jnp.einsum("td,tf->df", rows, gate_pre_grad, preferred_element_type=jnp.float32)
+    up_grad = jnp.einsum("td,tf->df", rows, up_pre_grad, preferred_element_type=jnp.float32)
+    back = jnp.zeros(rows.shape, jnp.float32)
+    for j in range(groups):
+        cut = slice(j * width, (j + 1) * width)
+        back = back + to_bf16(
+            jnp.einsum("tf,df->td", gate_pre_grad[:, cut], gate_w[j], preferred_element_type=jnp.float32)
+            + jnp.einsum("tf,df->td", up_pre_grad[:, cut], up_w[j], preferred_element_type=jnp.float32)
+        )
+    return (weighted, back.astype(jnp.bfloat16), gate_upstream, gate_grad, up_grad, down_grad)
 
 
 def local(
@@ -137,10 +127,12 @@
     sequence_length = tokens.shape[0]
     model_dim = tokens.shape[1]
     experts_all = router.shape[1]
-    capacity = min(sequence_length, 2 * sequence_length * TOP // experts_all)
-    slots_total = capacity * experts_all
     query_per_key_head = QUERY_HEADS // KEY_VALUE_HEADS
     score_scale = HEAD_SIZE ** (-0.5)
+    upstream_all = lax.all_gather(cotangent, "ep", axis=0, tiled=True)
+    gate_all = lax.all_gather(w_gate, "hs", axis=0, tiled=True)
+    up_all = lax.all_gather(w_up, "hs", axis=0, tiled=True)
+    down_all = lax.all_gather(w_down, "hs", axis=0, tiled=True)
     segment = segment_ids[0]
     live_row = live_mask[0]
     inputs = tokens.astype(jnp.float32)
@@ -197,62 +189,25 @@
     live_column = live_row.astype(jnp.float32)[:, None]
     route_gates = route_soft * live_column
     counts_local = jnp.sum(route_hot * live_column[:, :, None], axis=(0, 1))
-    flat_expert = routes.reshape(-1)
-    assign_hot = (flat_expert[:, None] == jnp.arange(experts_all)[None, :]).astype(jnp.int32)
-    running = jnp.cumsum(assign_hot, axis=0)
-    slot_index = jnp.sum(assign_hot * running, axis=1) - 1
-    destination = slot_index * experts_all + flat_expert
-    source = (
-        jnp.zeros((slots_total,), jnp.int32)
-        .at[destination]
-        .set(jnp.arange(sequence_length * TOP, dtype=jnp.int32))
-    )
-    filled = jnp.zeros((slots_total,), jnp.int32).at[destination].set(1) > 0
-    token_of_slot = source // TOP
-    dispatched = jnp.where(filled[:, None], moe_in[token_of_slot], jnp.zeros((), jnp.bfloat16))
-    dispatched = dispatched.reshape(capacity, experts_all, model_dim)
-    received = lax.all_to_all(dispatched, "ep", split_axis=1, concat_axis=0, tiled=True)
-    gathered = lax.all_gather(received, "hs", axis=0, tiled=True)
-    expert_sum = lax.psum_scatter(
-        expert_rows(gathered, w_gate, w_up, w_down).astype(jnp.bfloat16),
-        "hs",
-        scatter_dimension=0,
-        tiled=True,
-    )
-    returned = lax.all_to_all(expert_sum, "ep", split_axis=0, concat_axis=1, tiled=True)
-    per_route = (
-        returned.reshape(slots_total, model_dim)[destination]
-        .reshape(sequence_length, TOP, model_dim)
-        .astype(jnp.float32)
-    )
-    combined = jnp.sum(route_gates[:, :, None] * per_route, axis=1)
+    dense_gates = jnp.sum(route_hot * route_gates[:, :, None], axis=1)
+    rows_all = lax.all_gather(moe_in, "ep", axis=0, tiled=True)
+    gates_all = lax.all_to_all(
+        dense_gates.T.reshape(experts_all, 1, sequence_length), "ep", split_axis=0, concat_axis=1, tiled=True
+    ).reshape(-1)
+    weighted, back, gate_upstream_all, gate_w_grad, up_w_grad, down_w_grad = expert_pass(
+        rows_all, upstream_all, gates_all, gate_all, up_all, down_all
+    )
+    combined = lax.psum_scatter(weighted, "ep", scatter_dimension=0, tiled=True).astype(jnp.float32)
+    expert_input_grad = lax.psum_scatter(back, "ep", scatter_dimension=0, tiled=True).astype(jnp.float32)
     output = (middle + combined).astype(jnp.bfloat16)
     upstream = cotangent.astype(jnp.float32)
-    gate_upstream = jnp.sum(upstream[:, None, :] * per_route, axis=-1)
-    slot_gate = route_gates.reshape(-1)[source]
-    slot_upstream = jnp.where(
-        filled[:, None], slot_gate[:, None] * upstream[token_of_slot], 0.0
-    ).astype(jnp.bfloat16)
-    slot_upstream = slot_upstream.reshape(capacity, experts_all, model_dim)
-    upstream_recv = lax.all_to_all(slot_upstream, "ep", split_axis=1, concat_axis=0, tiled=True)
-    rows_all, grads_all = (
-        lax.all_gather(received, "hs", axis=0, tiled=True),
-        lax.all_gather(upstream_recv, "hs", axis=0, tiled=True),
-    )
-    gate_pre_grad, up_pre_grad, gate_w_grad, up_w_grad, down_w_grad = hidden_grads(
-        rows_all, grads_all, w_gate, w_up, w_down
-    )
-    input_sum = lax.psum_scatter(
-        input_partial(gate_pre_grad, up_pre_grad, w_gate, w_up).astype(jnp.bfloat16),
-        "hs",
-        scatter_dimension=0,
-        tiled=True,
-    )
-    input_back = lax.all_to_all(input_sum, "ep", split_axis=0, concat_axis=1, tiled=True)
-    back_routes = input_back.reshape(slots_total, model_dim)[destination].reshape(
-        sequence_length, TOP, model_dim
-    )
-    expert_input_grad = jnp.sum(back_routes.astype(jnp.float32), axis=1)
+    gate_upstream_dense = lax.all_to_all(
+        gate_upstream_all.reshape(experts_all, 1, sequence_length), "ep", split_axis=0, concat_axis=1, tiled=True
+    ).reshape(experts_all, sequence_length).T
+    gate_upstream = jnp.sum(route_hot * gate_upstream_dense[:, None, :], axis=-1)
+    gate_w_grad = lax.psum_scatter(gate_w_grad, "hs", scatter_dimension=1, tiled=True)[None]
+    up_w_grad = lax.psum_scatter(up_w_grad, "hs", scatter_dimension=1, tiled=True)[None]
+    down_w_grad = lax.psum_scatter(down_w_grad, "hs", scatter_dimension=0, tiled=True)[None]
     soft_upstream = gate_upstream * live_column
     chosen_grad = route_soft * (
         soft_upstream - jnp.sum(route_soft * soft_upstream, axis=-1, keepdims=True)

time: 1650 us -> 917 us (0.56)
  blocking collectives: 294 us -> 49.7 us
  local copies, waits for them, and re-layouts: 239 us -> 23 us
  waiting for transfers between devices: 834 us -> 621 us
  other arithmetic: 86.7 us -> 24.5 us
  matrix products: 153 us -> 174 us
    all_to_all x1, blocking collectives: 219 us -> 9.07 us  [local(): lax.all_to_all(dense_gates.T.reshape(experts_all, 1, sequence_length), 'e...]
    all_to_all x3 -> x1, waiting for transfers between devices: 192 us -> 5.96 us  [local(): lax.all_to_all(gate_upstream_all.reshape(experts_all, 1, sequence_length)...]
    reduce_scatter x2 -> x5, waiting for transfers between devices: 309 us -> 195 us  [the longest x1 106 us: local(): lax.psum_scatter(weighted, 'ep', scatter_dimension=0, tiled=True)]
    gather x5 -> x0, local copies, waits for them, and re-layouts: 91 us -> none  [the longest x1 23 us: local(): slot_gate = route_gates.reshape(-1)[source]]
    unnamed x170 -> x112, local copies, waits for them, and re-layouts: 107 us -> 19.1 us
    psum x1, waiting for transfers between devices: 159 us -> 246 us  [local(): lax.psum((attn_gain_grad, query_w_grad, key_w_grad, value_w_grad, out_w_g...]
    psum x1, blocking collectives: 75 us -> 40.6 us  [local(): lax.psum((attn_gain_grad, query_w_grad, key_w_grad, value_w_grad, out_w_g...]
    reduce_scatter x2 -> x0, other arithmetic: 25.4 us -> none  [the longest x1 12.7 us: local(): lax.psum_scatter(input_partial(gate_pre_grad, up_pre_grad, w_gate, w_up)....]
  transfers between devices with their start and end apart: 8 -> 12, of which waited for: 6 -> 10; matrix products, arithmetic and copies ran while one was open for 17% -> 13% of each run, Pallas kernels for 0% -> 0%
where the time goes in v1:
time: 917 us; the launch traced here: 912 us
  waiting for transfers between devices  621 us (68%)
  matrix products  174 us (19%)
  blocking collectives  49.7 us (5%)
  other arithmetic  24.5 us (3%)
  local copies, waits for them, and re-layouts  23 us (3%)
  between operations  14.9 us (2%)
    psum x1, waiting for transfers between devices, local(): lax.psum((attn_gain_grad, query_w_grad, key_w_grad, value_w_grad, out_w_g...  246 us
    reduce_scatter x1, waiting for transfers between devices, local(): lax.psum_scatter(weighted, 'ep', scatter_dimension=0, tiled=True)  106 us
    all_gather x1, waiting for transfers between devices, local(): rows_all = lax.all_gather(moe_in, 'ep', axis=0, tiled=True)  75.4 us
    all_gather x1, waiting for transfers between devices, local(): upstream_all = lax.all_gather(cotangent, 'ep', axis=0, tiled=True)  67 us
    reduce_scatter x1, waiting for transfers between devices, local(): lax.psum_scatter(back, 'ep', scatter_dimension=0, tiled=True)  56.8 us
    psum x1, blocking collectives, local(): lax.psum((attn_gain_grad, query_w_grad, key_w_grad, value_w_grad, out_w_g...  40.6 us
    reduce_scatter x1, waiting for transfers between devices, local(): lax.psum_scatter(up_w_grad, 'hs', scatter_dimension=1, tiled=True)[None]  32.5 us
    dot_general x2, matrix products, expert_pass(): jnp.dot(hidden[:, j * width:(j + 1) * width], down_w[j], preferred_elemen...  29.2 us
  transfers between devices with their start and end apart: 12, of which 10 were waited for; matrix products, arithmetic and copies ran while one was open for 13% of the time, Pallas kernels for 0%

profile of v1, /device:TPU:0, one launch (start us, length us, event | category | flops | bytes accessed | tf_op | source)
XLA Modules:
  0.0 911.6 jit_solution(5875552281925861520)
XLA Ops:
  27.0 6.6 all-gather.10.cloned.1.call-done
  34.9 21.6 %all-gather.8.cloned.1.call-done = bf16[2,1024,256]{2,1,0:T(8,128)(2,1)} async-done(((bf16[1,1024,256]{2,1,0:T(8,128)(2,1)}), bf16[2,1024,256]{2,1,0:T(8,128)(2,1)}) %all-gather.8.cloned.1.call-update) | async-done | bytes 1048592 | tf_op jit(solution)/shard_map/all_gather | solution.py:133
  58.8 75.4 %all-gather.6.cloned.1.call-done = bf16[4096,1024]{1,0:T(8,128)(2,1)} async-done(((bf16[256,1024]{1,0:T(8,128)(2,1)}), bf16[4096,1024]{1,0:T(8,128)(2,1)}) %all-gather.6.cloned.1.call-update) | async-done | bytes 8388624 | tf_op jit(solution)/shard_map/all_gather | solution.py:193
  134.2 8.0 fusion.46
  142.2 3.2 copy-done.52
  145.4 8.8 multiply_convert_fusion.3
  155.2 9.9 %fusion.22 = f32[4096,1024]{1,0:T(8,128)} fusion(bf16[4096,512]{1,0:T(8,128)(2,1)} %get-tuple-element.54, bf16[2,256,1024]{2,1,0:T(8,128)(2,1)} %all-gather.12.cloned.1.call-done), kind=kOutput, calls=%fused_computation.34 | convolution fusion | flops 2147483648 | bytes 19398656 | tf_op jit(solution)/shard_map/dot_general | solution.py:85
  165.1 67.0 %all-gather.14.cloned.1.call-done = bf16[4096,1024]{1,0:T(8,128)(2,1)} async-done(((bf16[256,1024]{1,0:T(8,128)(2,1)}), bf16[4096,1024]{1,0:T(8,128)(2,1)}) %all-gather.14.cloned.1.call-update) | async-done | bytes 8388624 | tf_op jit(solution)/shard_map/all_gather | solution.py:132
  232.1 19.3 %fusion.1 = (f32[4096]{0:T(1024)}, f32[4096,1024]{1,0:T(8,128)}) fusion(bf16[4096,1024]{1,0:T(8,128)(2,1)} %all-gather.14.cloned.1.call-done, bf16[2,256,1024]{2,1,0:T(8,128)(2,1)} %all-gather.12.cloned.1.call-done, bf16[4096,512]{1,0:T(8,128)(2,1)} %get-tuple-element.54, f32[4096,1024]{1,0:T(8,128)} %fusion.22), kind=kOutput, calls=%fused_computation.3 | convolution fusion | flops 2176839680 | bytes 44580864 | tf_op jit(solution)/shard_map/dot_general | solution.py:85
  251.4 3.5 all-to-all-start.1
  255.4 6.0 all-to-all-done.1
  261.7 9.1 all_to_all.8
  270.8 16.6 %multiply_convert_fusion.1 = (bf16[4096,512]{1,0:T(8,128)(2,1)}, bf16[4096,512]{1,0:T(8,128)(2,1)S(1)}) fusion(f32[4096,512]{1,0:T(8,128)} %copy-done.52, f32[4096,512]{1,0:T(8,128)} %get-tuple-element.55, bf16[512,1024]{1,0:T(8,128)(2,1)} %bitcast.141, bf16[4096,1024]{1,0:T(8,128)(2,1)} %all-gather.14.cloned.1.call-done, f32[4096]{0:T(1024)S(1)} %bitcast.156), kind=kOutput, calls=%fused_computation.7 | convolution fusion | flops 4334813184 | bytes 34619392 | tf_op jit(solution)/shard_map/td,fd->tf/dot_general | solution.py:92
  287.4 8.1 fusion.15
  295.5 8.1 fusion.19
  303.6 8.1 fusion.17
  311.7 20.7 %add_convert_fusion = bf16[4096,1024]{1,0:T(8,128)(2,1)} fusion(f32[4096,1024]{1,0:T(8,128)} %fusion.15, f32[4096,1024]{1,0:T(8,128)} %fusion.19, f32[4096,1024]{1,0:T(8,128)} %fusion.17, bf16[4096,512]{1,0:T(8,128)(2,1)S(1)} %copy-done.12, bf16[2,1024,256]{2,1,0:T(8,128)(2,1)} %all-gather.10.cloned.1.call-done), kind=kOutput, calls=%fused_computation.4 | convolution fusion | flops 2172649472 | bytes 61341696 | tf_op jit(solution)/shard_map/tf,df->td/dot_general | solution.py:105
  332.5 11.0 %multiply_convert_fusion = bf16[4096,1024]{1,0:T(8,128)(2,1)} fusion(f32[4096,1024]{1,0:T(8,128)} %get-tuple-element.57, f32[4096]{0:T(1024)S(1)} %bitcast.157), kind=kLoop, calls=%fused_computation.5 | loop fusion | flops 8388608 | bytes 25182208 | tf_op jit(solution)/shard_map/convert_element_type | solution.py:90
  343.5 11.9 %fusion.7 = f32[512,1024]{1,0:T(8,128)} fusion(bf16[4096,512]{1,0:T(8,128)(2,1)} %get-tuple-element.54, bf16[4096,1024]{1,0:T(8,128)(2,1)} %all-gather.14.cloned.1.call-done, f32[4096]{0:T(1024)S(1)} %bitcast.158), kind=kOutput, calls=%fused_computation.22 | convolution fusion | flops 4307550208 | bytes 14696448 | tf_op jit(solution)/shard_map/tf,td->fd/dot_general | solution.py:97
  355.5 10.4 %fusion.84 = f32[1024,512]{1,0:T(8,128)} fusion(bf16[4096,1024]{1,0:T(8,128)(2,1)} %all-gather.6.cloned.1.call-done, bf16[4096,512]{1,0:T(8,128)(2,1)} %copy-done.10), kind=kOutput, calls=%fused_computation.146 | convolution fusion | flops 4294967296 | bytes 14680064 | tf_op jit(solution)/shard_map/td,tf->df/dot_general | solution.py:98
  366.8 10.6 %fusion.85 = f32[1024,512]{1,0:T(8,128)} fusion(bf16[4096,1024]{1,0:T(8,128)(2,1)} %all-gather.6.cloned.1.call-done, bf16[4096,512]{1,0:T(8,128)(2,1)} %get-tuple-element.30), kind=kOutput, calls=%fused_computation.147 | convolution fusion | flops 4294967296 | bytes 14680064 | tf_op jit(solution)/shard_map/td,tf->df/dot_general | solution.py:99
  377.7 56.8 %reduce-scatter.8.cloned.1.call-done = bf16[256,1024]{1,0:T(8,128)(2,1)} async-done(((bf16[4096,1024]{1,0:T(8,128)(2,1)}), bf16[256,1024]{1,0:T(8,128)(2,1)}) %reduce-scatter.8.cloned.1.call-update) | async-done | bytes 524304 | tf_op jit(solution)/shard_map/reduce_scatter | solution.py:201
  437.0 106.0 %reduce-scatter.6.cloned.1.call-done = bf16[256,1024]{1,0:T(8,128)(2,1)} async-done(((bf16[4096,1024]{1,0:T(8,128)(2,1)}), bf16[256,1024]{1,0:T(8,128)(2,1)}) %reduce-scatter.6.cloned.1.call-update) | async-done | bytes 524304 | tf_op jit(solution)/shard_map/reduce_scatter | solution.py:200
  543.0 2.7 multiply_add_fusion
  547.7 3.3 fusion.3
  558.7 2.9 fusion.74
  561.6 2.7 fusion.54
  571.1 40.6 %all-reduce = (f32[1024]{0:T(1024)}, f32[1024]{0:T(1024)}, f32[16]{0:T(128)S(1)}) all-reduce(f32[1024]{0:T(1024)S(1)} %get-tuple-element.15, f32[1024]{0:T(1024)S(1)} %get-tuple-element.13, f32[16]{0:T(128)S(1)} %get-tuple-element.17), channel_id=1, replica_groups=mesh['ep'=16,'hs'=2] {'ep','hs'}, use_global_device_ids=true, to_apply=%region_19.20 | all-reduce | flops 2064 | bytes 16512 | tf_op jit(solution)/shard_map/psum | solution.py:292
  612.2 2.9 fusion.41
  615.1 32.5 %reduce-scatter.12.cloned.1.call-done = f32[1024,256]{1,0:T(8,128)} async-done(((f32[1024,512]{1,0:T(8,128)}), f32[1024,256]{1,0:T(8,128)}) %reduce-scatter.12.cloned.1.call-update) | async-done | bytes 1048592 | tf_op jit(solution)/shard_map/reduce_scatter | solution.py:209
  647.6 245.7 %all-reduce.4.cloned.1.call-done = (f32[1024,1024]{1,0:T(8,128)}, f32[1024,512]{1,0:T(8,128)}, f32[1024,512]{1,0:T(8,128)}, f32[1024,1024]{1,0:T(8,128)}, f32[1024,16]{0,1:T(8,128)}) async-done(((f32[1024,1024]{1,0:T(8,128)}, f32[1024,512]{1,0:T(8,128)}, f32[1024,512]{1,0:T(8,128)}, f32[1024,1024]{1,0:T(8,128)}, f32[1024,16]{0,1:T(8,128)}), (f32[1024,1024]{1,0:T(8,128)}, f32[1024,512]{1,0:T(8,128)}, ...) | async-done | bytes 12648464 | tf_op jit(solution)/shard_map/psum | solution.py:292
  893.3 4.9 copy.107
  (187 shorter events, 51.7 us)
Async XLA Ops:
  7.2 15.9 %copy-start = (bf16[1024,1024]{1,0:T(8,128)(2,1)S(1)}, bf16[1024,1024]{1,0:T(8,128)(2,1)}, u32[]{:S(2)}) copy-start(bf16[1024,1024]{1,0:T(8,128)(2,1)} %param.23) | copy-start | bytes 6291460
  7.2 7.3 copy-start.3
  7.2 7.3 copy-start.39
  7.2 26.4 %all-gather.10.cloned.1.call-start = ((), (), s32[]{:S(2)}) async-start(), calls=%async_computation.9 | async-start | bytes 1572864 | tf_op jit(solution)/shard_map/all_gather | solution.py:134
  8.0 48.6 %all-gather.8.cloned.1.call-start = ((), (), s32[]{:S(2)}) async-start(), calls=%async_computation.8 | async-start | bytes 1572864 | tf_op jit(solution)/shard_map/all_gather | solution.py:133
  8.7 125.5 %all-gather.6.cloned.1.call-start = ((), (), s32[]{:S(2)}) async-start(), calls=%async_computation.7 | async-start | bytes 8912896 | tf_op jit(solution)/shard_map/all_gather | solution.py:193
  11.6 7.5 copy-start.43
  14.5 7.2 copy-start.28
  25.9 129.3 %all-gather.12.cloned.1.call-start = ((), (), s32[]{:S(2)}) async-start(), calls=%async_computation.10 | async-start | bytes 1572864 | tf_op jit(solution)/shard_map/all_gather | solution.py:135
  26.4 205.7 %all-gather.14.cloned.1.call-start = ((), (), s32[]{:S(2)}) async-start(), calls=%async_computation.12 | async-start | bytes 8912896 | tf_op jit(solution)/shard_map/all_gather | solution.py:132
  134.2 11.2 %copy-start.51 = (bf16[4096,1024]{1,0:T(8,128)(2,1)S(1)}, bf16[4096,1024]{1,0:T(8,128)(2,1)}, u32[]{:S(2)}) copy-start(bf16[4096,1024]{1,0:T(8,128)(2,1)} %all-gather.6.cloned.1.call-done) | copy-start | bytes 25165828
  165.1 90.1 %copy-start.9 = (bf16[256,1024]{1,0:T(8,128)(2,1)S(1)}, bf16[256,1024]{1,0:T(8,128)(2,1)}, u32[]{:S(2)}) copy-start(bf16[256,1024]{1,0:T(8,128)(2,1)} %multiply_convert_fusion.4) | copy-start | bytes 1572868
  165.1 90.1 %copy-start.41 = (bf16[1024,16]{0,1:T(8,128)(2,1)S(1)}, bf16[1024,16]{0,1:T(8,128)(2,1)}, u32[]{:S(2)}) copy-start(bf16[1024,16]{0,1:T(8,128)(2,1)} %param.25) | copy-start | bytes 98308
  165.1 90.3 %copy-start.50 = (s32[1,256]{1,0:T(1,128)S(1)}, s32[1,256]{1,0:T(1,128)}, u32[]{:S(2)}) copy-start(s32[1,256]{1,0:T(1,128)} %param.17) | copy-start | bytes 3076
  165.1 96.3 %copy-start.47 = (s32[256,8]{0,1:T(8,128)S(1)}, s32[256,8]{0,1:T(8,128)}, u32[]{:S(2)}) copy-start(s32[256,8]{0,1:T(8,128)} %param.18) | copy-start | bytes 24580
  251.4 10.0 %all-to-all-start.1 = ((f32[16,1,256]{2,1,0:T(1,128)}), f32[16,1,256]{2,1,0:T(1,128)S(1)}, u32[]{:S(2)}, u32[]{:S(2)}) async-start(f32[16,1,256]{2,1,0:T(1,128)} %bitcast.24), calls=%async_computation.3 | async-start | bytes 32768 | tf_op jit(solution)/shard_map/all_to_all | solution.py:204
  254.9 179.6 %reduce-scatter.8.cloned.1.call-start = ((), (), s32[]{:S(2)}) async-start(), calls=%async_computation.13 | async-start | bytes 8912896 | tf_op jit(solution)/shard_map/reduce_scatter | solution.py:201
  270.8 16.6 %copy-start.16 = (bf16[2,1024,256]{2,1,0:T(8,128)(2,1)S(1)}, bf16[2,1024,256]{2,1,0:T(8,128)(2,1)}, u32[]{:S(2)}) copy-start(bf16[2,1024,256]{2,1,0:T(8,128)(2,1)} %all-gather.8.cloned.1.call-done) | copy-start | bytes 3145732
  287.4 8.1 copy-start.10
  295.5 8.1 copy-start.11
  295.5 8.1 copy-start.15
  303.6 8.1 copy-start.12
  332.4 210.6 %reduce-scatter.6.cloned.1.call-start = ((), (), s32[]{:S(2)}) async-start(), calls=%async_computation.11 | async-start | bytes 8912896 | tf_op jit(solution)/shard_map/reduce_scatter | solution.py:200
  343.5 271.6 %reduce-scatter.14.cloned.1.call-start = ((), (), s32[]{:S(2)}) async-start(), calls=%async_computation.16 | async-start | bytes 3145728 | tf_op jit(solution)/shard_map/reduce_scatter | solution.py:210
  355.4 259.7 %reduce-scatter.10.cloned.1.call-start = ((), (), s32[]{:S(2)}) async-start(), calls=%async_computation.14 | async-start | bytes 3145728 | tf_op jit(solution)/shard_map/reduce_scatter | solution.py:208
  365.9 281.7 %reduce-scatter.12.cloned.1.call-start = ((), (), s32[]{:S(2)}) async-start(), calls=%async_computation.15 | async-start | bytes 3145728 | tf_op jit(solution)/shard_map/reduce_scatter | solution.py:209
  366.8 67.7 %copy-start.6 = (f32[256,1024]{1,0:T(8,128)S(1)}, f32[256,1024]{1,0:T(8,128)}, u32[]{:S(2)}) copy-start(f32[256,1024]{1,0:T(8,128)} %copy-done.5) | copy-start | bytes 3145732
  366.8 67.7 %copy-start.46 = (f32[1024]{0:T(1024)S(1)}, f32[1024]{0:T(1024)}, u32[]{:S(2)}) copy-start(f32[1024]{0:T(1024)} %param.24) | copy-start | bytes 12292
  366.8 67.7 %copy-start.49 = (f32[256]{0:T(256)S(1)}, f32[256]{0:T(256)}, u32[]{:S(2)}) copy-start(f32[256]{0:T(256)} %copy-done.48) | copy-start | bytes 3076
  377.4 515.9 %all-reduce.4.cloned.1.call-start = ((), (), s32[]{:S(2)}) async-start(), calls=%async_computation.17 | async-start | bytes 25296896 | tf_op jit(solution)/shard_map/psum | solution.py:292
  893.3 4.9 copy-start.20
  893.3 6.3 copy-start.19
  (33 other events, 72.6 us)
Sparse Core Ops, SparseCore 0:
  9.6 23.9 all-gather.9
  35.2 21.2 all-gather.7
  59.3 74.8 all-gather.5
  135.6 19.5 all-gather.11
  157.2 74.8 all-gather.13
  332.5 101.9 reduce-scatter.7
  438.6 104.4 reduce-scatter.5
  545.8 31.5 reduce-scatter.13
  580.3 32.7 reduce-scatter.9
  615.8 31.8 reduce-scatter.11
  656.3 236.9 all-reduce.3

commit v2 on v1

--- a/solution.py
+++ b/solution.py
@@ -1,6 +1,10 @@
+import functools
+
 import jax
 import jax.numpy as jnp
 from jax import lax
+from jax.experimental import pallas as pl
+from jax.experimental.pallas import tpu as pltpu
 from jax.sharding import PartitionSpec as P
 
 QUERY_HEADS = 16
@@ -107,6 +111,253 @@
     return (weighted, back.astype(jnp.bfloat16), gate_upstream, gate_grad, up_grad, down_grad)
 
 
+def sum_halves(grad, dim):
+    return lax.psum_scatter(
+        grad.astype(jnp.bfloat16), "hs", scatter_dimension=dim, tiled=True
+    ).astype(jnp.float32)
+
+
+MESH = pl.DeviceIdType.MESH
+UNIT = 16
+
+
+def place():
+    ep, hs = lax.axis_index("ep"), lax.axis_index("hs")
+    return (ep // 4, (ep // 2) % 2, ep % 2, hs)
+
+
+def device(z, x, c, y):
+    return (z * 4 + x * 2 + c, y)
+
+
+def greet(peers):
+    barrier = pltpu.get_barrier_semaphore()
+    for peer in peers:
+        pl.semaphore_signal(barrier, inc=1, device_id=peer, device_id_type=MESH)
+    pl.semaphore_wait(barrier, len(peers))
+
+
+def sum_kernel(count, *refs):
+    grads, small = refs[:count], refs[count]
+    outs, small_out = refs[count + 1 : 2 * count + 1], refs[2 * count + 1]
+    rest = refs[2 * count + 2 :]
+    halves, totals, fulls = rest[:count], rest[count : 2 * count], rest[2 * count : 3 * count]
+    firsts, seconds, lines = rest[3 * count : 4 * count], rest[4 * count : 5 * count], rest[5 * count : 6 * count]
+    small_sum, small_in, send, recv, small_send, small_recv, local_sem = rest[6 * count :]
+    z, x, c, y = place()
+    sibling, beside, across = device(z, x, 1 - c, y), device(z, 1 - x, c, y), device(z, x, c, 1 - y)
+    along = [device((z + k) % 4, x, c, y) for k in (1, 2, 3)]
+    greet([sibling, beside, across] + along)
+    bits = ((x, y), (y, x))
+    partners = ((beside, across), (across, beside))
+
+    def push(i, slot, source, target, peer):
+        copy = pltpu.make_async_remote_copy(
+            src_ref=source,
+            dst_ref=target,
+            send_sem=send.at[i, slot],
+            recv_sem=recv.at[i, slot],
+            device_id=peer,
+            device_id_type=MESH,
+        )
+        copy.start()
+        return copy
+
+    def combine(i, target, start, length, terms):
+        def body(u, carry):
+            value = totals[i][start + u].astype(jnp.float32)
+            for ref, base in terms:
+                value = value + ref[base + u].astype(jnp.float32)
+            target[0][target[1] + u] = value.astype(jnp.bfloat16)
+            return carry
+
+        lax.fori_loop(0, length, body, 0)
+
+    copies = {}
+
+    def stage(i, step):
+        if step == 0:
+            copies[i, 0] = [
+                push(i, 0, grads[i].at[pl.ds((1 - c) * 32, 32)], halves[i], sibling)
+            ]
+        if step == 1:
+            copies[i, 0][0].wait_recv()
+
+            def body(u, carry):
+                value = grads[i][c * 32 + u].astype(jnp.float32) + halves[i][u].astype(jnp.float32)
+                totals[i][u] = value.astype(jnp.bfloat16)
+                return carry
+
+            lax.fori_loop(0, 32, body, 0)
+            copies[i, 1] = [
+                push(
+                    i,
+                    1 + part,
+                    totals[i].at[pl.ds(part * 16 + (1 - bits[part][0]) * 8, 8)],
+                    firsts[i].at[part],
+                    partners[part][0],
+                )
+                for part in (0, 1)
+            ]
+        if step == 2:
+            copies[i, 2] = []
+            for part in (0, 1):
+                copies[i, 1][part].wait_recv()
+                base = part * 16 + bits[part][0] * 8
+                combine(i, (totals[i], base), base, 8, [(firsts[i].at[part], 0)])
+                copies[i, 2].append(
+                    push(
+                        i,
+                        3 + part,
+                        totals[i].at[pl.ds(base + (1 - bits[part][1]) * 4, 4)],
+                        seconds[i].at[part],
+                        partners[part][1],
+                    )
+                )
+        if step == 3:
+            copies[i, 3] = []
+            for part in (0, 1):
+                copies[i, 2][part].wait_recv()
+                base = part * 16 + bits[part][0] * 8 + bits[part][1] * 4
+                combine(i, (totals[i], base), base, 4, [(seconds[i].at[part], 0)])
+                for k in (1, 2, 3):
+                    copies[i, 3].append(
+                        push(
+                            i,
+                            5 + part * 3 + k - 1,
+                            totals[i].at[base + (z + k) % 4],
+                            lines[i].at[part, k - 1],
+                            along[k - 1],
+                        )
+                    )
+        if step == 4:
+            copies[i, 4] = []
+            for part in (0, 1):
+                for k in (1, 2, 3):
+                    copies[i, 3][part * 3 + k - 1].wait_recv()
+                base = part * 16 + bits[part][0] * 8 + bits[part][1] * 4
+                combine(
+                    i, (fulls[i], c * 32 + base + z), base + z, 1, [(lines[i].at[part], k) for k in (0, 1, 2)]
+                )
+                for k in (1, 2, 3):
+                    piece = fulls[i].at[c * 32 + base + z]
+                    copies[i, 4].append(push(i, 11 + part * 3 + k - 1, piece, piece, along[k - 1]))
+        if step == 5:
+            copies[i, 5] = []
+            for part in (0, 1):
+                for k in (1, 2, 3):
+                    copies[i, 4][part * 3 + k - 1].wait_recv()
+                piece = fulls[i].at[pl.ds(c * 32 + part * 16 + bits[part][0] * 8 + bits[part][1] * 4, 4)]
+                copies[i, 5].append(push(i, 17 + part, piece, piece, partners[part][1]))
+        if step == 6:
+            copies[i, 6] = []
+            for part in (0, 1):
+                copies[i, 5][part].wait_recv()
+                piece = fulls[i].at[pl.ds(c * 32 + part * 16 + bits[part][0] * 8, 8)]
+                copies[i, 6].append(push(i, 19 + part, piece, piece, partners[part][0]))
+        if step == 7:
+            for part in (0, 1):
+                copies[i, 6][part].wait_recv()
+            piece = fulls[i].at[pl.ds(c * 32, 32)]
+            copies[i, 7] = [push(i, 21, piece, piece, sibling)]
+        if step == 8:
+            copies[i, 7][0].wait_recv()
+            done = pltpu.make_async_copy(fulls[i], outs[i], local_sem.at[i])
+            done.start()
+            copies[i, 8] = [done]
+
+    def small_push(slot, peer, target):
+        copy = pltpu.make_async_remote_copy(
+            src_ref=small_sum.at[slot],
+            dst_ref=small_in.at[target],
+            send_sem=small_send.at[target],
+            recv_sem=small_recv.at[target],
+            device_id=peer,
+            device_id_type=MESH,
+        )
+        copy.start()
+        return copy
+
+    def small_stage(step):
+        if step == 0:
+            small_sum[0] = small[...]
+            copies["s", 0] = [small_push(0, sibling, 0)]
+        if step in (1, 2):
+            copies["s", step - 1][0].wait_recv()
+            small_sum[step] = small_sum[step - 1] + small_in[step - 1]
+            copies["s", step] = [small_push(step, (beside, across)[step - 1], step)]
+        if step == 3:
+            copies["s", 2][0].wait_recv()
+            small_sum[3] = small_sum[2] + small_in[2]
+            copies["s", 3] = []
+            for k in (1, 2, 3):
+                copy = pltpu.make_async_remote_copy(
+                    src_ref=small_sum.at[3],
+                    dst_ref=small_in.at[3 + z],
+                    send_sem=small_send.at[2 + k],
+                    recv_sem=small_recv.at[2 + k],
+                    device_id=along[k - 1],
+                    device_id_type=MESH,
+                )
+                copy.start()
+                copies["s", 3].append(copy)
+            small_in[3 + z] = small_sum[3]
+        if step == 4:
+            for copy in copies["s", 3]:
+                copy.wait_recv()
+            small_out[...] = (small_in[3] + small_in[4]) + (small_in[5] + small_in[6])
+
+    for tick in range(count + 8):
+        for i in range(count):
+            if 0 <= tick - i <= 8:
+                stage(i, tick - i)
+        if tick <= 4:
+            small_stage(tick)
+    for key, group in copies.items():
+        for copy in group:
+            if key[0] != "s" and key[1] == 8:
+                copy.wait()
+            else:
+                copy.wait_send()
+
+
+def sum_everywhere(arrays, small):
+    count = len(arrays)
+    units = [a.reshape(a.shape[0] // UNIT, UNIT, a.shape[1]) for a in arrays]
+    vmem = pl.BlockSpec(memory_space=pltpu.VMEM)
+
+    def scratch(lead):
+        return [pltpu.VMEM((*lead, UNIT, a.shape[1]), jnp.bfloat16) for a in arrays]
+
+    out = pl.pallas_call(
+        functools.partial(sum_kernel, count),
+        out_shape=[jax.ShapeDtypeStruct(u.shape, u.dtype) for u in units]
+        + [jax.ShapeDtypeStruct(small.shape, small.dtype)],
+        in_specs=[vmem] * (count + 1),
+        out_specs=[pl.BlockSpec(memory_space=pl.ANY)] * count + [vmem],
+        scratch_shapes=[
+            *scratch((32,)),
+            *scratch((32,)),
+            *scratch((64,)),
+            *scratch((2, 8)),
+            *scratch((2, 4)),
+            *scratch((2, 3)),
+            pltpu.VMEM((4, *small.shape), jnp.float32),
+            pltpu.VMEM((7, *small.shape), jnp.float32),
+            pltpu.SemaphoreType.DMA((count, 22)),
+            pltpu.SemaphoreType.DMA((count, 22)),
+            pltpu.SemaphoreType.DMA((6,)),
+            pltpu.SemaphoreType.DMA((6,)),
+            pltpu.SemaphoreType.DMA((count,)),
+        ],
+        compiler_params=pltpu.CompilerParams(
+            collective_id=0, has_side_effects=True, vmem_limit_bytes=56 << 20
+        ),
+        name="sum_everywhere",
+    )(*units, small)
+    return [o.reshape(a.shape).astype(jnp.float32) for o, a in zip(out, arrays)] + [out[-1]]
+
+
 def local(
     tokens,
     segment_ids,
@@ -205,9 +456,9 @@
         gate_upstream_all.reshape(experts_all, 1, sequence_length), "ep", split_axis=0, concat_axis=1, tiled=True
     ).reshape(experts_all, sequence_length).T
     gate_upstream = jnp.sum(route_hot * gate_upstream_dense[:, None, :], axis=-1)
-    gate_w_grad = lax.psum_scatter(gate_w_grad, "hs", scatter_dimension=1, tiled=True)[None]
-    up_w_grad = lax.psum_scatter(up_w_grad, "hs", scatter_dimension=1, tiled=True)[None]
-    down_w_grad = lax.psum_scatter(down_w_grad, "hs", scatter_dimension=0, tiled=True)[None]
+    gate_w_grad = sum_halves(gate_w_grad, 1)[None]
+    up_w_grad = sum_halves(up_w_grad, 1)[None]
+    down_w_grad = sum_halves(down_w_grad, 0)[None]
     soft_upstream = gate_upstream * live_column
     chosen_grad = route_soft * (
         soft_upstream - jnp.sum(route_soft * soft_upstream, axis=-1, keepdims=True)
@@ -289,7 +540,16 @@
     )
     input_norm_grad, attn_gain_grad = rms_backward(inputs, inverse_one, attn_gain, normed_grad)
     input_grad = middle_grad + input_norm_grad
-    shared = lax.psum(
+    if lax.axis_size("ep") == 16 and lax.axis_size("hs") == 2:
+        small = jnp.zeros((24, model_dim), jnp.float32)
+        small = small.at[:experts_all].set(router_w_grad.T)
+        small = small.at[16].set(attn_gain_grad).at[17].set(moe_gain_grad)
+        small = small.at[18, :experts_all].set(counts_local)
+        wide = [g.astype(jnp.bfloat16) for g in (out_w_grad, query_w_grad, key_w_grad, value_w_grad)]
+        out_w_grad, query_w_grad, key_w_grad, value_w_grad, small = sum_everywhere(wide, small)
+        router_w_grad = small[:experts_all].T
+        attn_gain_grad, moe_gain_grad, counts = small[16], small[17], small[18, :experts_all]
+    else:
         (
             attn_gain_grad,
             query_w_grad,
@@ -298,24 +558,34 @@
             out_w_grad,
             moe_gain_grad,
             router_w_grad,
-            counts_local,
-        ),
-        ("ep", "hs"),
-    )
+            counts,
+        ) = lax.psum(
+            (
+                attn_gain_grad,
+                query_w_grad,
+                key_w_grad,
+                value_w_grad,
+                out_w_grad,
+                moe_gain_grad,
+                router_w_grad,
+                counts_local,
+            ),
+            ("ep", "hs"),
+        )
     return (
         output,
         input_grad,
-        shared[0],
-        shared[1],
-        shared[2],
-        shared[3],
-        shared[4],
-        shared[5],
-        shared[6],
+        attn_gain_grad,
+        query_w_grad,
+        key_w_grad,
+        value_w_grad,
+        out_w_grad,
+        moe_gain_grad,
+        router_w_grad,
         gate_w_grad,
         up_w_grad,
         down_w_grad,
-        shared[7].astype(jnp.int32),
+        counts.astype(jnp.int32),
     )
 
 

time: 917 us -> 708 us (0.77)
  waiting for transfers between devices: 621 us -> 368 us
  Pallas kernels: 0 us -> 82.1 us
  blocking collectives: 49.7 us -> 9.07 us
  other arithmetic: 24.5 us -> 39.1 us
    psum x1 -> x0, waiting for transfers between devices: 246 us -> none  [local(): lax.psum((attn_gain_grad, query_w_grad, key_w_grad, value_w_grad, out_w_g...]
    pallas_call x0 -> x1, Pallas kernels: none -> 82.1 us  [sum_everywhere(): pl.pallas_call(functools.partial(sum_kernel, count), out_shape=[jax.Shape...]
    psum x1 -> x0, blocking collectives: 40.6 us -> none  [local(): lax.psum((attn_gain_grad, query_w_grad, key_w_grad, value_w_grad, out_w_g...]
    reduce_scatter x3, waiting for transfers between devices: 32.5 us -> 0.02 us  [sum_halves(): lax.psum_scatter(grad.astype(jnp.bfloat16), 'hs', scatter_dimension=dim,...]
    reduce_scatter x1, waiting for transfers between devices: 56.8 us -> 81.9 us  [local(): lax.psum_scatter(back, 'ep', scatter_dimension=0, tiled=True)]
    convert_element_type x1 -> x3, other arithmetic: 0.52 us -> 10.4 us  [the longest x2 9.03 us: sum_everywhere(): o.reshape(a.shape).astype(jnp.float32)]
    unnamed x112 -> x115, local copies, waits for them, and re-layouts: 19.1 us -> 9.47 us
  transfers between devices with their start and end apart: 12 -> 11, of which waited for: 10 -> 8; matrix products, arithmetic and copies ran while one was open for 13% -> 21% of each run, Pallas kernels for 0% -> 0%
where the time goes in v2:
time: 708 us; the launch traced here: 701 us
  waiting for transfers between devices  368 us (52%)
  matrix products  165 us (23%)
  Pallas kernels  82.1 us (12%)
  other arithmetic  39.1 us (6%)
  local copies, waits for them, and re-layouts  16.8 us (2%)
  between operations  15.2 us (2%)
  blocking collectives  9.07 us (1%)
    reduce_scatter x1, waiting for transfers between devices, local(): lax.psum_scatter(weighted, 'ep', scatter_dimension=0, tiled=True)  106 us
    pallas_call x1, Pallas kernels, sum_everywhere(): pl.pallas_call(functools.partial(sum_kernel, count), out_shape=[jax.Shape...  82.1 us
    reduce_scatter x1, waiting for transfers between devices, local(): lax.psum_scatter(back, 'ep', scatter_dimension=0, tiled=True)  81.9 us
    all_gather x1, waiting for transfers between devices, local(): rows_all = lax.all_gather(moe_in, 'ep', axis=0, tiled=True)  75.4 us
    all_gather x1, waiting for transfers between devices, local(): upstream_all = lax.all_gather(cotangent, 'ep', axis=0, tiled=True)  67 us
    dot_general x2, matrix products, expert_pass(): jnp.einsum('tf,df->td', up_pre_grad[:, cut], up_w[j], preferred_element_t...  30.3 us
    dot_general x2, matrix products, expert_pass(): jnp.dot(hidden[:, j * width:(j + 1) * width], down_w[j], preferred_elemen...  29.2 us
    all_gather x1, waiting for transfers between devices, local(): gate_all = lax.all_gather(w_gate, 'hs', axis=0, tiled=True)  21.6 us
  transfers between devices with their start and end apart: 11, of which 8 were waited for; matrix products, arithmetic and copies ran while one was open for 21% of the time, Pallas kernels for 0%

profile of v2, /device:TPU:0, one launch (start us, length us, event | category | flops | bytes accessed | tf_op | source)
XLA Modules:
  0.0 700.5 jit_solution(13126120845333772895)
XLA Ops:
  16.5 2.6 fusion.75
  27.1 6.5 all-gather.10.cloned.1.call-done
  34.9 21.6 %all-gather.8.cloned.1.call-done = bf16[2,1024,256]{2,1,0:T(8,128)(2,1)} async-done(((bf16[1,1024,256]{2,1,0:T(8,128)(2,1)}), bf16[2,1024,256]{2,1,0:T(8,128)(2,1)}) %all-gather.8.cloned.1.call-update) | async-done | bytes 1048592 | tf_op jit(solution)/shard_map/all_gather | solution.py:384
  56.5 2.2 slice_bitcast_fusion.7
  58.8 75.4 %all-gather.6.cloned.1.call-done = bf16[4096,1024]{1,0:T(8,128)(2,1)} async-done(((bf16[256,1024]{1,0:T(8,128)(2,1)}), bf16[4096,1024]{1,0:T(8,128)(2,1)}) %all-gather.6.cloned.1.call-update) | async-done | bytes 8388624 | tf_op jit(solution)/shard_map/all_gather | solution.py:444
  134.2 8.0 %fusion.49 = f32[4096,512]{1,0:T(8,128)S(1)} fusion(bf16[4096,1024]{1,0:T(8,128)(2,1)} %all-gather.6.cloned.1.call-done, bf16[1024,256]{1,0:T(8,128)(2,1)} %get-tuple-element.89, bf16[1024,256]{1,0:T(8,128)(2,1)} %get-tuple-element.88), kind=kOutput, calls=%fused_computation.75 | convolution fusion | flops 4297064448 | bytes 17825792 | tf_op jit(solution)/shard_map/dot_general | solution.py:81
  142.2 3.2 copy-done.56
  145.4 8.8 %multiply_convert_fusion.3 = (bf16[4096,512]{1,0:T(8,128)(2,1)}, f32[4096,512]{1,0:T(8,128)}) fusion(f32[4096,512]{1,0:T(8,128)S(1)} %fusion.49, bf16[4096,1024]{1,0:T(8,128)(2,1)S(1)} %copy-done.55, bf16[1024,256]{1,0:T(8,128)(2,1)S(1)} %get-tuple-element.91, bf16[1024,256]{1,0:T(8,128)(2,1)S(1)} %get-tuple-element.90), kind=kOutput, calls=%fused_computation.9 | convolution fusion | flops 4309647360 | bytes 30408704 | tf_op jit(solution)/shard_map/dot_general | solution.py:82
  155.2 9.9 %fusion.22 = f32[4096,1024]{1,0:T(8,128)} fusion(bf16[4096,512]{1,0:T(8,128)(2,1)} %get-tuple-element.106, bf16[2,256,1024]{2,1,0:T(8,128)(2,1)} %all-gather.12.cloned.1.call-done), kind=kOutput, calls=%fused_computation.34 | convolution fusion | flops 2147483648 | bytes 19398656 | tf_op jit(solution)/shard_map/dot_general | solution.py:89
  165.1 67.0 %all-gather.14.cloned.1.call-done = bf16[4096,1024]{1,0:T(8,128)(2,1)} async-done(((bf16[256,1024]{1,0:T(8,128)(2,1)}), bf16[4096,1024]{1,0:T(8,128)(2,1)}) %all-gather.14.cloned.1.call-update) | async-done | bytes 8388624 | tf_op jit(solution)/shard_map/all_gather | solution.py:383
  232.1 19.3 %fusion.1 = (f32[4096]{0:T(1024)}, f32[4096,1024]{1,0:T(8,128)}) fusion(bf16[4096,1024]{1,0:T(8,128)(2,1)} %all-gather.14.cloned.1.call-done, bf16[2,256,1024]{2,1,0:T(8,128)(2,1)} %all-gather.12.cloned.1.call-done, bf16[4096,512]{1,0:T(8,128)(2,1)} %get-tuple-element.106, f32[4096,1024]{1,0:T(8,128)} %fusion.22), kind=kOutput, calls=%fused_computation.3 | convolution fusion | flops 2176839680 | bytes 44580864 | tf_op jit(solution)/shard_map/dot_general | solution.py:89
  251.4 3.5 all-to-all-start.1
  255.4 6.0 all-to-all-done.1
  261.7 9.1 %all_to_all.8 = f32[16,1,256]{2,1,0:T(1,128)S(1)} all-to-all(f32[16,1,256]{2,1,0:T(1,128)S(1)} %copy.79), channel_id=1, replica_groups=mesh['ep'=16,'hs'=2] {'ep'}, dimensions={0} | all-to-all | bytes 32768 | tf_op jit(solution)/shard_map/all_to_all | solution.py:445
  270.8 10.3 %fusion.26 = bf16[512,1024]{1,0:T(8,128)(2,1)} fusion(bf16[4096,512]{1,0:T(8,128)(2,1)} %get-tuple-element.106, bf16[4096,1024]{1,0:T(8,128)(2,1)} %all-gather.14.cloned.1.call-done, f32[4096]{0:T(1024)S(1)} %bitcast.191), kind=kOutput, calls=%fused_computation.51 | convolution fusion | flops 4308074496 | bytes 13647872 | tf_op jit(solution)/shard_map/tf,td->fd/dot_general | solution.py:101
  281.2 14.2 %multiply_convert_fusion.1 = (bf16[4096,512]{1,0:T(8,128)(2,1)S(1)}, bf16[4096,512]{1,0:T(8,128)(2,1)}) fusion(f32[4096,512]{1,0:T(8,128)} %copy-done.56, f32[4096,512]{1,0:T(8,128)} %get-tuple-element.107, bf16[512,1024]{1,0:T(8,128)(2,1)S(1)} %bitcast.176, bf16[4096,1024]{1,0:T(8,128)(2,1)} %all-gather.14.cloned.1.call-done, f32[4096]{0:T(1024)S(1)} %bitcast.192), kind=kOutput, calls=%fused_computation.7 | convolution fusion | flops 4334813184 | bytes 34619392 | tf_op jit(solution)/shard_map/td,fd->tf/dot_general | solution.py:96
  297.5 8.2 %convolution_convert_fusion.2 = bf16[1024,512]{1,0:T(8,128)(2,1)} fusion(bf16[4096,1024]{1,0:T(8,128)(2,1)} %all-gather.6.cloned.1.call-done, bf16[4096,512]{1,0:T(8,128)(2,1)S(1)} %get-tuple-element.80), kind=kOutput, calls=%fused_computation.47 | convolution fusion | flops 4295491584 | bytes 13631488 | tf_op jit(solution)/shard_map/td,tf->df/dot_general | solution.py:103
  305.9 10.5 %convolution_convert_fusion.3 = bf16[1024,512]{1,0:T(8,128)(2,1)} fusion(bf16[4096,1024]{1,0:T(8,128)(2,1)} %all-gather.6.cloned.1.call-done, bf16[4096,512]{1,0:T(8,128)(2,1)} %get-tuple-element.81), kind=kOutput, calls=%fused_computation.48 | convolution fusion | flops 4295491584 | bytes 13631488 | tf_op jit(solution)/shard_map/td,tf->df/dot_general | solution.py:102
  316.6 9.9 %fusion.17 = f32[4096,1024]{1,0:T(8,128)} fusion(bf16[4096,512]{1,0:T(8,128)(2,1)} %copy-done.12, bf16[2,1024,256]{2,1,0:T(8,128)(2,1)S(1)} %copy-done.14), kind=kOutput, calls=%fused_computation.29 | convolution fusion | flops 2147483648 | bytes 19398656 | tf_op jit(solution)/shard_map/tf,df->td/dot_general | solution.py:109
  326.5 8.3 %fusion.15 = f32[4096,1024]{1,0:T(8,128)} fusion(bf16[4096,512]{1,0:T(8,128)(2,1)S(1)} %copy-done.11, bf16[2,1024,256]{2,1,0:T(8,128)(2,1)S(1)} %copy-done.15), kind=kOutput, calls=%fused_computation.27 | convolution fusion | flops 2147483648 | bytes 19398656 | tf_op jit(solution)/shard_map/tf,df->td/dot_general | solution.py:108
  334.7 8.1 %fusion.19 = f32[4096,1024]{1,0:T(8,128)} fusion(bf16[4096,512]{1,0:T(8,128)(2,1)S(1)} %copy-done.11, bf16[2,1024,256]{2,1,0:T(8,128)(2,1)S(1)} %copy-done.15), kind=kOutput, calls=%fused_computation.31 | convolution fusion | flops 2147483648 | bytes 19398656 | tf_op jit(solution)/shard_map/tf,df->td/dot_general | solution.py:108
  342.9 20.4 %add_convert_fusion = bf16[4096,1024]{1,0:T(8,128)(2,1)} fusion(f32[4096,1024]{1,0:T(8,128)} %fusion.15, f32[4096,1024]{1,0:T(8,128)} %fusion.19, f32[4096,1024]{1,0:T(8,128)} %fusion.17, bf16[4096,512]{1,0:T(8,128)(2,1)S(1)} %copy-done.13, bf16[2,1024,256]{2,1,0:T(8,128)(2,1)S(1)} %copy-done.14), kind=kOutput, calls=%fused_computation.4 | convolution fusion | flops 2172649472 | bytes 61341696 | tf_op jit(solution)/shard_map/tf,df->td/dot_general | solution.py:109
  363.8 11.0 %multiply_convert_fusion = bf16[4096,1024]{1,0:T(8,128)(2,1)} fusion(f32[4096,1024]{1,0:T(8,128)} %get-tuple-element.109, f32[4096]{0:T(1024)S(1)} %bitcast.193), kind=kLoop, calls=%fused_computation.5 | loop fusion | flops 8388608 | bytes 25182208 | tf_op jit(solution)/shard_map/convert_element_type | solution.py:94
  383.3 81.9 %reduce-scatter.8.cloned.1.call-done = bf16[256,1024]{1,0:T(8,128)(2,1)} async-done(((bf16[4096,1024]{1,0:T(8,128)(2,1)}), bf16[256,1024]{1,0:T(8,128)(2,1)}) %reduce-scatter.8.cloned.1.call-update) | async-done | bytes 524304 | tf_op jit(solution)/shard_map/reduce_scatter | solution.py:452
  465.2 2.5 multiply_reduce_fusion
  467.7 106.3 %reduce-scatter.6.cloned.1.call-done = bf16[256,1024]{1,0:T(8,128)(2,1)} async-done(((bf16[4096,1024]{1,0:T(8,128)(2,1)}), bf16[256,1024]{1,0:T(8,128)(2,1)}) %reduce-scatter.6.cloned.1.call-update) | async-done | bytes 524304 | tf_op jit(solution)/shard_map/reduce_scatter | solution.py:451
  574.0 2.8 multiply_add_fusion
  580.0 3.1 fusion.37
  587.9 2.2 convolution_convert_fusion
  596.7 82.1 %sum_everywhere.1 = (bf16[64,16,1024]{2,1,0:T(8,128)(2,1)}, bf16[64,16,1024]{2,1,0:T(8,128)(2,1)}, bf16[64,16,512]{2,1,0:T(8,128)(2,1)}, bf16[64,16,512]{2,1,0:T(8,128)(2,1)}, f32[24,1024]{1,0:T(8,128)}) custom-call(bf16[64,16,1024]{2,1,0:T(8,128)(2,1)} %bitcast.160, bf16[64,16,1024]{2,1,0:T(8,128)(2,1)} %bitcast.161, bf16[64,16,512]{2,1,0:T(8,128)(2,1)} %bitcast.167, ...), custom_call_target="tpu_custom_call" | custom-call | tf_op jit(solution)/shard_map/sum_everywhere/pallas_call | solution.py:332
  684.5 6.3 bitcast_convert_fusion
  690.7 2.7 bitcast_convert_fusion.2
  (198 shorter events, 51.3 us)
Async XLA Ops:
  7.2 16.0 %copy-start = (bf16[1024,1024]{1,0:T(8,128)(2,1)S(1)}, bf16[1024,1024]{1,0:T(8,128)(2,1)}, u32[]{:S(2)}) copy-start(bf16[1024,1024]{1,0:T(8,128)(2,1)} %param.31) | copy-start | bytes 6291460
  7.2 7.3 %copy-start.3 = (bf16[256,1024]{1,0:T(8,128)(2,1)S(1)}, bf16[256,1024]{1,0:T(8,128)(2,1)}, u32[]{:S(2)}) copy-start(bf16[256,1024]{1,0:T(8,128)(2,1)} %param.23) | copy-start | bytes 1572868
  7.2 7.3 %copy-start.40 = (f32[1024]{0:T(1024)S(1)}, f32[1024]{0:T(1024)}, u32[]{:S(2)}) copy-start(f32[1024]{0:T(1024)} %param.27) | copy-start | bytes 12292
  7.2 26.4 %all-gather.10.cloned.1.call-start = ((), (), s32[]{:S(2)}) async-start(), calls=%async_computation.9 | async-start | bytes 1572864 | tf_op jit(solution)/shard_map/all_gather | solution.py:385
  8.0 48.6 %all-gather.8.cloned.1.call-start = ((), (), s32[]{:S(2)}) async-start(), calls=%async_computation.8 | async-start | bytes 1572864 | tf_op jit(solution)/shard_map/all_gather | solution.py:384
  8.7 125.5 %all-gather.6.cloned.1.call-start = ((), (), s32[]{:S(2)}) async-start(), calls=%async_computation.7 | async-start | bytes 8912896 | tf_op jit(solution)/shard_map/all_gather | solution.py:444
  11.6 7.5 %copy-start.47 = (f32[256]{0:T(256)}, f32[256]{0:T(256)S(1)}, u32[]{:S(2)}) copy-start(f32[256]{0:T(256)S(1)} %add_rsqrt_fusion.1) | copy-start | bytes 3076
  14.5 7.2 %copy-start.26 = (bf16[256,512]{0,1:T(8,128)(2,1)}, bf16[256,512]{0,1:T(8,128)(2,1)S(1)}, u32[]{:S(2)}) copy-start(bf16[256,512]{0,1:T(8,128)(2,1)S(1)} %copy.75) | copy-start | bytes 786436
  25.9 129.3 %all-gather.12.cloned.1.call-start = ((), (), s32[]{:S(2)}) async-start(), calls=%async_computation.10 | async-start | bytes 1572864 | tf_op jit(solution)/shard_map/all_gather | solution.py:386
  26.5 205.6 %all-gather.14.cloned.1.call-start = ((), (), s32[]{:S(2)}) async-start(), calls=%async_computation.12 | async-start | bytes 8912896 | tf_op jit(solution)/shard_map/all_gather | solution.py:383
  134.2 11.2 %copy-start.55 = (bf16[4096,1024]{1,0:T(8,128)(2,1)S(1)}, bf16[4096,1024]{1,0:T(8,128)(2,1)}, u32[]{:S(2)}) copy-start(bf16[4096,1024]{1,0:T(8,128)(2,1)} %all-gather.6.cloned.1.call-done) | copy-start | bytes 25165828
  165.1 90.1 %copy-start.10 = (bf16[256,1024]{1,0:T(8,128)(2,1)S(1)}, bf16[256,1024]{1,0:T(8,128)(2,1)}, u32[]{:S(2)}) copy-start(bf16[256,1024]{1,0:T(8,128)(2,1)} %multiply_convert_fusion.4) | copy-start | bytes 1572868
  165.1 90.1 %copy-start.42 = (bf16[1024,16]{0,1:T(8,128)(2,1)S(1)}, bf16[1024,16]{0,1:T(8,128)(2,1)}, u32[]{:S(2)}) copy-start(bf16[1024,16]{0,1:T(8,128)(2,1)} %param.33) | copy-start | bytes 98308
  165.1 90.3 %copy-start.54 = (s32[1,256]{1,0:T(1,128)S(1)}, s32[1,256]{1,0:T(1,128)}, u32[]{:S(2)}) copy-start(s32[1,256]{1,0:T(1,128)} %param.25) | copy-start | bytes 3076
  165.1 96.3 %copy-start.51 = (s32[256,8]{0,1:T(8,128)S(1)}, s32[256,8]{0,1:T(8,128)}, u32[]{:S(2)}) copy-start(s32[256,8]{0,1:T(8,128)} %param.26) | copy-start | bytes 24580
  251.4 10.0 %all-to-all-start.1 = ((f32[16,1,256]{2,1,0:T(1,128)}), f32[16,1,256]{2,1,0:T(1,128)S(1)}, u32[]{:S(2)}, u32[]{:S(2)}) async-start(f32[16,1,256]{2,1,0:T(1,128)} %bitcast.24), calls=%async_computation.3 | async-start | bytes 32768 | tf_op jit(solution)/shard_map/all_to_all | solution.py:455
  255.0 121.9 %reduce-scatter.14.cloned.1.call-start = ((), (), s32[]{:S(2)}) async-start(), calls=%async_computation.16 | async-start | bytes 1572864 | tf_op jit(solution)/shard_map/reduce_scatter | solution.py:115
  270.8 10.4 %copy-start.20 = (bf16[2,256,1024]{2,1,0:T(8,128)(2,1)S(1)}, bf16[2,256,1024]{2,1,0:T(8,128)(2,1)}, u32[]{:S(2)}) copy-start(bf16[2,256,1024]{2,1,0:T(8,128)(2,1)} %all-gather.12.cloned.1.call-done) | copy-start | bytes 3145732
  281.2 97.9 %reduce-scatter.12.cloned.1.call-start = ((), (), s32[]{:S(2)}) async-start(), calls=%async_computation.15 | async-start | bytes 1572864 | tf_op jit(solution)/shard_map/reduce_scatter | solution.py:115
  305.7 75.5 %reduce-scatter.10.cloned.1.call-start = ((), (), s32[]{:S(2)}) async-start(), calls=%async_computation.14 | async-start | bytes 1572864 | tf_op jit(solution)/shard_map/reduce_scatter | solution.py:115
  305.9 10.6 %copy-start.14 = (bf16[2,1024,256]{2,1,0:T(8,128)(2,1)S(1)}, bf16[2,1024,256]{2,1,0:T(8,128)(2,1)}, u32[]{:S(2)}) copy-start(bf16[2,1024,256]{2,1,0:T(8,128)(2,1)} %all-gather.10.cloned.1.call-done) | copy-start | bytes 3145732
  316.5 148.7 %reduce-scatter.8.cloned.1.call-start = ((), (), s32[]{:S(2)}) async-start(), calls=%async_computation.13 | async-start | bytes 8912896 | tf_op jit(solution)/shard_map/reduce_scatter | solution.py:452
  316.5 9.9 %copy-start.11 = (bf16[4096,512]{1,0:T(8,128)(2,1)S(1)}, bf16[4096,512]{1,0:T(8,128)(2,1)}, u32[]{:S(2)}) copy-start(bf16[4096,512]{1,0:T(8,128)(2,1)} %get-tuple-element.81) | copy-start | bytes 12582916
  316.5 9.9 %copy-start.15 = (bf16[2,1024,256]{2,1,0:T(8,128)(2,1)S(1)}, bf16[2,1024,256]{2,1,0:T(8,128)(2,1)}, u32[]{:S(2)}) copy-start(bf16[2,1024,256]{2,1,0:T(8,128)(2,1)} %all-gather.8.cloned.1.call-done) | copy-start | bytes 3145732
  334.7 8.1 %copy-start.13 = (bf16[4096,512]{1,0:T(8,128)(2,1)S(1)}, bf16[4096,512]{1,0:T(8,128)(2,1)}, u32[]{:S(2)}) copy-start(bf16[4096,512]{1,0:T(8,128)(2,1)} %copy-done.12) | copy-start | bytes 12582916
  363.3 210.7 %reduce-scatter.6.cloned.1.call-start = ((), (), s32[]{:S(2)}) async-start(), calls=%async_computation.11 | async-start | bytes 8912896 | tf_op jit(solution)/shard_map/reduce_scatter | solution.py:451
  374.8 90.4 %copy-start.6 = (f32[256,1024]{1,0:T(8,128)S(1)}, f32[256,1024]{1,0:T(8,128)}, u32[]{:S(2)}) copy-start(f32[256,1024]{1,0:T(8,128)} %copy-done.5) | copy-start | bytes 3145732
  374.8 90.4 %copy-start.50 = (f32[1024]{0:T(1024)S(1)}, f32[1024]{0:T(1024)}, u32[]{:S(2)}) copy-start(f32[1024]{0:T(1024)} %param.32) | copy-start | bytes 12292
  374.8 90.4 %copy-start.53 = (f32[256]{0:T(256)S(1)}, f32[256]{0:T(256)}, u32[]{:S(2)}) copy-start(f32[256]{0:T(256)} %copy-done.52) | copy-start | bytes 3076
  596.1 87.0 %copy-start.8 = (f32[256,1024]{1,0:T(8,128)S(1)}, f32[256,1024]{1,0:T(8,128)}, u32[]{:S(2)}) copy-start(f32[256,1024]{1,0:T(8,128)} %copy-done.7) | copy-start | bytes 3145732
  596.1 87.0 %copy-start.16 = (f32[256,1024]{1,0:T(8,128)S(1)}, f32[256,1024]{1,0:T(8,128)}, u32[]{:S(2)}) copy-start(f32[256,1024]{1,0:T(8,128)} %get-tuple-element.113) | copy-start | bytes 3145732
  684.5 6.3 copy-start.30
  (36 other events, 76.2 us)
Sparse Core Ops, SparseCore 0:
  9.6 23.9 all-gather.9
  35.2 21.2 all-gather.7
  59.3 74.8 all-gather.5
  135.6 19.5 all-gather.11
  157.2 74.8 all-gather.13
  281.3 17.5 reduce-scatter.13
  305.8 17.5 reduce-scatter.11
  326.2 20.2 reduce-scatter.9
  363.4 101.7 reduce-scatter.7
  469.6 104.3 reduce-scatter.5

commit v3 on v2

--- a/solution.py
+++ b/solution.py
@@ -358,6 +358,419 @@
     return [o.reshape(a.shape).astype(jnp.float32) for o, a in zip(out, arrays)] + [out[-1]]
 
 
+def contract(left, right, left_dim, right_dim):
+    return lax.dot_general(
+        left, right, (((left_dim,), (right_dim,)), ((), ())), preferred_element_type=jnp.float32
+    )
+
+
+def expert_kernel(
+    rows_in,
+    upstream_in,
+    gates_in,
+    gate_w,
+    up_w,
+    down_w,
+    weighted_out,
+    back_out,
+    slope_out,
+    gate_out,
+    up_out,
+    down_out,
+    streams,
+    gates,
+    slopes,
+    slopes_in,
+    w_gate,
+    w_up,
+    w_down,
+    sums,
+    partial,
+    from_sibling,
+    from_line,
+    staged,
+    returned,
+    load_sem,
+    gather_send,
+    gather_recv,
+    gate_send,
+    gate_recv,
+    slope_send,
+    slope_recv,
+    weight_send,
+    weight_recv,
+    pair_send,
+    pair_recv,
+    line_send,
+    line_recv,
+    grad_send,
+    grad_recv,
+):
+    z, x, c, y = place()
+    near, far, last = 1 + z % 2, (2 + 3 * z) % 5, 3 - 3 * (z // 2)
+    middle = (z == 1) | (z == 2)
+    edge = (z == 0) | (z == 3)
+    sibling, beside, across = device(z, x, 1 - c, y), device(z, 1 - x, c, y), device(z, x, c, 1 - y)
+    corner = device(z, 1 - x, c, 1 - y)
+    line = [((z + k) % 4, (c + d) % 2) for k in range(4) for d in range(2) if k or d]
+    greet([device(a, x, b, y) for a, b in line] + [beside, across, corner])
+
+    def chip(k):
+        half = z // 2
+        inner = z + half * (3 - 2 * z)
+        spot = k + inner * (1 - 3 * (k // 2) + 2 * (k // 3))
+        return spot + half * (3 - 2 * spot)
+
+    def remote(source, target, send, recv, peer):
+        return pltpu.make_async_remote_copy(
+            src_ref=source, dst_ref=target, send_sem=send, recv_sem=recv, device_id=peer, device_id_type=MESH
+        )
+
+    own = [
+        pltpu.make_async_copy(ref, streams.at[s, z, c], load_sem.at[s])
+        for s, ref in enumerate((rows_in, upstream_in))
+    ]
+    gates_own = pltpu.make_async_copy(gates_in.at[z, c], gates.at[z, c], load_sem.at[2])
+    weights_own = [
+        pltpu.make_async_copy(ref, held.at[x, y], load_sem.at[3 + a])
+        for a, (ref, held) in enumerate(((gate_w, w_gate), (up_w, w_up), (down_w, w_down)))
+    ]
+    for copy in (*own, gates_own, *weights_own):
+        copy.start()
+
+    def gather(s, block, slot, peer):
+        piece = streams.at[s, block, c]
+        return remote(piece, piece, gather_send.at[s, slot], gather_recv.at[s, block, c], peer)
+
+    def arrive(s, block, core):
+        piece = streams.at[s, block, core]
+        pltpu.make_async_copy(piece, piece, gather_recv.at[s, block, core]).wait()
+
+    for s in (0, 1):
+        own[s].wait()
+        gather(s, z, 0, device(near, x, c, y)).start()
+        gather(s, z, 1, device(far, x, c, y)).start()
+        gather(s, z, 2, sibling).start()
+    gate_copies = [
+        remote(
+            gates_in.at[a, b], gates.at[z, c], gate_send.at[n], gate_recv.at[z, c], device(a, x, b, y)
+        )
+        for n, (a, b) in enumerate(line)
+    ]
+    for copy in gate_copies:
+        copy.start()
+    weight_copies = []
+    for a, held in enumerate((w_gate, w_up, w_down)):
+        weights_own[a].wait()
+        for n, peer in enumerate((across, beside, corner)):
+            piece = held.at[x, y]
+            weight_copies.append(
+                remote(piece, piece, weight_send.at[n, a], weight_recv.at[x, y, a], peer)
+            )
+    for n in range(3):
+        for a in range(3):
+            weight_copies[a * 3 + n].start()
+
+    def weights_here(expert, group):
+        for a, held in enumerate((w_gate, w_up, w_down)):
+            piece = held.at[expert, group]
+            pltpu.make_async_copy(piece, piece, weight_recv.at[expert, group, a]).wait()
+
+    def zero(u, carry):
+        for e in (0, 1):
+            for a in range(3):
+                sums[e, a, u // 16, pl.ds(pl.multiple_of((u % 16) * 16, 16), 16), :] = jnp.zeros(
+                    (16, 1024), jnp.float32
+                )
+        return carry
+
+    lax.fori_loop(0, 32, zero, 0)
+
+    def handle(k):
+        block = chip(k)
+        for s in (0, 1):
+            arrive(s, block, c)
+            gather(s, block, 4 + k, sibling).start()
+            if k != 2:
+
+                @pl.when(middle)
+                def _():
+                    gather(s, block, 2 + (k + 1) // 2, device(far, x, c, y)).start()
+
+    handle(1)
+    gates_own.wait()
+    for a, b in line:
+        pltpu.make_async_copy(gates.at[a, b], gates.at[a, b], gate_recv.at[a, b]).wait()
+    weights_here(x, 1 - y)
+    row_id = lax.broadcasted_iota(jnp.int32, (256, 256), 0)
+    lane_id = lax.broadcasted_iota(jnp.int32, (256, 256), 1)
+
+    def compute(expert, block, core, first):
+        diagonal = row_id == lane_id
+        gate_row = gates[block, core, pl.ds(expert, 1), :]
+        gate = jnp.sum(jnp.where(diagonal, gate_row, 0.0), axis=1, keepdims=True)
+        rows = streams[0, block, core]
+        total = jnp.zeros((256, 1024), jnp.float32)
+        kept = []
+        for j in (0, 1):
+            gate_pre = contract(rows, w_gate[expert, j], 1, 0)
+            up_pre = contract(rows, w_up[expert, j], 1, 0)
+            sigmoid_part = jax.nn.sigmoid(gate_pre)
+            activated = gate_pre * sigmoid_part
+            hidden = (activated * up_pre).astype(jnp.bfloat16)
+            part = contract(hidden, w_down[expert, j], 1, 0)
+            total = total + part.astype(jnp.bfloat16).astype(jnp.float32)
+            inner = up_pre * sigmoid_part * (1.0 + gate_pre * (1.0 - sigmoid_part))
+            kept.append((activated, inner, hidden))
+        total = total.astype(jnp.bfloat16).astype(jnp.float32)
+        upstream = streams[1, block, core].astype(jnp.float32)
+        slope = jnp.sum(upstream * total, axis=1, keepdims=True)
+        slopes[block, core, pl.ds(expert, 1), :] = jnp.sum(
+            jnp.where(diagonal, slope, 0.0), axis=0, keepdims=True
+        )
+        weighted = gate * total
+        if not first:
+            weighted = weighted + partial[1, block, core].astype(jnp.float32)
+        partial[1, block, core] = weighted.astype(jnp.bfloat16)
+        upstream = (gate * upstream).astype(jnp.bfloat16)
+        back = jnp.zeros((256, 1024), jnp.float32)
+        for j in (0, 1):
+            activated, inner, hidden = kept[j]
+            hidden_grad = contract(upstream, w_down[expert, j], 1, 1)
+            up_grad = (hidden_grad * activated).astype(jnp.bfloat16)
+            gate_grad = (hidden_grad * inner).astype(jnp.bfloat16)
+            sums[expert, 0, j] += contract(gate_grad, rows, 0, 0)
+            sums[expert, 1, j] += contract(up_grad, rows, 0, 0)
+            sums[expert, 2, j] += contract(hidden, upstream, 0, 0)
+            step = contract(gate_grad, w_gate[expert, j], 1, 1) + contract(up_grad, w_up[expert, j], 1, 1)
+            back = back + step.astype(jnp.bfloat16).astype(jnp.float32)
+        if not first:
+            back = back + partial[0, block, core].astype(jnp.float32)
+        partial[0, block, core] = back.astype(jnp.bfloat16)
+
+    def first_pass(i, carry):
+        k = i // 2
+        block, core = chip(k), (c + i) % 2
+
+        @pl.when(i == 1)
+        def _():
+            for s in (0, 1):
+                arrive(s, z, 1 - c)
+
+        @pl.when((i == 2) & middle | (i == 4) & edge)
+        def _():
+            handle(2)
+
+        @pl.when((i == 4) & middle | (i == 6) & edge)
+        def _():
+            handle(3)
+
+        @pl.when((i % 2 == 1) & (i > 1))
+        def _():
+            for s in (0, 1):
+                arrive(s, block, 1 - c)
+
+        compute(x, block, core, True)
+        return carry
+
+    lax.fori_loop(0, 8, first_pass, 0)
+
+    def stage_grads(place_at, expert, group):
+        def body(u, carry):
+            at = pl.ds(pl.multiple_of(u * 32, 32), 32)
+            for a in range(3):
+                staged[place_at, a, at, :] = sums[expert, a, group, at, :].astype(jnp.bfloat16)
+            return carry
+
+        lax.fori_loop(0, 8, body, 0)
+
+    def grad_copy(n, a, peer):
+        return remote(staged.at[n, a], returned.at[n, a], grad_send.at[n, a], grad_recv.at[n, a], peer)
+
+    stage_grads(0, x, 1 - y)
+    for a in range(3):
+        grad_copy(0, a, across).start()
+    weights_here(1 - x, y)
+    weights_here(1 - x, 1 - y)
+
+    def pair_copy(s, block):
+        return remote(
+            partial.at[s, block, 1 - c],
+            from_sibling.at[s, block],
+            pair_send.at[s, block],
+            pair_recv.at[s, block],
+            sibling,
+        )
+
+    def line_copy(s, block):
+        return remote(
+            partial.at[s, block, c],
+            from_line.at[s, z],
+            line_send.at[s, block],
+            line_recv.at[s, z],
+            device(block, x, c, y),
+        )
+
+    def second_pass(i, carry):
+        block, core = chip(3 - i // 2), (c + 1 + i) % 2
+        compute(1 - x, block, core, False)
+
+        @pl.when(i % 2 == 0)
+        def _():
+            for s in (0, 1):
+                pair_copy(s, block).start()
+
+        @pl.when((i % 2 == 1) & (i < 6))
+        def _():
+            for s in (0, 1):
+                pair_copy(s, block).wait_recv()
+
+                def body(u, inner_carry):
+                    at = pl.ds(pl.multiple_of(u * 32, 32), 32)
+                    value = partial[s, block, c, at, :].astype(jnp.float32)
+                    value = value + from_sibling[s, block, at, :].astype(jnp.float32)
+                    partial[s, block, c, at, :] = value.astype(jnp.bfloat16)
+                    return inner_carry
+
+                lax.fori_loop(0, 8, body, 0)
+                line_copy(s, block).start()
+
+        return carry
+
+    lax.fori_loop(0, 8, second_pass, 0)
+    stage_grads(1, 1 - x, y)
+    for a in range(3):
+        grad_copy(1, a, beside).start()
+    stage_grads(2, 1 - x, 1 - y)
+    for a in range(3):
+        grad_copy(2, a, corner).start()
+    slope_copies = [
+        remote(
+            slopes.at[a, b], slopes_in.at[z, c], slope_send.at[n], slope_recv.at[z, c], device(a, x, b, y)
+        )
+        for n, (a, b) in enumerate(line)
+    ]
+    for copy in slope_copies:
+        copy.start()
+    slopes_in[z, c] = slopes[z, c]
+    for s in (0, 1):
+        pair_copy(s, z).wait_recv()
+        for k in (1, 2, 3):
+            source = chip(k)
+            pltpu.make_async_copy(from_line.at[s, source], from_line.at[s, source], line_recv.at[s, source]).wait()
+
+        def body(u, carry):
+            at = pl.ds(pl.multiple_of(u * 32, 32), 32)
+            value = partial[s, z, c, at, :].astype(jnp.float32)
+            value = value + from_sibling[s, z, at, :].astype(jnp.float32)
+            for k in (1, 2, 3):
+                value = value + from_line[s, chip(k), at, :].astype(jnp.float32)
+            (back_out, weighted_out)[s][at, :] = value
+            return carry
+
+        lax.fori_loop(0, 8, body, 0)
+    for a, b in line:
+        pltpu.make_async_copy(slopes_in.at[a, b], slopes_in.at[a, b], slope_recv.at[a, b]).wait()
+    slope_out[...] = slopes_in[...]
+    stores = []
+    for a, out in enumerate((gate_out, up_out, down_out)):
+        for n, peer in enumerate((across, beside, corner)):
+            grad_copy(n, a, peer).wait_recv()
+
+        def body(u, carry):
+            at = pl.ds(pl.multiple_of(u * 32, 32), 32)
+            value = sums[x, a, y, at, :]
+            for n in range(3):
+                value = value + returned[n, a, at, :].astype(jnp.float32)
+            sums[x, a, y, at, :] = value
+            return carry
+
+        lax.fori_loop(0, 8, body, 0)
+        stores.append(pltpu.make_async_copy(sums.at[x, a, y], out, load_sem.at[a]))
+        stores[a].start()
+    for s in (0, 1):
+        gather(s, z, 0, device(near, x, c, y)).wait_send()
+        gather(s, z, 1, device(far, x, c, y)).wait_send()
+        gather(s, z, 2, sibling).wait_send()
+        for k in (1, 2, 3):
+            gather(s, chip(k), 4 + k, sibling).wait_send()
+            line_copy(s, chip(k)).wait_send()
+
+        @pl.when(middle)
+        def _():
+            for k in (1, 3):
+                gather(s, chip(k), 2 + (k + 1) // 2, device(far, x, c, y)).wait_send()
+
+        for k in range(4):
+            pair_copy(s, chip(k)).wait_send()
+    for copy in (*gate_copies, *weight_copies, *slope_copies):
+        copy.wait_send()
+    for n, peer in enumerate((across, beside, corner)):
+        for a in range(3):
+            grad_copy(n, a, peer).wait_send()
+    for copy in stores:
+        copy.wait()
+
+
+def expert_part(rows, upstream, gates, gate_w, up_w, down_w):
+    tokens, model_dim = rows.shape
+    width = gate_w.shape[1]
+    vmem, anywhere = pl.BlockSpec(memory_space=pltpu.VMEM), pl.BlockSpec(memory_space=pl.ANY)
+    f32, bf16, dma = jnp.float32, jnp.bfloat16, pltpu.SemaphoreType.DMA
+    grad = jax.ShapeDtypeStruct((width, model_dim), f32)
+    by_owner = gates.T.reshape(4, 2, 2, tokens).swapaxes(1, 2)
+    by_owner = jnp.pad(by_owner, ((0, 0), (0, 0), (0, 6), (0, 0)))
+    weighted, back, slopes, gate_grad, up_grad, down_grad = pl.pallas_call(
+        expert_kernel,
+        out_shape=[
+            jax.ShapeDtypeStruct((tokens, model_dim), f32),
+            jax.ShapeDtypeStruct((tokens, model_dim), f32),
+            jax.ShapeDtypeStruct((4, 2, 8, tokens), f32),
+            grad,
+            grad,
+            grad,
+        ],
+        in_specs=[anywhere, anywhere, vmem, anywhere, anywhere, anywhere],
+        out_specs=[vmem, vmem, vmem, anywhere, anywhere, anywhere],
+        scratch_shapes=[
+            pltpu.VMEM((2, 4, 2, tokens, model_dim), bf16),
+            pltpu.VMEM((4, 2, 8, tokens), f32),
+            pltpu.VMEM((4, 2, 8, tokens), f32),
+            pltpu.VMEM((4, 2, 8, tokens), f32),
+            pltpu.VMEM((2, 2, model_dim, width), bf16),
+            pltpu.VMEM((2, 2, model_dim, width), bf16),
+            pltpu.VMEM((2, 2, width, model_dim), bf16),
+            pltpu.VMEM((2, 3, 2, width, model_dim), f32),
+            pltpu.VMEM((2, 4, 2, tokens, model_dim), bf16),
+            pltpu.VMEM((2, 4, tokens, model_dim), bf16),
+            pltpu.VMEM((2, 4, tokens, model_dim), bf16),
+            pltpu.VMEM((3, 3, width, model_dim), bf16),
+            pltpu.VMEM((3, 3, width, model_dim), bf16),
+            dma((6,)),
+            dma((2, 8)),
+            dma((2, 4, 2)),
+            dma((7,)),
+            dma((4, 2)),
+            dma((7,)),
+            dma((4, 2)),
+            dma((3, 3)),
+            dma((2, 2, 3)),
+            dma((2, 4)),
+            dma((2, 4)),
+            dma((2, 4)),
+            dma((2, 4)),
+            dma((3, 3)),
+            dma((3, 3)),
+        ],
+        compiler_params=pltpu.CompilerParams(
+            collective_id=1, has_side_effects=True, vmem_limit_bytes=62 << 20
+        ),
+        name="expert_part",
+    )(rows, upstream, by_owner, gate_w, up_w, down_w)
+    slopes = slopes[:, :, :2].swapaxes(1, 2).reshape(gates.shape[1], tokens).T
+    return (weighted, back, slopes, gate_grad.T, up_grad.T, down_grad)
+
+
 def local(
     tokens,
     segment_ids,
@@ -380,10 +793,7 @@
     experts_all = router.shape[1]
     query_per_key_head = QUERY_HEADS // KEY_VALUE_HEADS
     score_scale = HEAD_SIZE ** (-0.5)
-    upstream_all = lax.all_gather(cotangent, "ep", axis=0, tiled=True)
-    gate_all = lax.all_gather(w_gate, "hs", axis=0, tiled=True)
-    up_all = lax.all_gather(w_up, "hs", axis=0, tiled=True)
-    down_all = lax.all_gather(w_down, "hs", axis=0, tiled=True)
+    special = lax.axis_size("ep") == 16 and lax.axis_size("hs") == 2
     segment = segment_ids[0]
     live_row = live_mask[0]
     inputs = tokens.astype(jnp.float32)
@@ -441,24 +851,34 @@
     route_gates = route_soft * live_column
     counts_local = jnp.sum(route_hot * live_column[:, :, None], axis=(0, 1))
     dense_gates = jnp.sum(route_hot * route_gates[:, :, None], axis=1)
-    rows_all = lax.all_gather(moe_in, "ep", axis=0, tiled=True)
-    gates_all = lax.all_to_all(
-        dense_gates.T.reshape(experts_all, 1, sequence_length), "ep", split_axis=0, concat_axis=1, tiled=True
-    ).reshape(-1)
-    weighted, back, gate_upstream_all, gate_w_grad, up_w_grad, down_w_grad = expert_pass(
-        rows_all, upstream_all, gates_all, gate_all, up_all, down_all
-    )
-    combined = lax.psum_scatter(weighted, "ep", scatter_dimension=0, tiled=True).astype(jnp.float32)
-    expert_input_grad = lax.psum_scatter(back, "ep", scatter_dimension=0, tiled=True).astype(jnp.float32)
+    if special:
+        combined, expert_input_grad, gate_upstream_dense, gate_w_grad, up_w_grad, down_w_grad = expert_part(
+            moe_in, cotangent, dense_gates, w_gate[0], w_up[0], w_down[0]
+        )
+        gate_w_grad, up_w_grad, down_w_grad = gate_w_grad[None], up_w_grad[None], down_w_grad[None]
+    else:
+        upstream_all = lax.all_gather(cotangent, "ep", axis=0, tiled=True)
+        gate_all = lax.all_gather(w_gate, "hs", axis=0, tiled=True)
+        up_all = lax.all_gather(w_up, "hs", axis=0, tiled=True)
+        down_all = lax.all_gather(w_down, "hs", axis=0, tiled=True)
+        rows_all = lax.all_gather(moe_in, "ep", axis=0, tiled=True)
+        gates_all = lax.all_to_all(
+            dense_gates.T.reshape(experts_all, 1, sequence_length), "ep", split_axis=0, concat_axis=1, tiled=True
+        ).reshape(-1)
+        weighted, back, gate_upstream_all, gate_w_grad, up_w_grad, down_w_grad = expert_pass(
+            rows_all, upstream_all, gates_all, gate_all, up_all, down_all
+        )
+        combined = lax.psum_scatter(weighted, "ep", scatter_dimension=0, tiled=True).astype(jnp.float32)
+        expert_input_grad = lax.psum_scatter(back, "ep", scatter_dimension=0, tiled=True).astype(jnp.float32)
+        gate_upstream_dense = lax.all_to_all(
+            gate_upstream_all.reshape(experts_all, 1, sequence_length), "ep", split_axis=0, concat_axis=1, tiled=True
+        ).reshape(experts_all, sequence_length).T
+        gate_w_grad = sum_halves(gate_w_grad, 1)[None]
+        up_w_grad = sum_halves(up_w_grad, 1)[None]
+        down_w_grad = sum_halves(down_w_grad, 0)[None]
     output = (middle + combined).astype(jnp.bfloat16)
     upstream = cotangent.astype(jnp.float32)
-    gate_upstream_dense = lax.all_to_all(
-        gate_upstream_all.reshape(experts_all, 1, sequence_length), "ep", split_axis=0, concat_axis=1, tiled=True
-    ).reshape(experts_all, sequence_length).T
     gate_upstream = jnp.sum(route_hot * gate_upstream_dense[:, None, :], axis=-1)
-    gate_w_grad = sum_halves(gate_w_grad, 1)[None]
-    up_w_grad = sum_halves(up_w_grad, 1)[None]
-    down_w_grad = sum_halves(down_w_grad, 0)[None]
     soft_upstream = gate_upstream * live_column
     chosen_grad = route_soft * (
         soft_upstream - jnp.sum(route_soft * soft_upstream, axis=-1, keepdims=True)
@@ -540,7 +960,7 @@
     )
     input_norm_grad, attn_gain_grad = rms_backward(inputs, inverse_one, attn_gain, normed_grad)
     input_grad = middle_grad + input_norm_grad
-    if lax.axis_size("ep") == 16 and lax.axis_size("hs") == 2:
+    if special:
         small = jnp.zeros((24, model_dim), jnp.float32)
         small = small.at[:experts_all].set(router_w_grad.T)
         small = small.at[16].set(attn_gain_grad).at[17].set(moe_gain_grad)

time: 708 us -> 389 us (0.55)
  waiting for transfers between devices: 368 us -> 0 us
  Pallas kernels: 82.1 us -> 324 us
  matrix products: 165 us -> 26.5 us
  other arithmetic: 39.1 us -> 18.8 us
  between operations: 15.2 us -> 1.28 us
  blocking collectives: 9.07 us -> 0 us
    pallas_call x0 -> x1, Pallas kernels: none -> 206 us  [expert_part(): pl.pallas_call(expert_kernel, out_shape=[jax.ShapeDtypeStruct((tokens, mo...]
    reduce_scatter x5 -> x0, waiting for transfers between devices: 188 us -> none  [the longest x1 106 us: local(): lax.psum_scatter(weighted, 'ep', scatter_dimension=0, tiled=True)]
    all_gather x5 -> x0, waiting for transfers between devices: 172 us -> none  [the longest x1 75.4 us: local(): rows_all = lax.all_gather(moe_in, 'ep', axis=0, tiled=True)]
    dot_general x12 -> x0, matrix products: 136 us -> none  [the longest x2 30.3 us: expert_pass(): jnp.einsum('tf,df->td', up_pre_grad[:, cut], up_w[j], preferred_element_t...]
    pallas_call x1, Pallas kernels: 82.1 us -> 118 us  [sum_everywhere(): pl.pallas_call(functools.partial(sum_kernel, count), out_shape=[jax.Shape...]
    convert_element_type x1 -> x0, other arithmetic: 11 us -> none  [expert_pass(): weighted = (gates[:, None] * total).astype(jnp.bfloat16)]
    all_to_all x1 -> x0, blocking collectives: 9.07 us -> none  [local(): lax.all_to_all(dense_gates.T.reshape(experts_all, 1, sequence_length), 'e...]
  transfers between devices with their start and end apart: 11 -> 0, of which waited for: 8 -> 0; matrix products, arithmetic and copies ran while one was open for 21% -> 0% of each run, Pallas kernels for 0% -> 0%
where the time goes in v3:
time: 389 us; the launch traced here: 388 us
  Pallas kernels  324 us (83%)
  matrix products  26.5 us (7%)
  other arithmetic  18.8 us (5%)
  local copies, waits for them, and re-layouts  17 us (4%)
    pallas_call x1, Pallas kernels, expert_part(): pl.pallas_call(expert_kernel, out_shape=[jax.ShapeDtypeStruct((tokens, mo...  206 us
    pallas_call x1, Pallas kernels, sum_everywhere(): pl.pallas_call(functools.partial(sum_kernel, count), out_shape=[jax.Shape...  118 us
    unnamed x69, local copies, waits for them, and re-layouts  11.3 us
    convert_element_type x2, other arithmetic, sum_everywhere(): o.reshape(a.shape).astype(jnp.float32)  9.55 us

profile of v3, /device:TPU:0, one launch (start us, length us, event | category | flops | bytes accessed | tf_op | source)
XLA Modules:
  0.0 387.7 jit_solution(17352072916965752565)
XLA Ops:
  0.7 1.3 fusion.25
  2.0 1.6 convolution_convert_fusion.5
  3.8 2.9 fusion.45
  8.2 0.8 fusion.51
  9.6 0.9 fusion.9
  11.0 1.2 copy-done.5
  12.2 0.8 multiply_reduce_fusion.2
  13.1 1.0 copy-done.4
  14.2 0.8 copy-done.8
  16.1 206.2 %expert_part.1 = (f32[256,1024]{1,0:T(8,128)}, f32[256,1024]{1,0:T(8,128)}, f32[4,2,8,256]{3,2,1,0:T(8,128)}, f32[256,1024]{1,0:T(8,128)}, f32[256,1024]{1,0:T(8,128)}, /*index=5*/f32[256,1024]{1,0:T(8,128)}) custom-call(bf16[256,1024]{1,0:T(8,128)(2,1)} %copy-done.8, bf16[256,1024]{1,0:T(8,128)(2,1)} %upstream_in.1, f32[4,2,8,256]{3,2,1,0:T(8,128)} %pad.14.gates_in, ...), custom_call_target="tpu_custom_call" | custom-call | tf_op jit(solution)/shard_map/expert_part/pallas_call | solution.py:723
  222.3 0.8 slice_bitcast_fusion.1
  223.4 2.2 multiply_reduce_fusion
  225.6 2.9 multiply_add_fusion
  228.6 1.6 convolution_convert_fusion.4
  230.2 1.2 copy.69
  231.4 3.4 fusion
  234.9 1.0 fusion.2
  236.7 0.9 copy-done.7
  238.4 0.8 fusion.13
  239.7 0.8 fusion.17
  241.3 1.3 fusion.24
  242.6 2.0 convolution_convert_fusion.1
  244.6 2.2 convolution_convert_fusion
  246.8 1.6 convolution_convert_fusion.3
  248.4 1.6 convolution_convert_fusion.2
  251.5 118.0 %sum_everywhere.1 = (bf16[64,16,1024]{2,1,0:T(8,128)(2,1)}, bf16[64,16,1024]{2,1,0:T(8,128)(2,1)}, bf16[64,16,512]{2,1,0:T(8,128)(2,1)}, bf16[64,16,512]{2,1,0:T(8,128)(2,1)}, f32[24,1024]{1,0:T(8,128)}) custom-call(bf16[64,16,1024]{2,1,0:T(8,128)(2,1)} %bitcast.129, bf16[64,16,1024]{2,1,0:T(8,128)(2,1)} %bitcast.130, bf16[64,16,512]{2,1,0:T(8,128)(2,1)} %bitcast.135, ...), custom_call_target="tpu_custom_call" | custom-call | tf_op jit(solution)/shard_map/sum_everywhere/pallas_call | solution.py:332
  369.5 1.4 fusion.50
  371.0 6.8 %bitcast_convert_fusion = (f32[1024,1024]{1,0:T(8,128)}, f32[1024,1024]{1,0:T(8,128)}) fusion(bf16[64,16,1024]{2,1,0:T(8,128)(2,1)} %get-tuple-element.79, bf16[64,16,1024]{2,1,0:T(8,128)(2,1)} %get-tuple-element.76), kind=kLoop, calls=%fused_computation.12 | loop fusion | flops 2097152 | bytes 12582912 | tf_op jit(solution)/shard_map/convert_element_type | solution.py:358
  377.8 2.7 bitcast_convert_fusion.2
  381.2 2.5 copy.73
  383.7 2.5 copy.74
  386.7 1.0 copy.91
  (110 shorter events, 9.7 us)
Async XLA Ops:
  0.6 1.4 copy-start
  0.7 6.1 %copy-start.30 = (s32[1,256]{1,0:T(1,128)S(1)}, s32[1,256]{1,0:T(1,128)}, u32[]{:S(2)}) copy-start(s32[1,256]{1,0:T(1,128)} %param.24) | copy-start | bytes 3076
  2.0 5.3 %copy-start.3 = (bf16[256,1024]{1,0:T(8,128)(2,1)S(1)}, bf16[256,1024]{1,0:T(8,128)(2,1)}, u32[]{:S(2)}) copy-start(bf16[256,1024]{1,0:T(8,128)(2,1)} %param.23) | copy-start | bytes 1572868
  2.0 5.3 %copy-start.15 = (bf16[1024,512]{1,0:T(8,128)(2,1)S(1)}, bf16[1024,512]{1,0:T(8,128)(2,1)}, u32[]{:S(2)}) copy-start(bf16[1024,512]{1,0:T(8,128)(2,1)} %param.29) | copy-start | bytes 3145732
  2.0 5.3 %copy-start.25 = (f32[1024]{0:T(1024)S(1)}, f32[1024]{0:T(1024)}, u32[]{:S(2)}) copy-start(f32[1024]{0:T(1024)} %param.27) | copy-start | bytes 12292
  3.8 5.8 %copy-start.14 = (bf16[256,512]{0,1:T(8,128)(2,1)}, bf16[256,512]{0,1:T(8,128)(2,1)S(1)}, u32[]{:S(2)}) copy-start(bf16[256,512]{0,1:T(8,128)(2,1)S(1)} %copy.63) | copy-start | bytes 786436
  3.8 4.2 %copy-start.32 = (s32[1,256]{1,0:T(1,128)S(1)}, s32[1,256]{1,0:T(1,128)}, u32[]{:S(2)}) copy-start(s32[1,256]{1,0:T(1,128)} %param.25) | copy-start | bytes 3076
  7.2 0.9 copy-start.12
  8.0 1.7 copy-start.20
  8.0 1.7 copy-start.22
  9.0 2.0 copy-start.1
  9.6 2.6 copy-start.5
  11.0 4.2 %copy-start.10 = (bf16[8,64,2,256]{3,1,2,0:T(8,128)(2,1)}, bf16[8,64,2,256]{3,1,2,0:T(8,128)(2,1)S(1)}, u32[]{:S(2)}) copy-start(bf16[8,64,2,256]{3,1,2,0:T(8,128)(2,1)S(1)} %fusion.9) | copy-start | bytes 1572868
  11.0 3.0 copy-start.29
  11.0 4.0 %copy-start.26 = (bf16[1024,16]{0,1:T(8,128)(2,1)S(1)}, bf16[1024,16]{0,1:T(8,128)(2,1)}, u32[]{:S(2)}) copy-start(bf16[1024,16]{0,1:T(8,128)(2,1)} %param.33) | copy-start | bytes 98308
  11.0 4.2 %copy-start.27 = (s32[256,8]{0,1:T(8,128)S(1)}, s32[256,8]{0,1:T(8,128)}, u32[]{:S(2)}) copy-start(s32[256,8]{0,1:T(8,128)} %param.26) | copy-start | bytes 24580
  13.1 1.0 copy-start.4
  14.0 1.3 copy-start.31
  14.2 0.8 copy-start.8
  223.4 5.2 %copy-start.6 = (bf16[1024,1024]{1,0:T(8,128)(2,1)S(1)}, bf16[1024,1024]{1,0:T(8,128)(2,1)}, u32[]{:S(2)}) copy-start(bf16[1024,1024]{1,0:T(8,128)(2,1)} %param.31) | copy-start | bytes 6291460
  231.4 3.5 copy-start.2
  234.9 1.0 copy-start.21
  234.9 1.0 copy-start.23
  236.0 1.6 copy-start.7
  236.0 2.3 copy-start.13
  236.7 2.5 copy-start.16
  240.5 2.1 copy-start.11
  244.6 5.3 %copy-start.9 = (bf16[256,1024]{1,0:T(8,128)(2,1)S(1)}, bf16[256,1024]{1,0:T(8,128)(2,1)}, u32[]{:S(2)}) copy-start(bf16[256,1024]{1,0:T(8,128)(2,1)} %copy-done.8) | copy-start | bytes 1572868
  371.0 6.8 %copy-start.18 = (bf16[64,16,512]{2,1,0:T(8,128)(2,1)S(1)}, bf16[64,16,512]{2,1,0:T(8,128)(2,1)}, u32[]{:S(2)}) copy-start(bf16[64,16,512]{2,1,0:T(8,128)(2,1)} %get-tuple-element.77) | copy-start | bytes 3145732
  371.0 6.8 %copy-start.19 = (bf16[64,16,512]{2,1,0:T(8,128)(2,1)S(1)}, bf16[64,16,512]{2,1,0:T(8,128)(2,1)}, u32[]{:S(2)}) copy-start(bf16[64,16,512]{2,1,0:T(8,128)(2,1)} %get-tuple-element.78) | copy-start | bytes 3145732
  377.8 2.8 copy-start.28
  377.8 9.0 %copy-start.17 = (f32[256,1024]{1,0:T(8,128)S(1)}, f32[256,1024]{1,0:T(8,128)}, u32[]{:S(2)}) copy-start(f32[256,1024]{1,0:T(8,128)} %get-tuple-element.82) | copy-start | bytes 3145732
  (1 other events, 0.6 us)

commit v4 on v3

--- a/solution.py
+++ b/solution.py
@@ -358,6 +358,10 @@
     return [o.reshape(a.shape).astype(jnp.float32) for o, a in zip(out, arrays)] + [out[-1]]
 
 
+EDGE_ORDER = (0, 1, 2, 6, 5, 4, 7, 3)
+MIDDLE_ORDER = (0, 1, 2, 3, 7, 5, 6, 4)
+
+
 def contract(left, right, left_dim, right_dim):
     return lax.dot_general(
         left, right, (((left_dim,), (right_dim,)), ((), ())), preferred_element_type=jnp.float32
@@ -388,8 +392,12 @@
     partial,
     from_sibling,
     from_line,
-    staged,
-    returned,
+    staged_x,
+    staged_y,
+    staged_again,
+    returned_x,
+    returned_y,
+    returned_again,
     load_sem,
     gather_send,
     gather_recv,
@@ -449,8 +457,12 @@
     for s in (0, 1):
         own[s].wait()
         gather(s, z, 0, device(near, x, c, y)).start()
-        gather(s, z, 1, device(far, x, c, y)).start()
         gather(s, z, 2, sibling).start()
+
+        @pl.when(middle)
+        def _():
+            gather(s, z, 1, device(far, x, c, y)).start()
+
     gate_copies = [
         remote(
             gates_in.at[a, b], gates.at[z, c], gate_send.at[n], gate_recv.at[z, c], device(a, x, b, y)
@@ -482,9 +494,18 @@
                 sums[e, a, u // 16, pl.ds(pl.multiple_of((u % 16) * 16, 16), 16), :] = jnp.zeros(
                     (16, 1024), jnp.float32
                 )
+            partial[e, u // 8, (u // 4) % 2, pl.ds(pl.multiple_of((u % 4) * 64, 64), 64), :] = jnp.zeros(
+                (64, 1024), jnp.bfloat16
+            )
         return carry
 
     lax.fori_loop(0, 32, zero, 0)
+
+    @pl.when(edge)
+    def _():
+        for s in (0, 1):
+            gather(s, z, 0, device(near, x, c, y)).wait_send()
+            gather(s, z, 1, device(far, x, c, y)).start()
 
     def handle(k):
         block = chip(k)
@@ -505,7 +526,7 @@
     row_id = lax.broadcasted_iota(jnp.int32, (256, 256), 0)
     lane_id = lax.broadcasted_iota(jnp.int32, (256, 256), 1)
 
-    def compute(expert, block, core, first):
+    def compute(expert, block, core):
         diagonal = row_id == lane_id
         gate_row = gates[block, core, pl.ds(expert, 1), :]
         gate = jnp.sum(jnp.where(diagonal, gate_row, 0.0), axis=1, keepdims=True)
@@ -528,9 +549,7 @@
         slopes[block, core, pl.ds(expert, 1), :] = jnp.sum(
             jnp.where(diagonal, slope, 0.0), axis=0, keepdims=True
         )
-        weighted = gate * total
-        if not first:
-            weighted = weighted + partial[1, block, core].astype(jnp.float32)
+        weighted = gate * total + partial[1, block, core].astype(jnp.float32)
         partial[1, block, core] = weighted.astype(jnp.bfloat16)
         upstream = (gate * upstream).astype(jnp.bfloat16)
         back = jnp.zeros((256, 1024), jnp.float32)
@@ -544,54 +563,11 @@
             sums[expert, 2, j] += contract(hidden, upstream, 0, 0)
             step = contract(gate_grad, w_gate[expert, j], 1, 1) + contract(up_grad, w_up[expert, j], 1, 1)
             back = back + step.astype(jnp.bfloat16).astype(jnp.float32)
-        if not first:
-            back = back + partial[0, block, core].astype(jnp.float32)
+        back = back + partial[0, block, core].astype(jnp.float32)
         partial[0, block, core] = back.astype(jnp.bfloat16)
 
-    def first_pass(i, carry):
-        k = i // 2
-        block, core = chip(k), (c + i) % 2
-
-        @pl.when(i == 1)
-        def _():
-            for s in (0, 1):
-                arrive(s, z, 1 - c)
-
-        @pl.when((i == 2) & middle | (i == 4) & edge)
-        def _():
-            handle(2)
-
-        @pl.when((i == 4) & middle | (i == 6) & edge)
-        def _():
-            handle(3)
-
-        @pl.when((i % 2 == 1) & (i > 1))
-        def _():
-            for s in (0, 1):
-                arrive(s, block, 1 - c)
-
-        compute(x, block, core, True)
-        return carry
-
-    lax.fori_loop(0, 8, first_pass, 0)
-
-    def stage_grads(place_at, expert, group):
-        def body(u, carry):
-            at = pl.ds(pl.multiple_of(u * 32, 32), 32)
-            for a in range(3):
-                staged[place_at, a, at, :] = sums[expert, a, group, at, :].astype(jnp.bfloat16)
-            return carry
-
-        lax.fori_loop(0, 8, body, 0)
-
-    def grad_copy(n, a, peer):
-        return remote(staged.at[n, a], returned.at[n, a], grad_send.at[n, a], grad_recv.at[n, a], peer)
-
-    stage_grads(0, x, 1 - y)
-    for a in range(3):
-        grad_copy(0, a, across).start()
-    weights_here(1 - x, y)
-    weights_here(1 - x, 1 - y)
+    def grad_copy(n, source, target, peer):
+        return remote(source, target, grad_send.at[n], grad_recv.at[n], peer)
 
     def pair_copy(s, block):
         return remote(
@@ -602,48 +578,117 @@
             sibling,
         )
 
-    def line_copy(s, block):
+    def line_copy(s, block, slot, peer):
         return remote(
             partial.at[s, block, c],
-            from_line.at[s, z],
+            from_line.at[s, slot],
             line_send.at[s, block],
-            line_recv.at[s, z],
-            device(block, x, c, y),
-        )
-
-    def second_pass(i, carry):
-        block, core = chip(3 - i // 2), (c + 1 + i) % 2
-        compute(1 - x, block, core, False)
-
-        @pl.when(i % 2 == 0)
+            line_recv.at[s, slot],
+            device(peer, x, c, y),
+        )
+
+    def line_wait(s, slot):
+        piece = from_line.at[s, slot]
+        pltpu.make_async_copy(piece, piece, line_recv.at[s, slot]).wait()
+
+    def add_to(s, block, ref):
+        def body(u, carry):
+            at = pl.ds(pl.multiple_of(u * 32, 32), 32)
+            value = partial[s, block, c, at, :].astype(jnp.float32) + ref[at, :].astype(jnp.float32)
+            partial[s, block, c, at, :] = value.astype(jnp.bfloat16)
+            return carry
+
+        lax.fori_loop(0, 8, body, 0)
+
+    at_edge = (z * z - 3 * z + 2) // 2
+    orders = [sum(code << (3 * t) for t, code in enumerate(codes)) for codes in (EDGE_ORDER, MIDDLE_ORDER)]
+    order = at_edge * orders[0] + (1 - at_edge) * orders[1]
+
+    def step(i, carry):
+        t = i // 2
+        code = lax.shift_right_logical(order, 3 * t) % 8
+        again = at_edge * ((t // 3) % 2 + t // 7) + (1 - at_edge) * (t // 4)
+        k = code % 4
+        expert = x + (code // 4) * (1 - 2 * x)
+        block, core = chip(k), (c + i + again) % 2
+
+        @pl.when((i == 2) & middle | (i == 4) & edge)
+        def _():
+            handle(2)
+
+        @pl.when((i == 4) & middle | (i == 12) & edge)
+        def _():
+            handle(3)
+
+        @pl.when((i == 8) & middle | (i == 6) & edge)
+        def _():
+            weights_here(1 - x, y)
+            weights_here(1 - x, 1 - y)
+
+        @pl.when((i % 2 == 1) & (again == 0))
+        def _():
+            for s in (0, 1):
+                arrive(s, block, 1 - c)
+
+        compute(expert, block, core)
+
+        @pl.when((i % 2 == 0) & (again == 1))
         def _():
             for s in (0, 1):
                 pair_copy(s, block).start()
 
-        @pl.when((i % 2 == 1) & (i < 6))
+        @pl.when((i % 2 == 1) & (again == 1) & (k > 0))
         def _():
             for s in (0, 1):
                 pair_copy(s, block).wait_recv()
-
-                def body(u, inner_carry):
-                    at = pl.ds(pl.multiple_of(u * 32, 32), 32)
-                    value = partial[s, block, c, at, :].astype(jnp.float32)
-                    value = value + from_sibling[s, block, at, :].astype(jnp.float32)
-                    partial[s, block, c, at, :] = value.astype(jnp.bfloat16)
-                    return inner_carry
-
-                lax.fori_loop(0, 8, body, 0)
-                line_copy(s, block).start()
+                add_to(s, block, from_sibling.at[s, block])
+
+                @pl.when(edge & (k == 2))
+                def _():
+                    line_copy(s, block, 3, near).start()
+
+                @pl.when(edge & (k == 1))
+                def _():
+                    line_copy(s, block, 1, near).start()
+
+                @pl.when(edge & (k == 3))
+                def _():
+                    line_copy(s, block, 2, last).start()
+
+                @pl.when(middle & (k == 3))
+                def _():
+                    line_copy(s, block, 1, last).start()
+
+                @pl.when(middle & (k == 2))
+                def _():
+                    line_copy(s, block, 0, far).start()
 
         return carry
 
-    lax.fori_loop(0, 8, second_pass, 0)
-    stage_grads(1, 1 - x, y)
-    for a in range(3):
-        grad_copy(1, a, beside).start()
-    stage_grads(2, 1 - x, 1 - y)
-    for a in range(3):
-        grad_copy(2, a, corner).start()
+    lax.fori_loop(0, 16, step, 0)
+    low, high = pl.ds(0, 512), pl.ds(512, 512)
+
+    def each(body):
+        def rows_of(u, carry):
+            at = pl.ds(pl.multiple_of(u * 32, 32), 32)
+            for a in range(3):
+                body(a, at)
+            return carry
+
+        lax.fori_loop(0, 8, rows_of, 0)
+
+    def stage_low(a, at):
+        for j in (0, 1):
+            staged_x[j, a, at, :] = sums[1 - x, a, j, at, low].astype(jnp.bfloat16)
+
+    def stage_high(a, at):
+        staged_y[0, a, at, :] = sums[1 - x, a, 1 - y, at, high].astype(jnp.bfloat16)
+        staged_y[1, a, at, :] = sums[x, a, 1 - y, at, high].astype(jnp.bfloat16)
+
+    each(stage_low)
+    grad_copy(0, staged_x, returned_x, beside).start()
+    each(stage_high)
+    grad_copy(1, staged_y, returned_y, across).start()
     slope_copies = [
         remote(
             slopes.at[a, b], slopes_in.at[z, c], slope_send.at[n], slope_recv.at[z, c], device(a, x, b, y)
@@ -653,48 +698,88 @@
     for copy in slope_copies:
         copy.start()
     slopes_in[z, c] = slopes[z, c]
+
+    @pl.when(middle)
+    def _():
+        for s in (0, 1):
+            line_wait(s, 3)
+            add_to(s, near, from_line.at[s, 3])
+            line_copy(s, near, 0, near).start()
+
+    grad_copy(0, staged_x, returned_x, beside).wait_recv()
+
+    def second_low(a, at):
+        value = sums[x, a, 1 - y, at, low] + returned_x[1 - y, a, at, :].astype(jnp.float32)
+        staged_again[0, a, at, :] = value.astype(jnp.bfloat16)
+
+    each(second_low)
+    grad_copy(2, staged_again.at[0], returned_again.at[0], across).start()
+    grad_copy(1, staged_y, returned_y, across).wait_recv()
+
+    def second_high(a, at):
+        value = sums[1 - x, a, y, at, high] + returned_y[0, a, at, :].astype(jnp.float32)
+        staged_again[1, a, at, :] = value.astype(jnp.bfloat16)
+
+    each(second_high)
+    grad_copy(3, staged_again.at[1], returned_again.at[1], beside).start()
+
+    def finish(slots):
+        for s in (0, 1):
+            for slot in slots:
+                line_wait(s, slot)
+
+            def body(u, carry):
+                at = pl.ds(pl.multiple_of(u * 32, 32), 32)
+                value = partial[s, z, c, at, :].astype(jnp.float32)
+                value = value + from_sibling[s, z, at, :].astype(jnp.float32)
+                for slot in slots:
+                    value = value + from_line[s, slot, at, :].astype(jnp.float32)
+                (back_out, weighted_out)[s][at, :] = value
+                return carry
+
+            lax.fori_loop(0, 8, body, 0)
+
     for s in (0, 1):
         pair_copy(s, z).wait_recv()
-        for k in (1, 2, 3):
-            source = chip(k)
-            pltpu.make_async_copy(from_line.at[s, source], from_line.at[s, source], line_recv.at[s, source]).wait()
-
-        def body(u, carry):
-            at = pl.ds(pl.multiple_of(u * 32, 32), 32)
-            value = partial[s, z, c, at, :].astype(jnp.float32)
-            value = value + from_sibling[s, z, at, :].astype(jnp.float32)
-            for k in (1, 2, 3):
-                value = value + from_line[s, chip(k), at, :].astype(jnp.float32)
-            (back_out, weighted_out)[s][at, :] = value
-            return carry
-
-        lax.fori_loop(0, 8, body, 0)
+
+    @pl.when(middle)
+    def _():
+        finish((0, 1))
+
+    @pl.when(edge)
+    def _():
+        finish((0, 1, 2))
+
     for a, b in line:
         pltpu.make_async_copy(slopes_in.at[a, b], slopes_in.at[a, b], slope_recv.at[a, b]).wait()
     slope_out[...] = slopes_in[...]
-    stores = []
-    for a, out in enumerate((gate_out, up_out, down_out)):
-        for n, peer in enumerate((across, beside, corner)):
-            grad_copy(n, a, peer).wait_recv()
-
-        def body(u, carry):
-            at = pl.ds(pl.multiple_of(u * 32, 32), 32)
-            value = sums[x, a, y, at, :]
-            for n in range(3):
-                value = value + returned[n, a, at, :].astype(jnp.float32)
-            sums[x, a, y, at, :] = value
-            return carry
-
-        lax.fori_loop(0, 8, body, 0)
-        stores.append(pltpu.make_async_copy(sums.at[x, a, y], out, load_sem.at[a]))
-        stores[a].start()
+    grad_copy(2, staged_again.at[0], returned_again.at[0], across).wait_recv()
+    grad_copy(3, staged_again.at[1], returned_again.at[1], beside).wait_recv()
+
+    def final_grad(a, at):
+        value = sums[x, a, y, at, low] + returned_x[y, a, at, :].astype(jnp.float32)
+        sums[x, a, y, at, low] = value + returned_again[0, a, at, :].astype(jnp.float32)
+        value = sums[x, a, y, at, high] + returned_y[1, a, at, :].astype(jnp.float32)
+        sums[x, a, y, at, high] = value + returned_again[1, a, at, :].astype(jnp.float32)
+
+    each(final_grad)
+    stores = [
+        pltpu.make_async_copy(sums.at[x, a, y], out, load_sem.at[a])
+        for a, out in enumerate((gate_out, up_out, down_out))
+    ]
+    for copy in stores:
+        copy.start()
     for s in (0, 1):
-        gather(s, z, 0, device(near, x, c, y)).wait_send()
+
+        @pl.when(middle)
+        def _():
+            gather(s, z, 0, device(near, x, c, y)).wait_send()
+
         gather(s, z, 1, device(far, x, c, y)).wait_send()
         gather(s, z, 2, sibling).wait_send()
         for k in (1, 2, 3):
             gather(s, chip(k), 4 + k, sibling).wait_send()
-            line_copy(s, chip(k)).wait_send()
+            line_copy(s, chip(k), 0, near).wait_send()
 
         @pl.when(middle)
         def _():
@@ -705,9 +790,10 @@
             pair_copy(s, chip(k)).wait_send()
     for copy in (*gate_copies, *weight_copies, *slope_copies):
         copy.wait_send()
-    for n, peer in enumerate((across, beside, corner)):
-        for a in range(3):
-            grad_copy(n, a, peer).wait_send()
+    grad_copy(0, staged_x, returned_x, beside).wait_send()
+    grad_copy(1, staged_y, returned_y, across).wait_send()
+    grad_copy(2, staged_again.at[0], returned_again.at[0], across).wait_send()
+    grad_copy(3, staged_again.at[1], returned_again.at[1], beside).wait_send()
     for copy in stores:
         copy.wait()
 
@@ -744,8 +830,7 @@
             pltpu.VMEM((2, 4, 2, tokens, model_dim), bf16),
             pltpu.VMEM((2, 4, tokens, model_dim), bf16),
             pltpu.VMEM((2, 4, tokens, model_dim), bf16),
-            pltpu.VMEM((3, 3, width, model_dim), bf16),
-            pltpu.VMEM((3, 3, width, model_dim), bf16),
+            *[pltpu.VMEM((2, 3, width, model_dim // 2), bf16)] * 6,
             dma((6,)),
             dma((2, 8)),
             dma((2, 4, 2)),
@@ -759,8 +844,8 @@
             dma((2, 4)),
             dma((2, 4)),
             dma((2, 4)),
-            dma((3, 3)),
-            dma((3, 3)),
+            dma((4,)),
+            dma((4,)),
         ],
         compiler_params=pltpu.CompilerParams(
             collective_id=1, has_side_effects=True, vmem_limit_bytes=62 << 20

time: 389 us -> 335 us (0.86)
  Pallas kernels: 324 us -> 270 us
    pallas_call x1, Pallas kernels: 118 us -> 78.8 us  [sum_everywhere(): pl.pallas_call(functools.partial(sum_kernel, count), out_shape=[jax.Shape...]
    pallas_call x1, Pallas kernels: 206 us -> 191 us  [expert_part(): pl.pallas_call(expert_kernel, out_shape=[jax.ShapeDtypeStruct((tokens, mo...]
where the time goes in v4:
time: 335 us; the launch traced here: 333 us
  Pallas kernels  270 us (81%)
  matrix products  26.5 us (8%)
  other arithmetic  18.8 us (6%)
  local copies, waits for them, and re-layouts  16.9 us (5%)
    pallas_call x1, Pallas kernels, expert_part(): pl.pallas_call(expert_kernel, out_shape=[jax.ShapeDtypeStruct((tokens, mo...  191 us
    pallas_call x1, Pallas kernels, sum_everywhere(): pl.pallas_call(functools.partial(sum_kernel, count), out_shape=[jax.Shape...  78.8 us
    unnamed x69, local copies, waits for them, and re-layouts  11.3 us
    convert_element_type x2, other arithmetic, sum_everywhere(): o.reshape(a.shape).astype(jnp.float32)  9.55 us

profile of v4, /device:TPU:0, one launch (start us, length us, event | category | flops | bytes accessed | tf_op | source)
XLA Modules:
  0.0 333.0 jit_solution(10704422665076066838)
XLA Ops:
  0.7 1.3 fusion.25
  2.0 1.6 convolution_convert_fusion.5
  3.8 2.9 fusion.45
  8.2 0.8 fusion.51
  9.6 0.9 fusion.9
  11.0 1.2 copy-done.5
  12.2 0.8 multiply_reduce_fusion.2
  13.1 1.0 copy-done.4
  14.2 0.8 copy-done.8
  16.1 190.7 %expert_part.1 = (f32[256,1024]{1,0:T(8,128)}, f32[256,1024]{1,0:T(8,128)}, f32[4,2,8,256]{3,2,1,0:T(8,128)}, f32[256,1024]{1,0:T(8,128)}, f32[256,1024]{1,0:T(8,128)}, /*index=5*/f32[256,1024]{1,0:T(8,128)}) custom-call(bf16[256,1024]{1,0:T(8,128)(2,1)} %copy-done.8, bf16[256,1024]{1,0:T(8,128)(2,1)} %upstream_in.1, f32[4,2,8,256]{3,2,1,0:T(8,128)} %pad.14.gates_in, ...), custom_call_target="tpu_custom_call" | custom-call | tf_op jit(solution)/shard_map/expert_part/pallas_call | solution.py:809
  206.8 0.8 slice_bitcast_fusion.1
  207.9 2.2 multiply_reduce_fusion
  210.2 2.9 multiply_add_fusion
  213.1 1.6 convolution_convert_fusion.4
  214.7 1.2 copy.69
  215.9 3.4 %fusion = (f32[8,2,256]{2,1,0:T(2,128)S(1)}, f32[8,256,256,2]{2,1,3,0:T(8,128)S(1)}) fusion(f32[8,2,256,256]{2,3,1,0:T(8,128)} %copy-done.1, f32[8,2,256]{2,1,0:T(2,128)S(1)} %bitcast.158, bf16[256,8,64,1]{0,2,3,1:T(8,128)(2,1)} %bitcast.150, bf16[256,8,2,64]{0,3,2,1:T(8,128)(2,1)S(1)} %bitcast.131), kind=kOutput, calls=%fused_computation.2 | convolution fusion | flops 137359360 | bytes 9207808 | tf_op jit(solution)/shard_map/qgrd,kgd->grqk/dot_general | solution.py:992
  219.5 1.0 fusion.2
  221.2 0.9 copy-done.7
  222.9 0.8 fusion.13
  224.2 0.8 fusion.17
  225.8 1.3 fusion.24
  227.1 2.0 convolution_convert_fusion.1
  229.1 2.2 convolution_convert_fusion
  231.3 1.6 convolution_convert_fusion.3
  232.9 1.6 convolution_convert_fusion.2
  236.0 78.8 %sum_everywhere.1 = (bf16[64,16,1024]{2,1,0:T(8,128)(2,1)}, bf16[64,16,1024]{2,1,0:T(8,128)(2,1)}, bf16[64,16,512]{2,1,0:T(8,128)(2,1)}, bf16[64,16,512]{2,1,0:T(8,128)(2,1)}, f32[24,1024]{1,0:T(8,128)}) custom-call(bf16[64,16,1024]{2,1,0:T(8,128)(2,1)} %bitcast.129, bf16[64,16,1024]{2,1,0:T(8,128)(2,1)} %bitcast.130, bf16[64,16,512]{2,1,0:T(8,128)(2,1)} %bitcast.135, ...), custom_call_target="tpu_custom_call" | custom-call | tf_op jit(solution)/shard_map/sum_everywhere/pallas_call | solution.py:332
  314.8 1.4 fusion.50
  316.2 6.8 %bitcast_convert_fusion = (f32[1024,1024]{1,0:T(8,128)}, f32[1024,1024]{1,0:T(8,128)}) fusion(bf16[64,16,1024]{2,1,0:T(8,128)(2,1)} %get-tuple-element.79, bf16[64,16,1024]{2,1,0:T(8,128)(2,1)} %get-tuple-element.76), kind=kLoop, calls=%fused_computation.12 | loop fusion | flops 2097152 | bytes 12582912 | tf_op jit(solution)/shard_map/convert_element_type | solution.py:358
  323.1 2.7 bitcast_convert_fusion.2
  326.5 2.5 copy.73
  329.0 2.5 copy.74
  332.0 1.0 copy.91
  (110 shorter events, 9.6 us)
Async XLA Ops:
  0.6 1.4 copy-start
  0.7 6.1 %copy-start.30 = (s32[1,256]{1,0:T(1,128)S(1)}, s32[1,256]{1,0:T(1,128)}, u32[]{:S(2)}) copy-start(s32[1,256]{1,0:T(1,128)} %param.24) | copy-start | bytes 3076
  2.0 5.3 %copy-start.3 = (bf16[256,1024]{1,0:T(8,128)(2,1)S(1)}, bf16[256,1024]{1,0:T(8,128)(2,1)}, u32[]{:S(2)}) copy-start(bf16[256,1024]{1,0:T(8,128)(2,1)} %param.23) | copy-start | bytes 1572868
  2.0 5.3 %copy-start.15 = (bf16[1024,512]{1,0:T(8,128)(2,1)S(1)}, bf16[1024,512]{1,0:T(8,128)(2,1)}, u32[]{:S(2)}) copy-start(bf16[1024,512]{1,0:T(8,128)(2,1)} %param.29) | copy-start | bytes 3145732
  2.0 5.3 %copy-start.25 = (f32[1024]{0:T(1024)S(1)}, f32[1024]{0:T(1024)}, u32[]{:S(2)}) copy-start(f32[1024]{0:T(1024)} %param.27) | copy-start | bytes 12292
  3.8 5.8 %copy-start.14 = (bf16[256,512]{0,1:T(8,128)(2,1)}, bf16[256,512]{0,1:T(8,128)(2,1)S(1)}, u32[]{:S(2)}) copy-start(bf16[256,512]{0,1:T(8,128)(2,1)S(1)} %copy.63) | copy-start | bytes 786436
  3.8 4.2 %copy-start.32 = (s32[1,256]{1,0:T(1,128)S(1)}, s32[1,256]{1,0:T(1,128)}, u32[]{:S(2)}) copy-start(s32[1,256]{1,0:T(1,128)} %param.25) | copy-start | bytes 3076
  7.2 0.9 copy-start.12
  8.0 1.7 copy-start.20
  8.0 1.7 copy-start.22
  9.0 2.0 copy-start.1
  9.6 2.6 copy-start.5
  11.0 4.2 %copy-start.10 = (bf16[8,64,2,256]{3,1,2,0:T(8,128)(2,1)}, bf16[8,64,2,256]{3,1,2,0:T(8,128)(2,1)S(1)}, u32[]{:S(2)}) copy-start(bf16[8,64,2,256]{3,1,2,0:T(8,128)(2,1)S(1)} %fusion.9) | copy-start | bytes 1572868
  11.0 3.0 copy-start.29
  11.0 4.0 %copy-start.26 = (bf16[1024,16]{0,1:T(8,128)(2,1)S(1)}, bf16[1024,16]{0,1:T(8,128)(2,1)}, u32[]{:S(2)}) copy-start(bf16[1024,16]{0,1:T(8,128)(2,1)} %param.33) | copy-start | bytes 98308
  11.0 4.2 %copy-start.27 = (s32[256,8]{0,1:T(8,128)S(1)}, s32[256,8]{0,1:T(8,128)}, u32[]{:S(2)}) copy-start(s32[256,8]{0,1:T(8,128)} %param.26) | copy-start | bytes 24580
  13.1 1.0 copy-start.4
  14.0 1.3 copy-start.31
  14.2 0.8 copy-start.8
  207.9 5.2 %copy-start.6 = (bf16[1024,1024]{1,0:T(8,128)(2,1)S(1)}, bf16[1024,1024]{1,0:T(8,128)(2,1)}, u32[]{:S(2)}) copy-start(bf16[1024,1024]{1,0:T(8,128)(2,1)} %param.31) | copy-start | bytes 6291460
  215.9 3.5 %copy-start.2 = (f32[8,2,256,256]{2,3,1,0:T(8,128)S(1)}, f32[8,2,256,256]{2,3,1,0:T(8,128)}, u32[]{:S(2)}) copy-start(f32[8,2,256,256]{2,3,1,0:T(8,128)} %copy-done.1) | copy-start | bytes 12582916
  219.5 1.0 copy-start.21
  219.5 1.0 copy-start.23
  220.5 1.6 copy-start.7
  220.5 2.3 copy-start.13
  221.2 2.5 copy-start.16
  225.0 2.1 copy-start.11
  229.1 5.3 %copy-start.9 = (bf16[256,1024]{1,0:T(8,128)(2,1)S(1)}, bf16[256,1024]{1,0:T(8,128)(2,1)}, u32[]{:S(2)}) copy-start(bf16[256,1024]{1,0:T(8,128)(2,1)} %copy-done.8) | copy-start | bytes 1572868
  316.2 6.8 %copy-start.18 = (bf16[64,16,512]{2,1,0:T(8,128)(2,1)S(1)}, bf16[64,16,512]{2,1,0:T(8,128)(2,1)}, u32[]{:S(2)}) copy-start(bf16[64,16,512]{2,1,0:T(8,128)(2,1)} %get-tuple-element.77) | copy-start | bytes 3145732
  316.2 6.8 %copy-start.19 = (bf16[64,16,512]{2,1,0:T(8,128)(2,1)S(1)}, bf16[64,16,512]{2,1,0:T(8,128)(2,1)}, u32[]{:S(2)}) copy-start(bf16[64,16,512]{2,1,0:T(8,128)(2,1)} %get-tuple-element.78) | copy-start | bytes 3145732
  323.1 2.8 copy-start.28
  323.1 9.0 %copy-start.17 = (f32[256,1024]{1,0:T(8,128)S(1)}, f32[256,1024]{1,0:T(8,128)}, u32[]{:S(2)}) copy-start(f32[256,1024]{1,0:T(8,128)} %get-tuple-element.82) | copy-start | bytes 3145732
  (1 other events, 0.6 us)

commit v5 on v4

v5 whole, which is shorter than its diff:
```python
import functools

import jax
import jax.numpy as jnp
from jax import lax
from jax.experimental import pallas as pl
from jax.experimental.pallas import tpu as pltpu
from jax.sharding import PartitionSpec as P

QUERY_HEADS = 16
KEY_VALUE_HEADS = 8
HEAD_SIZE = 64
TOP = 8


EPSILON = 1e-05


def rms_forward(value_rows, norm_gain):
    inverse = lax.rsqrt(jnp.mean(value_rows * value_rows, axis=-1, keepdims=True) + EPSILON)
    return (value_rows * inverse * norm_gain, inverse)


def rms_backward(value_rows, inverse, norm_gain, upstream):
    scaled = upstream * norm_gain
    gain_grad = jnp.sum(upstream * value_rows * inverse, axis=0)
    input_grad = inverse * (
        scaled
        - value_rows * inverse * inverse * jnp.mean(scaled * value_rows, axis=-1, keepdims=True)
    )
    return (input_grad, gain_grad)


def positions_of(segment):
    before = (segment[None, :] < segment[:, None]).astype(jnp.int32)
    return jnp.arange(segment.shape[-1], dtype=jnp.int32) - jnp.sum(before, axis=1)


def rotary_tables(positions, head_dim):
    half_dim = head_dim // 2
    frequency = 10000.0 ** (-(jnp.arange(half_dim, dtype=jnp.float32) * 2.0) / head_dim)
    angles = positions.astype(jnp.float32)[:, None] * frequency[None, :]
    return (jnp.cos(angles)[:, None, :], jnp.sin(angles)[:, None, :])


def rotary(heads, cosine_table, sine_table):
    half_dim = heads.shape[-1] // 2
    first_half = heads[..., :half_dim]
    second_half = heads[..., half_dim:]
    return jnp.concatenate(
        [
            first_half * cosine_table - second_half * sine_table,
            second_half * cosine_table + first_half * sine_table,
        ],
        axis=-1,
    )


def rotary_backward(grads, cosine_table, sine_table):
    half_dim = grads.shape[-1] // 2
    first_half = grads[..., :half_dim]
    second_half = grads[..., half_dim:]
    return jnp.concatenate(
        [
            first_half * cosine_table + second_half * sine_table,
            second_half * cosine_table - first_half * sine_table,
        ],
        axis=-1,
    )


def to_bf16(value):
    return lax.reduce_precision(value, 8, 7)


def expert_pass(rows, upstream, gates, gate_w, up_w, down_w):
    groups, model_dim, width = gate_w.shape
    gate_all = jnp.concatenate([gate_w[j] for j in range(groups)], axis=1)
    up_all = jnp.concatenate([up_w[j] for j in range(groups)], axis=1)
    down_all = down_w.reshape(groups * width, model_dim)
    gate_pre = jnp.dot(rows, gate_all, preferred_element_type=jnp.float32)
    up_pre = jnp.dot(rows, up_all, preferred_element_type=jnp.float32)
    sigmoid_part = jax.nn.sigmoid(gate_pre)
    activated = gate_pre * sigmoid_part
    hidden = (activated * up_pre).astype(jnp.bfloat16)
    total = jnp.zeros(rows.shape, jnp.float32)
    for j in range(groups):
        total = total + to_bf16(
            jnp.dot(hidden[:, j * width : (j + 1) * width], down_w[j], preferred_element_type=jnp.float32)
        )
    total = to_bf16(total)
    upstream_f = upstream.astype(jnp.float32)
    gate_upstream = jnp.sum(upstream_f * total, axis=-1)
    weighted = (gates[:, None] * total).astype(jnp.bfloat16)
    upstream_e = (gates[:, None] * upstream_f).astype(jnp.bfloat16)
    hidden_grad = jnp.einsum("td,fd->tf", upstream_e, down_all, preferred_element_type=jnp.float32)
    up_pre_grad = (hidden_grad * activated).astype(jnp.bfloat16)
    gate_pre_grad = (
        hidden_grad * up_pre * sigmoid_part * (1.0 + gate_pre * (1.0 - sigmoid_part))
    ).astype(jnp.bfloat16)
    down_grad = jnp.einsum("tf,td->fd", hidden, upstream_e, preferred_element_type=jnp.float32)
    gate_grad = jnp.einsum("td,tf->df", rows, gate_pre_grad, preferred_element_type=jnp.float32)
    up_grad = jnp.einsum("td,tf->df", rows, up_pre_grad, preferred_element_type=jnp.float32)
    back = jnp.zeros(rows.shape, jnp.float32)
    for j in range(groups):
        cut = slice(j * width, (j + 1) * width)
        back = back + to_bf16(
            jnp.einsum("tf,df->td", gate_pre_grad[:, cut], gate_w[j], preferred_element_type=jnp.float32)
            + jnp.einsum("tf,df->td", up_pre_grad[:, cut], up_w[j], preferred_element_type=jnp.float32)
        )
    return (weighted, back.astype(jnp.bfloat16), gate_upstream, gate_grad, up_grad, down_grad)


def sum_halves(grad, dim):
    return lax.psum_scatter(
        grad.astype(jnp.bfloat16), "hs", scatter_dimension=dim, tiled=True
    ).astype(jnp.float32)


MESH = pl.DeviceIdType.MESH
UNIT = 16


def place():
    ep, hs = lax.axis_index("ep"), lax.axis_index("hs")
    return (ep // 4, (ep // 2) % 2, ep % 2, hs)


def device(z, x, c, y):
    return (z * 4 + x * 2 + c, y)


def greet(peers):
    barrier = pltpu.get_barrier_semaphore()
    for peer in peers:
        pl.semaphore_signal(barrier, inc=1, device_id=peer, device_id_type=MESH)
    pl.semaphore_wait(barrier, len(peers))


EDGE_ORDER = (0, 1, 2, 6, 5, 4, 7, 3)
MIDDLE_ORDER = (0, 1, 2, 3, 7, 5, 6, 4)


def contract(left, right, left_dim, right_dim):
    return lax.dot_general(
        left, right, (((left_dim,), (right_dim,)), ((), ())), preferred_element_type=jnp.float32
    )


def expert_kernel(
    rows_in,
    upstream_in,
    gates_in,
    gate_w,
    up_w,
    down_w,
    weighted_out,
    back_out,
    slope_out,
    own_out,
    again_out,
    streams,
    gates,
    slopes,
    slopes_in,
    w_gate,
    w_up,
    w_down,
    sums,
    partial,
    from_sibling,
    from_line,
    staged_x,
    staged_y,
    staged_again,
    returned_x,
    returned_y,
    load_sem,
    gather_send,
    gather_recv,
    gate_send,
    gate_recv,
    slope_send,
    slope_recv,
    weight_send,
    weight_recv,
    pair_send,
    pair_recv,
    line_send,
    line_recv,
    grad_send,
    grad_recv,
):
    z, x, c, y = place()
    near, far, last = 1 + z % 2, (2 + 3 * z) % 5, 3 - 3 * (z // 2)
    middle = (z == 1) | (z == 2)
    edge = (z == 0) | (z == 3)
    sibling, beside, across = device(z, x, 1 - c, y), device(z, 1 - x, c, y), device(z, x, c, 1 - y)
    corner = device(z, 1 - x, c, 1 - y)
    line = [((z + k) % 4, (c + d) % 2) for k in range(4) for d in range(2) if k or d]
    greet([device(a, x, b, y) for a, b in line] + [beside, across, corner])

    def chip(k):
        half = z // 2
        inner = z + half * (3 - 2 * z)
        spot = k + inner * (1 - 3 * (k // 2) + 2 * (k // 3))
        return spot + half * (3 - 2 * spot)

    def remote(source, target, send, recv, peer):
        return pltpu.make_async_remote_copy(
            src_ref=source, dst_ref=target, send_sem=send, recv_sem=recv, device_id=peer, device_id_type=MESH
        )

    own = [
        pltpu.make_async_copy(ref, streams.at[s, z, c], load_sem.at[s])
        for s, ref in enumerate((rows_in, upstream_in))
    ]
    gates_own = pltpu.make_async_copy(gates_in.at[z, c], gates.at[z, c], load_sem.at[2])
    weights_own = [
        pltpu.make_async_copy(ref, held.at[x, y], load_sem.at[3 + a])
        for a, (ref, held) in enumerate(((gate_w, w_gate), (up_w, w_up), (down_w, w_down)))
    ]
    for copy in (*own, gates_own, *weights_own):
        copy.start()

    def gather(s, block, slot, peer):
        piece = streams.at[s, block, c]
        return remote(piece, piece, gather_send.at[s, slot], gather_recv.at[s, block, c], peer)

    def arrive(s, block, core):
        piece = streams.at[s, block, core]
        pltpu.make_async_copy(piece, piece, gather_recv.at[s, block, core]).wait()

    for s in (0, 1):
        own[s].wait()
        gather(s, z, 0, device(near, x, c, y)).start()
        gather(s, z, 2, sibling).start()

        @pl.when(middle)
        def _():
            gather(s, z, 1, device(far, x, c, y)).start()

    gate_copies = [
        remote(
            gates_in.at[a, b], gates.at[z, c], gate_send.at[n], gate_recv.at[z, c], device(a, x, b, y)
        )
        for n, (a, b) in enumerate(line)
    ]
    for copy in gate_copies:
        copy.start()
    weight_copies = []
    for a, held in enumerate((w_gate, w_up, w_down)):
        weights_own[a].wait()
        for n, peer in enumerate((across, beside, corner)):
            piece = held.at[x, y]
            weight_copies.append(
                remote(piece, piece, weight_send.at[n, a], weight_recv.at[x, y, a], peer)
            )
    for n in range(3):
        for a in range(3):
            weight_copies[a * 3 + n].start()

    def weights_here(expert, group):
        for a, held in enumerate((w_gate, w_up, w_down)):
            piece = held.at[expert, group]
            pltpu.make_async_copy(piece, piece, weight_recv.at[expert, group, a]).wait()

    def zero(u, carry):
        for e in (0, 1):
            for a in range(3):
                sums[e, a, u // 16, pl.ds(pl.multiple_of((u % 16) * 16, 16), 16), :] = jnp.zeros(
                    (16, 1024), jnp.float32
                )
            partial[e, u // 8, (u // 4) % 2, pl.ds(pl.multiple_of((u % 4) * 64, 64), 64), :] = jnp.zeros(
                (64, 1024), jnp.bfloat16
            )
        return carry

    lax.fori_loop(0, 32, zero, 0)

    @pl.when(edge)
    def _():
        for s in (0, 1):
            gather(s, z, 0, device(near, x, c, y)).wait_send()
            gather(s, z, 1, device(far, x, c, y)).start()

    def handle(k):
        block = chip(k)
        for s in (0, 1):
            arrive(s, block, c)
            gather(s, block, 4 + k, sibling).start()
            if k != 2:

                @pl.when(middle)
                def _():
                    gather(s, block, 2 + (k + 1) // 2, device(far, x, c, y)).start()

    handle(1)
    gates_own.wait()
    for a, b in line:
        pltpu.make_async_copy(gates.at[a, b], gates.at[a, b], gate_recv.at[a, b]).wait()
    weights_here(x, 1 - y)
    row_id = lax.broadcasted_iota(jnp.int32, (256, 256), 0)
    lane_id = lax.broadcasted_iota(jnp.int32, (256, 256), 1)

    def compute(expert, block, core):
        diagonal = row_id == lane_id
        gate_row = gates[block, core, pl.ds(expert, 1), :]
        gate = jnp.sum(jnp.where(diagonal, gate_row, 0.0), axis=1, keepdims=True)
        rows = streams[0, block, core]
        total = jnp.zeros((256, 1024), jnp.float32)
        kept = []
        for j in (0, 1):
            gate_pre = contract(rows, w_gate[expert, j], 1, 0)
            up_pre = contract(rows, w_up[expert, j], 1, 0)
            sigmoid_part = jax.nn.sigmoid(gate_pre)
            activated = gate_pre * sigmoid_part
            hidden = (activated * up_pre).astype(jnp.bfloat16)
            part = contract(hidden, w_down[expert, j], 1, 0)
            total = total + part.astype(jnp.bfloat16).astype(jnp.float32)
            inner = up_pre * sigmoid_part * (1.0 + gate_pre * (1.0 - sigmoid_part))
            kept.append((activated, inner, hidden))
        total = total.astype(jnp.bfloat16).astype(jnp.float32)
        upstream = streams[1, block, core].astype(jnp.float32)
        slope = jnp.sum(upstream * total, axis=1, keepdims=True)
        slopes[block, core, pl.ds(expert, 1), :] = jnp.sum(
            jnp.where(diagonal, slope, 0.0), axis=0, keepdims=True
        )
        weighted = gate * total + partial[1, block, core].astype(jnp.float32)
        partial[1, block, core] = weighted.astype(jnp.bfloat16)
        upstream = (gate * upstream).astype(jnp.bfloat16)
        back = jnp.zeros((256, 1024), jnp.float32)
        for j in (0, 1):
            activated, inner, hidden = kept[j]
            hidden_grad = contract(upstream, w_down[expert, j], 1, 1)
            up_grad = (hidden_grad * activated).astype(jnp.bfloat16)
            gate_grad = (hidden_grad * inner).astype(jnp.bfloat16)
            sums[expert, 0, j] += contract(gate_grad, rows, 0, 0)
            sums[expert, 1, j] += contract(up_grad, rows, 0, 0)
            sums[expert, 2, j] += contract(hidden, upstream, 0, 0)
            step = contract(gate_grad, w_gate[expert, j], 1, 1) + contract(up_grad, w_up[expert, j], 1, 1)
            back = back + step.astype(jnp.bfloat16).astype(jnp.float32)
        back = back + partial[0, block, core].astype(jnp.float32)
        partial[0, block, core] = back.astype(jnp.bfloat16)

    def grad_copy(n, source, target, peer):
        return remote(source, target, grad_send.at[n], grad_recv.at[n], peer)

    def pair_copy(s, block):
        return remote(
            partial.at[s, block, 1 - c],
            from_sibling.at[s, block],
            pair_send.at[s, block],
            pair_recv.at[s, block],
            sibling,
        )

    def line_copy(s, block, slot, peer):
        return remote(
            partial.at[s, block, c],
            from_line.at[s, slot],
            line_send.at[s, block],
            line_recv.at[s, slot],
            device(peer, x, c, y),
        )

    def line_wait(s, slot):
        piece = from_line.at[s, slot]
        pltpu.make_async_copy(piece, piece, line_recv.at[s, slot]).wait()

    def add_to(s, block, ref):
        def body(u, carry):
            at = pl.ds(pl.multiple_of(u * 32, 32), 32)
            value = partial[s, block, c, at, :].astype(jnp.float32) + ref[at, :].astype(jnp.float32)
            partial[s, block, c, at, :] = value.astype(jnp.bfloat16)
            return carry

        lax.fori_loop(0, 8, body, 0)

    at_edge = (z * z - 3 * z + 2) // 2
    orders = [sum(code << (3 * t) for t, code in enumerate(codes)) for codes in (EDGE_ORDER, MIDDLE_ORDER)]
    order = at_edge * orders[0] + (1 - at_edge) * orders[1]

    def step(i, carry):
        t = i // 2
        code = lax.shift_right_logical(order, 3 * t) % 8
        again = at_edge * ((t // 3) % 2 + t // 7) + (1 - at_edge) * (t // 4)
        k = code % 4
        expert = x + (code // 4) * (1 - 2 * x)
        block, core = chip(k), (c + i + again) % 2

        @pl.when((i == 2) & middle | (i == 4) & edge)
        def _():
            handle(2)

        @pl.when((i == 4) & middle | (i == 12) & edge)
        def _():
            handle(3)

        @pl.when((i == 8) & middle | (i == 6) & edge)
        def _():
            weights_here(1 - x, y)
            weights_here(1 - x, 1 - y)

        @pl.when((i % 2 == 1) & (again == 0))
        def _():
            for s in (0, 1):
                arrive(s, block, 1 - c)

        compute(expert, block, core)

        @pl.when((i % 2 == 0) & (again == 1))
        def _():
            for s in (0, 1):
                pair_copy(s, block).start()

        @pl.when((i % 2 == 1) & (again == 1) & (k > 0))
        def _():
            for s in (0, 1):
                pair_copy(s, block).wait_recv()
                add_to(s, block, from_sibling.at[s, block])

                @pl.when(edge & (k == 2))
                def _():
                    line_copy(s, block, 3, near).start()

                @pl.when(edge & (k == 1))
                def _():
                    line_copy(s, block, 1, near).start()

                @pl.when(edge & (k == 3))
                def _():
                    line_copy(s, block, 2, last).start()

                @pl.when(middle & (k == 3))
                def _():
                    line_copy(s, block, 1, last).start()

                @pl.when(middle & (k == 2))
                def _():
                    line_copy(s, block, 0, far).start()

        return carry

    lax.fori_loop(0, 16, step, 0)
    low, high = pl.ds(0, 512), pl.ds(512, 512)

    def each(body):
        def rows_of(u, carry):
            at = pl.ds(pl.multiple_of(u * 32, 32), 32)
            for a in range(3):
                body(a, at)
            return carry

        lax.fori_loop(0, 8, rows_of, 0)

    def stage_low(a, at):
        for j in (0, 1):
            staged_x[j, a, at, :] = sums[1 - x, a, j, at, low].astype(jnp.bfloat16)

    def stage_high(a, at):
        staged_y[0, a, at, :] = sums[1 - x, a, 1 - y, at, high].astype(jnp.bfloat16)
        staged_y[1, a, at, :] = sums[x, a, 1 - y, at, high].astype(jnp.bfloat16)

    each(stage_low)
    grad_copy(0, staged_x, returned_x, beside).start()
    each(stage_high)
    grad_copy(1, staged_y, returned_y, across).start()
    slope_copies = [
        remote(
            slopes.at[a, b], slopes_in.at[z, c], slope_send.at[n], slope_recv.at[z, c], device(a, x, b, y)
        )
        for n, (a, b) in enumerate(line)
    ]
    for copy in slope_copies:
        copy.start()
    slopes_in[z, c] = slopes[z, c]

    @pl.when(middle)
    def _():
        for s in (0, 1):
            line_wait(s, 3)
            add_to(s, near, from_line.at[s, 3])
            line_copy(s, near, 0, near).start()

    grad_copy(0, staged_x, returned_x, beside).wait_recv()

    def second_low(a, at):
        value = sums[x, a, 1 - y, at, low] + returned_x[1 - y, a, at, :].astype(jnp.float32)
        staged_again[0, a, at, :] = value.astype(jnp.bfloat16)

    each(second_low)
    again_stores = [pltpu.make_async_copy(staged_again.at[0], again_out.at[0], load_sem.at[3])]
    again_stores[0].start()
    grad_copy(1, staged_y, returned_y, across).wait_recv()

    def second_high(a, at):
        value = sums[1 - x, a, y, at, high] + returned_y[0, a, at, :].astype(jnp.float32)
        staged_again[1, a, at, :] = value.astype(jnp.bfloat16)

    each(second_high)
    again_stores.append(pltpu.make_async_copy(staged_again.at[1], again_out.at[1], load_sem.at[4]))
    again_stores[1].start()

    def own_grad(a, at):
        sums[x, a, y, at, low] += returned_x[y, a, at, :].astype(jnp.float32)
        sums[x, a, y, at, high] += returned_y[1, a, at, :].astype(jnp.float32)

    each(own_grad)
    stores = [pltpu.make_async_copy(sums.at[x, a, y], own_out.at[a], load_sem.at[a]) for a in range(3)]
    for copy in stores:
        copy.start()

    def finish(slots):
        for s in (0, 1):
            for slot in slots:
                line_wait(s, slot)

            def body(u, carry):
                at = pl.ds(pl.multiple_of(u * 32, 32), 32)
                value = partial[s, z, c, at, :].astype(jnp.float32)
                value = value + from_sibling[s, z, at, :].astype(jnp.float32)
                for slot in slots:
                    value = value + from_line[s, slot, at, :].astype(jnp.float32)
                (back_out, weighted_out)[s][at, :] = value
                return carry

            lax.fori_loop(0, 8, body, 0)

    for s in (0, 1):
        pair_copy(s, z).wait_recv()

    @pl.when(middle)
    def _():
        finish((0, 1))

    @pl.when(edge)
    def _():
        finish((0, 1, 2))

    for a, b in line:
        pltpu.make_async_copy(slopes_in.at[a, b], slopes_in.at[a, b], slope_recv.at[a, b]).wait()
    slope_out[...] = slopes_in[...]
    for s in (0, 1):

        @pl.when(middle)
        def _():
            gather(s, z, 0, device(near, x, c, y)).wait_send()

        gather(s, z, 1, device(far, x, c, y)).wait_send()
        gather(s, z, 2, sibling).wait_send()
        for k in (1, 2, 3):
            gather(s, chip(k), 4 + k, sibling).wait_send()
            line_copy(s, chip(k), 0, near).wait_send()

        @pl.when(middle)
        def _():
            for k in (1, 3):
                gather(s, chip(k), 2 + (k + 1) // 2, device(far, x, c, y)).wait_send()

        for k in range(4):
            pair_copy(s, chip(k)).wait_send()
    for copy in (*gate_copies, *weight_copies, *slope_copies):
        copy.wait_send()
    grad_copy(0, staged_x, returned_x, beside).wait_send()
    grad_copy(1, staged_y, returned_y, across).wait_send()
    for copy in (*stores, *again_stores):
        copy.wait()


def expert_part(rows, upstream, gates, gate_w, up_w, down_w):
    tokens, model_dim = rows.shape
    width = gate_w.shape[1]
    vmem, anywhere = pl.BlockSpec(memory_space=pltpu.VMEM), pl.BlockSpec(memory_space=pl.ANY)
    f32, bf16, dma = jnp.float32, jnp.bfloat16, pltpu.SemaphoreType.DMA
    by_owner = gates.T.reshape(4, 2, 2, tokens).swapaxes(1, 2)
    by_owner = jnp.pad(by_owner, ((0, 0), (0, 0), (0, 6), (0, 0)))
    return pl.pallas_call(
        expert_kernel,
        out_shape=[
            jax.ShapeDtypeStruct((tokens, model_dim), f32),
            jax.ShapeDtypeStruct((tokens, model_dim), f32),
            jax.ShapeDtypeStruct((4, 2, 8, tokens), f32),
            jax.ShapeDtypeStruct((3, width, model_dim), f32),
            jax.ShapeDtypeStruct((2, 3, width, model_dim // 2), bf16),
        ],
        in_specs=[anywhere, anywhere, vmem, anywhere, anywhere, anywhere],
        out_specs=[vmem, vmem, vmem, anywhere, anywhere],
        scratch_shapes=[
            pltpu.VMEM((2, 4, 2, tokens, model_dim), bf16),
            pltpu.VMEM((4, 2, 8, tokens), f32),
            pltpu.VMEM((4, 2, 8, tokens), f32),
            pltpu.VMEM((4, 2, 8, tokens), f32),
            pltpu.VMEM((2, 2, model_dim, width), bf16),
            pltpu.VMEM((2, 2, model_dim, width), bf16),
            pltpu.VMEM((2, 2, width, model_dim), bf16),
            pltpu.VMEM((2, 3, 2, width, model_dim), f32),
            pltpu.VMEM((2, 4, 2, tokens, model_dim), bf16),
            pltpu.VMEM((2, 4, tokens, model_dim), bf16),
            pltpu.VMEM((2, 4, tokens, model_dim), bf16),
            *[pltpu.VMEM((2, 3, width, model_dim // 2), bf16)] * 5,
            dma((6,)),
            dma((2, 8)),
            dma((2, 4, 2)),
            dma((7,)),
            dma((4, 2)),
            dma((7,)),
            dma((4, 2)),
            dma((3, 3)),
            dma((2, 2, 3)),
            dma((2, 4)),
            dma((2, 4)),
            dma((2, 4)),
            dma((2, 4)),
            dma((2,)),
            dma((2,)),
        ],
        compiler_params=pltpu.CompilerParams(
            collective_id=1, has_side_effects=True, vmem_limit_bytes=62 << 20
        ),
        name="expert_part",
    )(rows, upstream, by_owner, gate_w, up_w, down_w)
TAIL_ORDER = (
    (0, 4), (2, 1), (3, 1), (4, 1), (5, 1), (1, 4), (0, 5), (2, 2), (1, 5), (3, 2),
    (4, 2), (5, 2), (0, 6), (2, 3), (1, 6), (3, 3), (4, 3), (2, 4), (5, 3), (3, 4),
    (0, 7), (4, 4), (0, 8), (1, 7), (2, 5), (1, 8), (5, 4), (2, 6), (3, 5), (2, 7),
    (4, 5), (3, 6), (2, 8), (5, 5), (4, 6), (3, 7), (5, 6), (3, 8), (4, 7), (4, 8),
    (5, 7), (5, 8),
)


def turn(value, cosine, sine):
    lane = lax.broadcasted_iota(jnp.int32, value.shape, 1) % HEAD_SIZE
    swapped = jnp.where(
        lane < HEAD_SIZE // 2, pltpu.roll(value, 128 - HEAD_SIZE // 2, 1), pltpu.roll(value, HEAD_SIZE // 2, 1)
    )
    return value * cosine + swapped * sine


def tail_kernel(
    tokens,
    normed,
    query,
    key,
    value,
    mixed,
    middle,
    moe_in,
    upstream_in,
    combined,
    back,
    slopes,
    soft,
    live,
    counts,
    router,
    cosine,
    sine,
    bias,
    attn_gain,
    moe_gain,
    w_query_in,
    w_key_in,
    w_value_in,
    w_out_in,
    again_in,
    own_in,
    output,
    input_grad,
    out_sum,
    query_sum,
    key_sum,
    value_sum,
    small_out,
    tiny_out,
    gate_grad,
    up_grad,
    down_grad,
    w_query,
    w_key,
    w_value,
    w_out,
    keys,
    values,
    key_slopes,
    value_slopes,
    mixed_slope,
    query_slope,
    again,
    returned_again,
    own,
    *rest,
):
    count = 6
    grads, halves, totals, fulls, firsts, seconds, lines = [rest[n * count : (n + 1) * count] for n in range(7)]
    small_sum, small_in, tiny_sum, tiny_in, send, recv, small_send, small_recv, local_sem, load_sem, again_send, again_recv = rest[7 * count :]
    outs = [ref.at[:, :, pl.ds(n * 512, 512)] for ref in (out_sum, query_sum) for n in (0, 1)]
    outs += [key_sum, value_sum]
    z, x, c, y = place()
    sibling, beside, across = device(z, x, 1 - c, y), device(z, 1 - x, c, y), device(z, x, c, 1 - y)
    along = [device((z + k) % 4, x, c, y) for k in (1, 2, 3)]
    loads = [
        pltpu.make_async_copy(source, target, load_sem.at[n])
        for n, (source, target) in enumerate(
            (
                (again_in, again),
                (w_out_in, w_out),
                (w_query_in, w_query),
                (w_key_in, w_key),
                (w_value_in, w_value),
                (own_in, own),
            )
        )
    ]
    for copy in loads:
        copy.start()
    greet([sibling, beside, across] + along)
    loads[0].wait()
    again_copies = [
        pltpu.make_async_remote_copy(
            src_ref=again.at[n],
            dst_ref=returned_again.at[n],
            send_sem=again_send.at[n],
            recv_sem=again_recv.at[n],
            device_id=peer,
            device_id_type=MESH,
        )
        for n, peer in enumerate((across, beside))
    ]
    for copy in again_copies:
        copy.start()
    bits = ((x, y), (y, x))
    partners = ((beside, across), (across, beside))

    def push(i, slot, source, target, peer):
        copy = pltpu.make_async_remote_copy(
            src_ref=source,
            dst_ref=target,
            send_sem=send.at[i, slot],
            recv_sem=recv.at[i, slot],
            device_id=peer,
            device_id_type=MESH,
        )
        copy.start()
        return copy

    def combine(i, target, start, length, terms):
        def body(u, carry):
            value = totals[i][start + u].astype(jnp.float32)
            for ref, base in terms:
                value = value + ref[base + u].astype(jnp.float32)
            target[0][target[1] + u] = value.astype(jnp.bfloat16)
            return carry

        lax.fori_loop(0, length, body, 0)

    copies = {}

    def stage(i, step):
        if step == 0:
            copies[i, 0] = [
                push(i, 0, grads[i].at[pl.ds((1 - c) * 32, 32)], halves[i], sibling)
            ]
        if step == 1:
            copies[i, 0][0].wait_recv()

            def body(u, carry):
                value = grads[i][c * 32 + u].astype(jnp.float32) + halves[i][u].astype(jnp.float32)
                totals[i][u] = value.astype(jnp.bfloat16)
                return carry

            lax.fori_loop(0, 32, body, 0)
            copies[i, 1] = [
                push(
                    i,
                    1 + part,
                    totals[i].at[pl.ds(part * 16 + (1 - bits[part][0]) * 8, 8)],
                    firsts[i].at[part],
                    partners[part][0],
                )
                for part in (0, 1)
            ]
        if step == 2:
            copies[i, 2] = []
            for part in (0, 1):
                copies[i, 1][part].wait_recv()
                base = part * 16 + bits[part][0] * 8
                combine(i, (totals[i], base), base, 8, [(firsts[i].at[part], 0)])
                copies[i, 2].append(
                    push(
                        i,
                        3 + part,
                        totals[i].at[pl.ds(base + (1 - bits[part][1]) * 4, 4)],
                        seconds[i].at[part],
                        partners[part][1],
                    )
                )
        if step == 3:
            copies[i, 3] = []
            for part in (0, 1):
                copies[i, 2][part].wait_recv()
                base = part * 16 + bits[part][0] * 8 + bits[part][1] * 4
                combine(i, (totals[i], base), base, 4, [(seconds[i].at[part], 0)])
                for k in (1, 2, 3):
                    copies[i, 3].append(
                        push(
                            i,
                            5 + part * 3 + k - 1,
                            totals[i].at[base + (z + k) % 4],
                            lines[i].at[part, k - 1],
                            along[k - 1],
                        )
                    )
        if step == 4:
            copies[i, 4] = []
            for part in (0, 1):
                for k in (1, 2, 3):
                    copies[i, 3][part * 3 + k - 1].wait_recv()
                base = part * 16 + bits[part][0] * 8 + bits[part][1] * 4
                combine(
                    i, (fulls[i], c * 32 + base + z), base + z, 1, [(lines[i].at[part], k) for k in (0, 1, 2)]
                )
                for k in (1, 2, 3):
                    piece = fulls[i].at[c * 32 + base + z]
                    copies[i, 4].append(push(i, 11 + part * 3 + k - 1, piece, piece, along[k - 1]))
        if step == 5:
            copies[i, 5] = []
            for part in (0, 1):
                for k in (1, 2, 3):
                    copies[i, 4][part * 3 + k - 1].wait_recv()
                piece = fulls[i].at[pl.ds(c * 32 + part * 16 + bits[part][0] * 8 + bits[part][1] * 4, 4)]
                copies[i, 5].append(push(i, 17 + part, piece, piece, partners[part][1]))
        if step == 6:
            copies[i, 6] = []
            for part in (0, 1):
                copies[i, 5][part].wait_recv()
                piece = fulls[i].at[pl.ds(c * 32 + part * 16 + bits[part][0] * 8, 8)]
                copies[i, 6].append(push(i, 19 + part, piece, piece, partners[part][0]))
        if step == 7:
            for part in (0, 1):
                copies[i, 6][part].wait_recv()
            piece = fulls[i].at[pl.ds(c * 32, 32)]
            copies[i, 7] = [push(i, 21, piece, piece, sibling)]
        if step == 8:
            copies[i, 7][0].wait_recv()
            done = pltpu.make_async_copy(fulls[i], outs[i], local_sem.at[i])
            done.start()
            copies[i, 8] = [done]

    def small_stage(n, step):
        total, arrived = (small_sum, tiny_sum)[n], (small_in, tiny_in)[n]

        def small_push(slot, peer, source, target):
            copy = pltpu.make_async_remote_copy(
                src_ref=total.at[source],
                dst_ref=arrived.at[target],
                send_sem=small_send.at[n, slot],
                recv_sem=small_recv.at[n, slot],
                device_id=peer,
                device_id_type=MESH,
            )
            copy.start()
            copies.setdefault((n, "s", step), []).append(copy)

        if step == 0:
            small_push(0, sibling, 0, 0)
        if step in (1, 2, 3):
            copies[n, "s", step - 1][0].wait_recv()
            total[step] = total[step - 1] + arrived[step - 1]
        if step in (1, 2):
            small_push(step, (beside, across)[step - 1], step, step)
        if step == 3:
            for k in (1, 2, 3):
                small_push(2 + k, along[k - 1], 3, 3 + z)
            arrived[3 + z] = total[3]
        if step == 4:
            for copy in copies[n, "s", 3]:
                copy.wait_recv()
            (small_out, tiny_out)[n][...] = (arrived[3] + arrived[4]) + (arrived[5] + arrived[6])

    inner = upstream_in[...].astype(jnp.float32)
    slope_rows = jnp.concatenate([slopes[e // 4, e % 2, pl.ds((e // 2) % 2, 1), :] for e in range(16)], axis=0)
    soft_slope = slope_rows * live[...]
    soft_t = soft[...]
    dlogits = soft_t * (soft_slope - jnp.sum(soft_t * soft_slope, axis=0, keepdims=True))
    dlogits = dlogits.astype(jnp.bfloat16)
    small_sum[0] = jnp.zeros(small_sum.shape[1:], jnp.float32)
    small_sum[0, pl.ds(0, 16), :] = contract(dlogits, moe_in[...], 1, 0)
    small_sum[0, pl.ds(18, 1), :] = counts[...]
    dmoe_in = back[...] + contract(dlogits, router[...], 0, 0)
    mid = middle[...]
    output[...] = (mid + combined[...]).astype(jnp.bfloat16)
    inverse = lax.rsqrt(jnp.mean(mid * mid, axis=1, keepdims=True) + EPSILON)
    small_sum[0, pl.ds(17, 1), :] = jnp.sum(dmoe_in * mid * inverse, axis=0, keepdims=True)
    scaled = dmoe_in * moe_gain[...]
    dmiddle = inner + inverse * (
        scaled - mid * inverse * inverse * jnp.mean(scaled * mid, axis=1, keepdims=True)
    )
    input_grad[...] = dmiddle
    dattn = dmiddle.astype(jnp.bfloat16)

    def weight_grad(i, left, right):
        for r in range(4):
            rows = contract(left[:, pl.ds(r * 256, 256)], right, 0, 0).astype(jnp.bfloat16)
            grads[i][pl.ds(r * 16, 16)] = rows.reshape(16, 16, 512)

    small_stage(0, 0)
    weight_grad(0, mixed, dattn[:, :512])
    stage(0, 0)
    weight_grad(1, mixed, dattn[:, 512:])
    stage(1, 0)
    loads[1].wait()
    mixed_slope[...] = contract(dattn, w_out[...], 1, 1).astype(jnp.bfloat16)
    for g in range(8):
        keys[g] = key[:, pl.ds(g * 64, 64)]
        values[g] = value[:, pl.ds(g * 64, 64)]
    scale = HEAD_SIZE ** (-0.5)

    def group(g, carry):
        columns = pl.ds(pl.multiple_of(g * 128, 128), 128)
        key_g, value_g = keys[g], values[g]
        query_pair, slope_pair = query[:, columns], mixed_slope[:, columns]
        key_slope = jnp.zeros((256, 64), jnp.float32)
        value_slope = jnp.zeros((256, 64), jnp.float32)
        query_slopes = []
        for r in (0, 1):
            query_h, slope_h = query_pair[:, r * 64 : r * 64 + 64], slope_pair[:, r * 64 : r * 64 + 64]
            scores = contract(query_h, key_g, 1, 1) * scale + bias[...]
            weights = jnp.exp(scores - jnp.max(scores, axis=1, keepdims=True))
            probs = weights / jnp.sum(weights, axis=1, keepdims=True)
            prob_slope = contract(slope_h, value_g, 1, 1)
            value_slope = value_slope + contract(probs.astype(jnp.bfloat16), slope_h, 0, 0)
            delta = jnp.sum(probs * prob_slope, axis=1, keepdims=True)
            score_slope = (probs * (prob_slope - delta)).astype(jnp.bfloat16)
            query_slopes.append(contract(score_slope, key_g, 1, 0) * scale)
            key_slope = key_slope + contract(score_slope, query_h, 0, 0) * scale
        pair = turn(jnp.concatenate(query_slopes, axis=1), cosine[...], -sine[...])
        query_slope[:, columns] = pair.astype(jnp.bfloat16)
        key_slopes[g] = key_slope
        value_slopes[g] = value_slope
        return carry

    stage(0, 1)
    stage(1, 1)
    small_stage(0, 1)
    lax.fori_loop(0, 5, group, 0)
    small_stage(0, 2)
    stage(0, 2)
    stage(1, 2)
    lax.fori_loop(5, 8, group, 0)
    small_stage(0, 3)
    stage(0, 3)
    stage(1, 3)
    loads[2].wait()
    loads[3].wait()
    loads[4].wait()
    for n in (0, 1):
        weight_grad(2 + n, normed, query_slope[:, n * 512 : n * 512 + 512])
        stage(2 + n, 0)
    key_slope = jnp.concatenate(
        [
            turn(jnp.concatenate([key_slopes[2 * p], key_slopes[2 * p + 1]], axis=1), cosine[...], -sine[...])
            for p in range(4)
        ],
        axis=1,
    ).astype(jnp.bfloat16)
    weight_grad(4, normed, key_slope)
    stage(4, 0)
    value_slope = jnp.concatenate(
        [jnp.concatenate([value_slopes[2 * p], value_slopes[2 * p + 1]], axis=1) for p in range(4)], axis=1
    ).astype(jnp.bfloat16)
    weight_grad(5, normed, value_slope)
    stage(5, 0)
    todo = list(TAIL_ORDER)

    def proceed(steps):
        for _ in range(min(steps, len(todo))):
            stage(*todo.pop(0))

    proceed(6)
    dnormed = contract(query_slope[...], w_query[...], 1, 1)
    dnormed = dnormed + contract(key_slope, w_key[...], 1, 1)
    dnormed = dnormed + contract(value_slope, w_value[...], 1, 1)
    start = tokens[...].astype(jnp.float32)
    inverse = lax.rsqrt(jnp.mean(start * start, axis=1, keepdims=True) + EPSILON)
    gain_slope = jnp.sum(dnormed * start * inverse, axis=0, keepdims=True)
    for r in range(8):
        tiny_sum[0, pl.ds(r, 1), :] = gain_slope[:, r * 128 : r * 128 + 128]
    scaled = dnormed * attn_gain[...]
    input_grad[...] += inverse * (
        scaled - start * inverse * inverse * jnp.mean(scaled * start, axis=1, keepdims=True)
    )
    small_stage(1, 0)
    proceed(4)
    small_stage(1, 1)
    proceed(4)
    small_stage(1, 2)
    small_stage(0, 4)
    loads[5].wait()
    for copy in again_copies:
        copy.wait_recv()
    for a, target in enumerate((gate_grad, up_grad, down_grad)):
        for n in (0, 1):
            columns = pl.ds(n * 512, 512)
            summed = own[a, :, columns] + returned_again[n, a].astype(jnp.float32)
            if a < 2:
                target[columns, :] = summed.T
            else:
                target[:, columns] = summed
    proceed(4)
    small_stage(1, 3)
    proceed(4)
    small_stage(1, 4)
    proceed(len(todo))
    for key_of, made in copies.items():
        for copy in made:
            if key_of[1] == 8:
                copy.wait()
            else:
                copy.wait_send()
    for copy in again_copies:
        copy.wait_send()


def tail_part(operands, weights, again, own):
    tokens, model_dim = operands[0].shape
    narrow = weights[1].shape[1]
    vmem, anywhere = pl.BlockSpec(memory_space=pltpu.VMEM), pl.BlockSpec(memory_space=pl.ANY)
    f32, bf16, dma = jnp.float32, jnp.bfloat16, pltpu.SemaphoreType.DMA
    widths = (model_dim, model_dim, narrow, narrow)
    leads = ((64,), (32,), (32,), (64,), (2, 8), (2, 4), (2, 3))
    shape = jax.ShapeDtypeStruct
    width = own.shape[1]
    out = pl.pallas_call(
        tail_kernel,
        out_shape=[
            shape((tokens, model_dim), bf16),
            shape((tokens, model_dim), f32),
            *[shape((64, UNIT, w), bf16) for w in widths],
            shape((24, model_dim), f32),
            shape((8, 128), f32),
            shape((model_dim, width), f32),
            shape((model_dim, width), f32),
            shape((width, model_dim), f32),
        ],
        in_specs=[vmem] * len(operands) + [anywhere] * 6,
        out_specs=[vmem, vmem] + [anywhere] * 4 + [vmem] * 5,
        scratch_shapes=[
            *[pltpu.VMEM(w.shape, bf16) for w in weights],
            pltpu.VMEM((8, tokens, HEAD_SIZE), bf16),
            pltpu.VMEM((8, tokens, HEAD_SIZE), bf16),
            pltpu.VMEM((8, tokens, HEAD_SIZE), f32),
            pltpu.VMEM((8, tokens, HEAD_SIZE), f32),
            pltpu.VMEM((tokens, model_dim), bf16),
            pltpu.VMEM((tokens, model_dim), bf16),
            pltpu.VMEM(again.shape, bf16),
            pltpu.VMEM(again.shape, bf16),
            pltpu.VMEM(own.shape, f32),
            *[pltpu.VMEM((*lead, UNIT, 512), bf16) for lead in leads for _ in range(6)],
            pltpu.VMEM((4, 24, model_dim), f32),
            pltpu.VMEM((7, 24, model_dim), f32),
            pltpu.VMEM((4, 8, 128), f32),
            pltpu.VMEM((7, 8, 128), f32),
            dma((6, 22)),
            dma((6, 22)),
            dma((2, 6)),
            dma((2, 6)),
            dma((6,)),
            dma((6,)),
            dma((2,)),
            dma((2,)),
        ],
        compiler_params=pltpu.CompilerParams(
            collective_id=0, has_side_effects=True, vmem_limit_bytes=60 << 20
        ),
        name="tail_part",
    )(*operands, *weights, again, own)
    grads = [o.reshape(-1, o.shape[2]).astype(jnp.float32) for o in out[2:6]]
    return (out[0], out[1], grads, out[6], out[7], out[8:11])


def local(
    tokens,
    segment_ids,
    live_mask,
    routes,
    attn_gain,
    w_query,
    key_weight,
    value_weight,
    w_out,
    moe_gain,
    router,
    w_gate,
    w_up,
    w_down,
    cotangent,
):
    sequence_length = tokens.shape[0]
    model_dim = tokens.shape[1]
    experts_all = router.shape[1]
    query_per_key_head = QUERY_HEADS // KEY_VALUE_HEADS
    score_scale = HEAD_SIZE ** (-0.5)
    special = lax.axis_size("ep") == 16 and lax.axis_size("hs") == 2
    segment = segment_ids[0]
    live_row = live_mask[0]
    inputs = tokens.astype(jnp.float32)
    normed_rows, inverse_one = rms_forward(inputs, attn_gain)
    normed_rows_back = normed_rows.astype(jnp.bfloat16)
    query_pre = jnp.dot(normed_rows_back, w_query, preferred_element_type=jnp.float32).reshape(
        sequence_length, QUERY_HEADS, HEAD_SIZE
    )
    key_before_rotary = jnp.dot(
        normed_rows_back, key_weight, preferred_element_type=jnp.float32
    ).reshape(sequence_length, KEY_VALUE_HEADS, HEAD_SIZE)
    value_b = (
        jnp.dot(normed_rows_back, value_weight, preferred_element_type=jnp.float32)
        .astype(jnp.bfloat16)
        .reshape(sequence_length, KEY_VALUE_HEADS, HEAD_SIZE)
    )
    positions = positions_of(segment)
    cosine_table, sine_table = rotary_tables(positions, HEAD_SIZE)
    query_back_rows = rotary(query_pre, cosine_table, sine_table).astype(jnp.bfloat16)
    key_b = rotary(key_before_rotary, cosine_table, sine_table).astype(jnp.bfloat16)
    indices = jnp.arange(sequence_length)
    allowed = (
        (segment[:, None] == segment[None, :])
        & (indices[None, :] <= indices[:, None])
        & ((live_row[None, :] > 0) | (indices[None, :] == indices[:, None]))
    )
    grouped_rows = query_back_rows.reshape(
        sequence_length, KEY_VALUE_HEADS, query_per_key_head, HEAD_SIZE
    )
    scores = (
        jnp.einsum("qgrd,kgd->grqk", grouped_rows, key_b, preferred_element_type=jnp.float32)
        * score_scale
    )
    scores = jnp.where(allowed, scores, -1e30)
    highest = jnp.max(scores, axis=-1, keepdims=True)
    weights_exp = jnp.exp(scores - highest)
    denominator = jnp.sum(weights_exp, axis=-1, keepdims=True)
    log_total = highest + jnp.log(denominator)
    probabilities = weights_exp / denominator
    mixed = jnp.einsum(
        "grqk,kgd->qgrd",
        probabilities.astype(jnp.bfloat16),
        value_b,
        preferred_element_type=jnp.float32,
    )
    mixed_b = mixed.reshape(sequence_length, QUERY_HEADS * HEAD_SIZE).astype(jnp.bfloat16)
    middle = inputs + jnp.dot(mixed_b, w_out, preferred_element_type=jnp.float32)
    moe_normed, inverse_two = rms_forward(middle, moe_gain)
    moe_in = moe_normed.astype(jnp.bfloat16)
    logits = jnp.dot(moe_in, router, preferred_element_type=jnp.float32)
    route_hot = (routes[:, :, None] == jnp.arange(experts_all)[None, None, :]).astype(jnp.float32)
    chosen = jnp.sum(route_hot * logits[:, None, :], axis=-1)
    route_soft = jax.nn.softmax(chosen, axis=-1)
    live_column = live_row.astype(jnp.float32)[:, None]
    route_gates = route_soft * live_column
    counts_local = jnp.sum(route_hot * live_column[:, :, None], axis=(0, 1))
    dense_gates = jnp.sum(route_hot * route_gates[:, :, None], axis=1)
    if special:
        route_soft_dense = jnp.sum(route_hot * route_soft[:, :, None], axis=1)
        combined, back, slopes, own, again = expert_part(
            moe_in, cotangent, dense_gates, w_gate[0], w_up[0], w_down[0]
        )
        sign = jnp.concatenate([-sine_table[:, 0], sine_table[:, 0]], axis=1)
        operands = (
            tokens,
            normed_rows_back,
            query_back_rows.reshape(sequence_length, -1),
            key_b.reshape(sequence_length, -1),
            value_b.reshape(sequence_length, -1),
            mixed_b,
            middle,
            moe_in,
            cotangent,
            combined,
            back,
            slopes,
            route_soft_dense.T,
            live_row.astype(jnp.float32)[None],
            jnp.pad(counts_local, (0, model_dim - experts_all))[None],
            router.T,
            jnp.tile(cosine_table[:, 0], (1, 4)),
            jnp.tile(sign, (1, 2)),
            jnp.where(allowed, 0.0, -1e30),
            attn_gain[None],
            moe_gain[None],
        )
        output, input_grad, grads, small, tiny, expert_grads = tail_part(
            operands, (w_query, key_weight, value_weight, w_out), again, own
        )
        return (
            output,
            input_grad,
            tiny.reshape(model_dim),
            grads[1],
            grads[2],
            grads[3],
            grads[0],
            small[17],
            small[:experts_all].T,
            *[g[None] for g in expert_grads],
            small[18, :experts_all].astype(jnp.int32),
        )
    upstream_all = lax.all_gather(cotangent, "ep", axis=0, tiled=True)
    gate_all = lax.all_gather(w_gate, "hs", axis=0, tiled=True)
    up_all = lax.all_gather(w_up, "hs", axis=0, tiled=True)
    down_all = lax.all_gather(w_down, "hs", axis=0, tiled=True)
    rows_all = lax.all_gather(moe_in, "ep", axis=0, tiled=True)
    gates_all = lax.all_to_all(
        dense_gates.T.reshape(experts_all, 1, sequence_length), "ep", split_axis=0, concat_axis=1, tiled=True
    ).reshape(-1)
    weighted, back, gate_upstream_all, gate_w_grad, up_w_grad, down_w_grad = expert_pass(
        rows_all, upstream_all, gates_all, gate_all, up_all, down_all
    )
    combined = lax.psum_scatter(weighted, "ep", scatter_dimension=0, tiled=True).astype(jnp.float32)
    expert_input_grad = lax.psum_scatter(back, "ep", scatter_dimension=0, tiled=True).astype(jnp.float32)
    gate_upstream_dense = lax.all_to_all(
        gate_upstream_all.reshape(experts_all, 1, sequence_length), "ep", split_axis=0, concat_axis=1, tiled=True
    ).reshape(experts_all, sequence_length).T
    gate_w_grad = sum_halves(gate_w_grad, 1)[None]
    up_w_grad = sum_halves(up_w_grad, 1)[None]
    down_w_grad = sum_halves(down_w_grad, 0)[None]
    output = (middle + combined).astype(jnp.bfloat16)
    upstream = cotangent.astype(jnp.float32)
    gate_upstream = jnp.sum(route_hot * gate_upstream_dense[:, None, :], axis=-1)
    soft_upstream = gate_upstream * live_column
    chosen_grad = route_soft * (
        soft_upstream - jnp.sum(route_soft * soft_upstream, axis=-1, keepdims=True)
    )
    logit_grad = jnp.sum(route_hot * chosen_grad[:, :, None], axis=1).astype(jnp.bfloat16)
    router_w_grad = jnp.einsum("td,te->de", moe_in, logit_grad, preferred_element_type=jnp.float32)
    moe_in_grad = expert_input_grad + jnp.einsum(
        "te,de->td", logit_grad, router, preferred_element_type=jnp.float32
    )
    middle_norm_grad, moe_gain_grad = rms_backward(middle, inverse_two, moe_gain, moe_in_grad)
    middle_grad = upstream + middle_norm_grad
    attn_grad_b = middle_grad.astype(jnp.bfloat16)
    out_w_grad = jnp.einsum("tm,td->md", mixed_b, attn_grad_b, preferred_element_type=jnp.float32)
    attention_mixed_grad = jnp.einsum(
        "td,md->tm", attn_grad_b, w_out, preferred_element_type=jnp.float32
    ).astype(jnp.bfloat16)
    attention_mixed_grad = attention_mixed_grad.reshape(
        sequence_length, KEY_VALUE_HEADS, query_per_key_head, HEAD_SIZE
    )
    scores_again = (
        jnp.einsum("qgrd,kgd->grqk", grouped_rows, key_b, preferred_element_type=jnp.float32)
        * score_scale
    )
    scores_again = jnp.where(allowed, scores_again, -1e30)
    probs_again = jnp.exp(scores_again - log_total)
    prob_grad = jnp.einsum(
        "qgrd,kgd->grqk", attention_mixed_grad, value_b, preferred_element_type=jnp.float32
    )
    value_per_head_grad = jnp.einsum(
        "grqk,qgrd->kgd",
        probs_again.astype(jnp.bfloat16),
        attention_mixed_grad,
        preferred_element_type=jnp.float32,
    )
    value_per_head_grad = value_per_head_grad.astype(jnp.bfloat16).reshape(
        sequence_length, KEY_VALUE_HEADS * HEAD_SIZE
    )
    row_delta = jnp.sum(probs_again * prob_grad, axis=-1, keepdims=True)
    score_grad = (probs_again * (prob_grad - row_delta)).astype(jnp.bfloat16)
    query_rot_grad = (
        jnp.einsum("grqk,kgd->qgrd", score_grad, key_b, preferred_element_type=jnp.float32)
        * score_scale
    )
    rotated_key_grad = (
        jnp.einsum("grqk,qgrd->kgd", score_grad, grouped_rows, preferred_element_type=jnp.float32)
        * score_scale
    )
    query_head_grad = (
        rotary_backward(
            query_rot_grad.reshape(sequence_length, QUERY_HEADS, HEAD_SIZE),
            cosine_table,
            sine_table,
        )
        .astype(jnp.bfloat16)
        .reshape(sequence_length, QUERY_HEADS * HEAD_SIZE)
    )
    key_head_grad = (
        rotary_backward(rotated_key_grad, cosine_table, sine_table)
        .astype(jnp.bfloat16)
        .reshape(sequence_length, KEY_VALUE_HEADS * HEAD_SIZE)
    )
    query_w_grad = jnp.einsum(
        "td,te->de", normed_rows_back, query_head_grad, preferred_element_type=jnp.float32
    )
    key_w_grad = jnp.einsum(
        "td,te->de", normed_rows_back, key_head_grad, preferred_element_type=jnp.float32
    )
    value_w_grad = jnp.einsum(
        "td,te->de", normed_rows_back, value_per_head_grad, preferred_element_type=jnp.float32
    )
    normed_grad = jnp.einsum(
        "te,de->td", query_head_grad, w_query, preferred_element_type=jnp.float32
    )
    normed_grad = normed_grad + jnp.einsum(
        "te,de->td", key_head_grad, key_weight, preferred_element_type=jnp.float32
    )
    normed_grad = normed_grad + jnp.einsum(
        "te,de->td", value_per_head_grad, value_weight, preferred_element_type=jnp.float32
    )
    input_norm_grad, attn_gain_grad = rms_backward(inputs, inverse_one, attn_gain, normed_grad)
    input_grad = middle_grad + input_norm_grad
    (
        attn_gain_grad,
        query_w_grad,
        key_w_grad,
        value_w_grad,
        out_w_grad,
        moe_gain_grad,
        router_w_grad,
        counts,
    ) = lax.psum(
        (
            attn_gain_grad,
            query_w_grad,
            key_w_grad,
            value_w_grad,
            out_w_grad,
            moe_gain_grad,
            router_w_grad,
            counts_local,
        ),
        ("ep", "hs"),
    )
    return (
        output,
        input_grad,
        attn_gain_grad,
        query_w_grad,
        key_w_grad,
        value_w_grad,
        out_w_grad,
        moe_gain_grad,
        router_w_grad,
        gate_w_grad,
        up_w_grad,
        down_w_grad,
        counts.astype(jnp.int32),
    )


def solution(mesh):
    in_specs = (
        P(("ep", "hs"), None),
        P(("ep", "hs"), None),
        P(("ep", "hs"), None),
        P(("ep", "hs"), None),
        P(),
        P(),
        P(),
        P(),
        P(),
        P(),
        P(),
        P("ep", None, "hs"),
        P("ep", None, "hs"),
        P("ep", "hs", None),
        P(("ep", "hs"), None),
    )
    out_specs = (
        P(("ep", "hs"), None),
        P(("ep", "hs"), None),
        P(),
        P(),
        P(),
        P(),
        P(),
        P(),
        P(),
        P("ep", None, "hs"),
        P("ep", None, "hs"),
        P("ep", "hs", None),
        P(),
    )
    return jax.shard_map(local, mesh=mesh, in_specs=in_specs, out_specs=out_specs, check_vma=False)
```

time: 335 us -> 320 us (0.955)
  matrix products: 26.5 us -> 8.42 us
  Pallas kernels: 270 us -> 274 us
    pallas_call x1, Pallas kernels: 78.8 us -> 115 us  [tail_part(): pl.pallas_call(tail_kernel, out_shape=[shape((tokens, model_dim), bf16),...]
    pallas_call x1, Pallas kernels: 191 us -> 159 us  [expert_part(): pl.pallas_call(expert_kernel, out_shape=[jax.ShapeDtypeStruct((tokens, mo...]
    dot_general x14 -> x0, matrix products: 18.7 us -> none  [the longest x1 3.39 us: local(): jnp.einsum('qgrd,kgd->grqk', attention_mixed_grad, value_b, preferred_ele...]
    unnamed x69 -> x44, local copies, waits for them, and re-layouts: 11.3 us -> 5.36 us
    add x3 -> x0, other arithmetic: 4.26 us -> none  [the longest x1 2.93 us: local(): middle_grad = upstream + middle_norm_grad]
    convert_element_type x4 -> x5, other arithmetic: 11.1 us -> 12.2 us  [the longest x2 8.87 us: tail_part(): grads = [o.reshape(-1, o.shape[2]).astype(jnp.float32) for o in out[2:6]]]
where the time goes in v5:
time: 320 us
  Pallas kernels  274 us (86%)
  other arithmetic  20.7 us (6%)
  local copies, waits for them, and re-layouts  15.8 us (5%)
  matrix products  8.42 us (3%)
    pallas_call x1, Pallas kernels, expert_part(): pl.pallas_call(expert_kernel, out_shape=[jax.ShapeDtypeStruct((tokens, mo...  159 us
    pallas_call x1, Pallas kernels, tail_part(): pl.pallas_call(tail_kernel, out_shape=[shape((tokens, model_dim), bf16),...  115 us
    convert_element_type x2, other arithmetic, tail_part(): grads = [o.reshape(-1, o.shape[2]).astype(jnp.float32) for o in out[2:6]]  8.87 us

profile of v5, /device:TPU:0, one launch (start us, length us, event | category | flops | bytes accessed | tf_op | source)
XLA Modules:
  0.0 319.5 jit_solution(9351311337320007993)
XLA Ops:
  0.6 0.7 compare_reduce_fusion
  1.4 0.7 convert_element_type.109.live
  2.0 0.9 convert_reduce_fusion
  3.0 1.2 fusion.7
  4.2 0.9 fusion.16
  5.5 0.7 copy.66.sine
  6.3 0.8 copy.65.cosine
  7.0 1.6 broadcast_select_fusion.bias
  8.6 1.2 fusion.9.normed
  9.8 1.8 convolution_convert_fusion.value
  11.7 0.8 copy.58
  12.5 1.7 fusion.27
  14.4 0.7 maximum_convert_fusion
  15.1 1.8 copy.63.key
  16.9 0.9 fusion.26
  18.1 1.0 copy.62.query
  19.1 0.8 fusion.10
  19.9 1.2 fusion.25
  21.6 1.0 copy.64.mixed
  22.6 2.4 multiply_reduce_fusion
  27.5 158.5 %expert_part.1 = (f32[256,1024]{1,0:T(8,128)}, f32[256,1024]{1,0:T(8,128)}, f32[4,2,8,256]{3,2,1,0:T(8,128)}, f32[3,256,1024]{2,1,0:T(8,128)}, bf16[2,3,256,512]{3,2,1,0:T(8,128)(2,1)}) custom-call(bf16[256,1024]{1,0:T(8,128)(2,1)} %copy-done.3, bf16[256,1024]{1,0:T(8,128)(2,1)} %upstream_in.3, f32[4,2,8,256]{3,2,1,0:T(8,128)} %pad.8.gates_in, ...), custom_call_target="tpu_custom_call" | custom-call | tf_op jit(solution)/shard_map/expert_part/pallas_call | solution.py:578
  186.1 115.1 %tail_part.1 = (bf16[256,1024]{1,0:T(8,128)(2,1)}, f32[256,1024]{1,0:T(8,128)}, bf16[64,16,1024]{2,1,0:T(8,128)(2,1)}, bf16[64,16,1024]{2,1,0:T(8,128)(2,1)}, bf...) custom-call(bf16[256,1024]{1,0:T(8,128)(2,1)} %tokens.1, ...), custom_call_target="tpu_custom_call" | custom-call | tf_op jit(solution)/shard_map/tail_part/pallas_call | solution.py:1034
  301.1 1.3 convert_bitcast_fusion
  302.5 1.4 slice.25
  303.8 1.5 slice_bitcast_fusion
  305.3 4.1 %bitcast_convert_fusion.2 = (f32[1024,512]{1,0:T(8,128)}, f32[1024,512]{1,0:T(8,128)}) fusion(bf16[64,16,512]{2,1,0:T(8,128)(2,1)} %get-tuple-element.39, bf16[64,16,512]{2,1,0:T(8,128)(2,1)} %get-tuple-element.38), kind=kLoop, calls=%fused_computation.19 | loop fusion | flops 1048576 | bytes 6291456 | tf_op jit(solution)/shard_map/convert_element_type | solution.py:1078
  309.5 4.7 %bitcast_convert_fusion = (f32[1024,1024]{1,0:T(8,128)}, f32[1024,1024]{1,0:T(8,128)}) fusion(bf16[64,16,1024]{2,1,0:T(8,128)(2,1)S(1)} %copy-done.6, bf16[64,16,1024]{2,1,0:T(8,128)(2,1)S(1)} %copy-done.7), kind=kLoop, calls=%fused_computation.5 | loop fusion | flops 2097152 | bytes 12582912 | tf_op jit(solution)/shard_map/convert_element_type | solution.py:1078
  314.2 0.8 copy.80
  315.0 1.0 copy.81
  316.6 1.0 copy.83
  317.6 1.0 copy.84
  318.5 1.0 copy.85
  (63 shorter events, 4.3 us)
Async XLA Ops:
  2.0 23.6 %copy-start.16 = (f32[1,256]{1,0:T(1,128)}, f32[1,256]{1,0:T(1,128)S(1)}, u32[]{:S(2)}) copy-start(f32[1,256]{1,0:T(1,128)S(1)} %convert_element_type.109.live) | copy-start | bytes 3076
  5.5 11.4 %copy-start.4 = (bf16[1024,1024]{1,0:T(8,128)(2,1)S(1)}, bf16[1024,1024]{1,0:T(8,128)(2,1)}, u32[]{:S(2)}) copy-start(bf16[1024,1024]{1,0:T(8,128)(2,1)} %w_query_in.1) | copy-start | bytes 6291460
  9.8 8.0 %copy-start = (bf16[256,1024]{1,0:T(8,128)(2,1)}, bf16[256,1024]{1,0:T(8,128)(2,1)S(1)}, u32[]{:S(2)}) copy-start(bf16[256,1024]{1,0:T(8,128)(2,1)S(1)} %fusion.9.normed) | copy-start | bytes 1572868
  11.7 6.3 %copy-start.5 = (bf16[256,512]{1,0:T(8,128)(2,1)}, bf16[256,512]{1,0:T(8,128)(2,1)S(1)}, u32[]{:S(2)}) copy-start(bf16[256,512]{1,0:T(8,128)(2,1)S(1)} %convolution_convert_fusion.value) | copy-start | bytes 786436
  19.8 1.2 copy-start.13
  21.1 1.5 copy-start.2
  21.6 3.5 %copy-start.17 = (f32[1024]{0:T(1024)S(1)}, f32[1024]{0:T(1024)}, u32[]{:S(2)}) copy-start(f32[1024]{0:T(1024)} %param.24) | copy-start | bytes 12292
  21.6 3.6 %copy-start.14 = (bf16[1024,16]{0,1:T(8,128)(2,1)S(1)}, bf16[1024,16]{0,1:T(8,128)(2,1)}, u32[]{:S(2)}) copy-start(bf16[1024,16]{0,1:T(8,128)(2,1)} %param.25) | copy-start | bytes 98308
  21.6 3.9 %copy-start.15 = (s32[256,8]{0,1:T(8,128)S(1)}, s32[256,8]{0,1:T(8,128)}, u32[]{:S(2)}) copy-start(s32[256,8]{0,1:T(8,128)} %param.18) | copy-start | bytes 24580
  25.0 161.0 %copy-start.1 = (f32[256,1024]{1,0:T(8,128)}, f32[256,1024]{1,0:T(8,128)S(1)}, u32[]{:S(2)}) copy-start(f32[256,1024]{1,0:T(8,128)S(1)} %get-tuple-element.60.middle) | copy-start | bytes 3145732
  25.2 2.3 copy-start.3
  301.1 8.3 %copy-start.6 = (bf16[64,16,1024]{2,1,0:T(8,128)(2,1)S(1)}, bf16[64,16,1024]{2,1,0:T(8,128)(2,1)}, u32[]{:S(2)}) copy-start(bf16[64,16,1024]{2,1,0:T(8,128)(2,1)} %get-tuple-element.40) | copy-start | bytes 6291460
  301.1 8.3 %copy-start.7 = (bf16[64,16,1024]{2,1,0:T(8,128)(2,1)S(1)}, bf16[64,16,1024]{2,1,0:T(8,128)(2,1)}, u32[]{:S(2)}) copy-start(bf16[64,16,1024]{2,1,0:T(8,128)(2,1)} %get-tuple-element.37) | copy-start | bytes 6291460
  309.5 4.8 %copy-start.12 = (bf16[256,1024]{1,0:T(8,128)(2,1)S(1)}, bf16[256,1024]{1,0:T(8,128)(2,1)}, u32[]{:S(2)}) copy-start(bf16[256,1024]{1,0:T(8,128)(2,1)} %get-tuple-element.78) | copy-start | bytes 1572868
  309.5 5.6 %copy-start.11 = (f32[256,1024]{1,0:T(8,128)S(1)}, f32[256,1024]{1,0:T(8,128)}, u32[]{:S(2)}) copy-start(f32[256,1024]{1,0:T(8,128)} %get-tuple-element.79) | copy-start | bytes 3145732
  309.5 6.5 %copy-start.18 = (f32[8,128]{1,0:T(8,128)S(1)}, f32[8,128]{1,0:T(8,128)}, u32[]{:S(2)}) copy-start(f32[8,128]{1,0:T(8,128)} %get-tuple-element.36) | copy-start | bytes 12292
  309.5 7.1 %copy-start.10 = (f32[1024,256]{1,0:T(8,128)S(1)}, f32[1024,256]{1,0:T(8,128)}, u32[]{:S(2)}) copy-start(f32[1024,256]{1,0:T(8,128)} %get-tuple-element.42) | copy-start | bytes 3145732
  314.2 3.3 %copy-start.9 = (f32[1024,256]{1,0:T(8,128)S(1)}, f32[1024,256]{1,0:T(8,128)}, u32[]{:S(2)}) copy-start(f32[1024,256]{1,0:T(8,128)} %get-tuple-element.43) | copy-start | bytes 3145732
  314.2 4.3 %copy-start.8 = (f32[256,1024]{1,0:T(8,128)S(1)}, f32[256,1024]{1,0:T(8,128)}, u32[]{:S(2)}) copy-start(f32[256,1024]{1,0:T(8,128)} %get-tuple-element.44) | copy-start | bytes 3145732

commit v6 on v5

--- a/solution.py
+++ b/solution.py
@@ -1,7 +1,6 @@
-import functools
-
 import jax
 import jax.numpy as jnp
+import numpy as np
 from jax import lax
 from jax.experimental import pallas as pl
 from jax.experimental.pallas import tpu as pltpu
@@ -141,6 +140,14 @@
 MIDDLE_ORDER = (0, 1, 2, 3, 7, 5, 6, 4)
 
 
+def turn(value, cosine, sine):
+    lane = lax.broadcasted_iota(jnp.int32, value.shape, 1) % HEAD_SIZE
+    swapped = jnp.where(
+        lane < HEAD_SIZE // 2, pltpu.roll(value, 128 - HEAD_SIZE // 2, 1), pltpu.roll(value, HEAD_SIZE // 2, 1)
+    )
+    return value * cosine + swapped * sine
+
+
 def contract(left, right, left_dim, right_dim):
     return lax.dot_general(
         left, right, (((left_dim,), (right_dim,)), ((), ())), preferred_element_type=jnp.float32
@@ -148,18 +155,42 @@
 
 
 def expert_kernel(
-    rows_in,
+    segment,
+    live,
+    routes,
+    rotation,
+    attn_gain,
+    moe_gain,
+    router,
+    tokens_in,
+    w_query_in,
+    w_key_in,
+    w_value_in,
+    w_out_in,
     upstream_in,
-    gates_in,
     gate_w,
     up_w,
     down_w,
+    rows_out,
+    normed,
+    query,
+    key_value,
+    mixed,
+    middle_out,
+    cosine,
+    sine,
+    bias,
+    soft_out,
+    counts,
     weighted_out,
     back_out,
     slope_out,
     own_out,
     again_out,
+    keys,
+    values,
     streams,
+    gates_in,
     gates,
     slopes,
     slopes_in,
@@ -176,6 +207,7 @@
     returned_x,
     returned_y,
     load_sem,
+    head_sem,
     gather_send,
     gather_recv,
     gate_send,
@@ -198,7 +230,6 @@
     sibling, beside, across = device(z, x, 1 - c, y), device(z, 1 - x, c, y), device(z, x, c, 1 - y)
     corner = device(z, 1 - x, c, 1 - y)
     line = [((z + k) % 4, (c + d) % 2) for k in range(4) for d in range(2) if k or d]
-    greet([device(a, x, b, y) for a, b in line] + [beside, across, corner])
 
     def chip(k):
         half = z // 2
@@ -211,17 +242,27 @@
             src_ref=source, dst_ref=target, send_sem=send, recv_sem=recv, device_id=peer, device_id_type=MESH
         )
 
-    own = [
-        pltpu.make_async_copy(ref, streams.at[s, z, c], load_sem.at[s])
-        for s, ref in enumerate((rows_in, upstream_in))
-    ]
-    gates_own = pltpu.make_async_copy(gates_in.at[z, c], gates.at[z, c], load_sem.at[2])
+    own = pltpu.make_async_copy(upstream_in, streams.at[1, z, c], load_sem.at[0])
     weights_own = [
         pltpu.make_async_copy(ref, held.at[x, y], load_sem.at[3 + a])
         for a, (ref, held) in enumerate(((gate_w, w_gate), (up_w, w_up), (down_w, w_down)))
     ]
-    for copy in (*own, gates_own, *weights_own):
+    tokens = from_sibling.at[1, 0]
+    head_loads = [pltpu.make_async_copy(tokens_in, tokens, head_sem.at[0])]
+    for r in range(4):
+        rows = pl.ds(r * 256, 256)
+        for n, (source, target) in enumerate(
+            (
+                (w_query_in, partial.at[0, r // 2, r % 2]),
+                (w_out_in, partial.at[1, r // 2, r % 2]),
+                (w_key_in, from_sibling.at[0, r, :, pl.ds(0, 512)]),
+                (w_value_in, from_sibling.at[0, r, :, pl.ds(512, 512)]),
+            )
+        ):
+            head_loads.append(pltpu.make_async_copy(source.at[rows, :], target, head_sem.at[1 + r * 4 + n]))
+    for copy in (own, *weights_own, *head_loads):
         copy.start()
+    greet([device(a, x, b, y) for a, b in line] + [beside, across, corner])
 
     def gather(s, block, slot, peer):
         piece = streams.at[s, block, c]
@@ -231,8 +272,7 @@
         piece = streams.at[s, block, core]
         pltpu.make_async_copy(piece, piece, gather_recv.at[s, block, core]).wait()
 
-    for s in (0, 1):
-        own[s].wait()
+    def gather_own(s):
         gather(s, z, 0, device(near, x, c, y)).start()
         gather(s, z, 2, sibling).start()
 
@@ -240,14 +280,8 @@
         def _():
             gather(s, z, 1, device(far, x, c, y)).start()
 
-    gate_copies = [
-        remote(
-            gates_in.at[a, b], gates.at[z, c], gate_send.at[n], gate_recv.at[z, c], device(a, x, b, y)
-        )
-        for n, (a, b) in enumerate(line)
-    ]
-    for copy in gate_copies:
-        copy.start()
+    own.wait()
+    gather_own(1)
     weight_copies = []
     for a, held in enumerate((w_gate, w_up, w_down)):
         weights_own[a].wait()
@@ -276,17 +310,9 @@
             )
         return carry
 
-    lax.fori_loop(0, 32, zero, 0)
-
-    @pl.when(edge)
-    def _():
-        for s in (0, 1):
-            gather(s, z, 0, device(near, x, c, y)).wait_send()
-            gather(s, z, 1, device(far, x, c, y)).start()
-
-    def handle(k):
+    def handle(k, order=(1, 0)):
         block = chip(k)
-        for s in (0, 1):
+        for s in order:
             arrive(s, block, c)
             gather(s, block, 4 + k, sibling).start()
             if k != 2:
@@ -295,16 +321,110 @@
                 def _():
                     gather(s, block, 2 + (k + 1) // 2, device(far, x, c, y)).start()
 
-    handle(1)
-    gates_own.wait()
+    row_id = lax.broadcasted_iota(jnp.int32, (256, 256), 0)
+    lane_id = lax.broadcasted_iota(jnp.int32, (256, 256), 1)
+    diagonal = row_id == lane_id
+    segment_row = segment[...].astype(jnp.float32)
+    segment_column = jnp.sum(jnp.where(diagonal, segment_row, 0.0), axis=1, keepdims=True)
+    live_row = live[...].astype(jnp.float32)
+    before = jnp.sum(jnp.where(segment_row < segment_column, 1.0, 0.0), axis=1, keepdims=True)
+    position = lax.broadcasted_iota(jnp.int32, (256, 128), 0).astype(jnp.float32) - before
+    angle = position * rotation[...]
+    side = lax.broadcasted_iota(jnp.int32, (256, 128), 1) % HEAD_SIZE < HEAD_SIZE // 2
+    cosine[...] = jnp.cos(angle)
+    angle_sine = jnp.sin(angle)
+    sine[...] = jnp.where(side, -angle_sine, angle_sine)
+    allowed = (segment_row == segment_column) & (lane_id <= row_id) & ((live_row > 0.0) | diagonal)
+    bias[...] = jnp.where(allowed, 0.0, -1e30)
+    for copy in head_loads:
+        copy.wait()
+    start = tokens[...].astype(jnp.float32)
+    inverse = lax.rsqrt(jnp.mean(start * start, axis=1, keepdims=True) + EPSILON)
+    normed[...] = (start * inverse * attn_gain[...]).astype(jnp.bfloat16)
+
+    def project(source, weight):
+        total = jnp.zeros((256, 1024), jnp.float32)
+        for r in range(4):
+            total = total + contract(source[:, pl.ds(r * 256, 256)], weight(r), 1, 0)
+        return total
+
+    made = project(normed, lambda r: partial[0, r // 2, r % 2])
+    for p in range(8):
+        columns = pl.ds(p * 128, 128)
+        query[:, columns] = turn(made[:, p * 128 : p * 128 + 128], cosine[...], sine[...]).astype(jnp.bfloat16)
+    made = project(normed, lambda r: from_sibling[0, r])
+    for p in range(4):
+        columns = pl.ds(p * 128, 128)
+        key_value[:, columns] = turn(made[:, p * 128 : p * 128 + 128], cosine[...], sine[...]).astype(jnp.bfloat16)
+    key_value[:, pl.ds(512, 512)] = made[:, 512:].astype(jnp.bfloat16)
+    for g in range(8):
+        keys[g] = key_value[:, pl.ds(g * 64, 64)]
+        values[g] = key_value[:, pl.ds(512 + g * 64, 64)]
+
+    def attend(g, carry):
+        columns = pl.ds(pl.multiple_of(g * 128, 128), 128)
+        pair = query[:, columns]
+        found = []
+        for r in (0, 1):
+            scores = contract(pair[:, r * 64 : r * 64 + 64], keys[g], 1, 1) * HEAD_SIZE ** (-0.5) + bias[...]
+            weights = jnp.exp(scores - jnp.max(scores, axis=1, keepdims=True))
+            probs = (weights / jnp.sum(weights, axis=1, keepdims=True)).astype(jnp.bfloat16)
+            found.append(contract(probs, values[g], 1, 0))
+        mixed[:, columns] = jnp.concatenate(found, axis=1).astype(jnp.bfloat16)
+        return carry
+
+    lax.fori_loop(0, 8, attend, 0)
+
+    @pl.when(edge)
+    def _():
+        gather(1, z, 1, device(far, x, c, y)).start()
+
+    handle(1, (1,))
+    mid = start + project(mixed, lambda r: partial[1, r // 2, r % 2])
+    middle_out[...] = mid
+    inverse = lax.rsqrt(jnp.mean(mid * mid, axis=1, keepdims=True) + EPSILON)
+    streams[0, z, c] = (mid * inverse * moe_gain[...]).astype(jnp.bfloat16)
+    gather_own(0)
+    rows_store = pltpu.make_async_copy(streams.at[0, z, c], rows_out, load_sem.at[1])
+    rows_store.start()
+    logits = contract(router[...], streams[0, z, c], 1, 1)
+    expert_id = lax.broadcasted_iota(jnp.int32, (16, 256), 0)
+    routed = routes[pl.ds(0, 1), :] == expert_id
+    for n in range(1, TOP):
+        routed = routed | (routes[pl.ds(n, 1), :] == expert_id)
+    logits = jnp.where(routed, logits, -1e30)
+    raised = jnp.where(routed, jnp.exp(logits - jnp.max(logits, axis=0, keepdims=True)), 0.0)
+    soft = raised / jnp.sum(raised, axis=0, keepdims=True)
+    soft_out[...] = soft
+    held_gates = soft * live_row
+    for e in range(16):
+        gates_in[e // 4, e % 2, pl.ds((e // 2) % 2, 1), :] = held_gates[e : e + 1, :]
+    count = jnp.sum(jnp.where(routed, live_row, 0.0), axis=1, keepdims=True)
+    square = lax.broadcasted_iota(jnp.int32, (16, 128), 0) == lax.broadcasted_iota(jnp.int32, (16, 128), 1)
+    counts[...] = jnp.sum(jnp.where(square, count, 0.0), axis=0, keepdims=True)
+    gate_copies = [
+        remote(
+            gates_in.at[a, b], gates.at[z, c], gate_send.at[n], gate_recv.at[z, c], device(a, x, b, y)
+        )
+        for n, (a, b) in enumerate(line)
+    ]
+    for copy in gate_copies:
+        copy.start()
+    gates[z, c] = gates_in[z, c]
+    lax.fori_loop(0, 32, zero, 0)
+
+    @pl.when(edge)
+    def _():
+        gather(0, z, 0, device(near, x, c, y)).wait_send()
+        gather(0, z, 1, device(far, x, c, y)).start()
+
+    handle(1, (0,))
     for a, b in line:
         pltpu.make_async_copy(gates.at[a, b], gates.at[a, b], gate_recv.at[a, b]).wait()
     weights_here(x, 1 - y)
-    row_id = lax.broadcasted_iota(jnp.int32, (256, 256), 0)
-    lane_id = lax.broadcasted_iota(jnp.int32, (256, 256), 1)
 
     def compute(expert, block, core):
-        diagonal = row_id == lane_id
+        diagonal = lax.broadcasted_iota(jnp.int32, (256, 256), 0) == lax.broadcasted_iota(jnp.int32, (256, 256), 1)
         gate_row = gates[block, core, pl.ds(expert, 1), :]
         gate = jnp.sum(jnp.where(diagonal, gate_row, 0.0), axis=1, keepdims=True)
         rows = streams[0, block, core]
@@ -541,12 +661,13 @@
     for a, b in line:
         pltpu.make_async_copy(slopes_in.at[a, b], slopes_in.at[a, b], slope_recv.at[a, b]).wait()
     slope_out[...] = slopes_in[...]
+    gather(1, z, 0, device(near, x, c, y)).wait_send()
+
+    @pl.when(middle)
+    def _():
+        gather(0, z, 0, device(near, x, c, y)).wait_send()
+
     for s in (0, 1):
-
-        @pl.when(middle)
-        def _():
-            gather(s, z, 0, device(near, x, c, y)).wait_send()
-
         gather(s, z, 1, device(far, x, c, y)).wait_send()
         gather(s, z, 2, sibling).wait_send()
         for k in (1, 2, 3):
@@ -564,42 +685,69 @@
         copy.wait_send()
     grad_copy(0, staged_x, returned_x, beside).wait_send()
     grad_copy(1, staged_y, returned_y, across).wait_send()
-    for copy in (*stores, *again_stores):
+    for copy in (rows_store, *stores, *again_stores):
         copy.wait()
 
 
-def expert_part(rows, upstream, gates, gate_w, up_w, down_w):
-    tokens, model_dim = rows.shape
+def expert_part(
+    segment_ids,
+    live_mask,
+    routes,
+    attn_gain,
+    moe_gain,
+    router,
+    tokens,
+    attention_weights,
+    upstream,
+    gate_w,
+    up_w,
+    down_w,
+):
+    count, model_dim = tokens.shape
     width = gate_w.shape[1]
     vmem, anywhere = pl.BlockSpec(memory_space=pltpu.VMEM), pl.BlockSpec(memory_space=pl.ANY)
-    f32, bf16, dma = jnp.float32, jnp.bfloat16, pltpu.SemaphoreType.DMA
-    by_owner = gates.T.reshape(4, 2, 2, tokens).swapaxes(1, 2)
-    by_owner = jnp.pad(by_owner, ((0, 0), (0, 0), (0, 6), (0, 0)))
+    f32, bf16, dma, shape = jnp.float32, jnp.bfloat16, pltpu.SemaphoreType.DMA, jax.ShapeDtypeStruct
+    half = HEAD_SIZE // 2
+    frequency = np.float32(10000.0) ** (-(np.arange(half, dtype=np.float32) * np.float32(2.0)) / np.float32(HEAD_SIZE))
+    rotation = jnp.asarray(np.tile(frequency.astype(np.float32), 4)[None])
+    block = (count, model_dim)
     return pl.pallas_call(
         expert_kernel,
         out_shape=[
-            jax.ShapeDtypeStruct((tokens, model_dim), f32),
-            jax.ShapeDtypeStruct((tokens, model_dim), f32),
-            jax.ShapeDtypeStruct((4, 2, 8, tokens), f32),
-            jax.ShapeDtypeStruct((3, width, model_dim), f32),
-            jax.ShapeDtypeStruct((2, 3, width, model_dim // 2), bf16),
+            shape(block, bf16),
+            shape(block, bf16),
+            shape(block, bf16),
+            shape(block, bf16),
+            shape(block, bf16),
+            shape(block, f32),
+            shape((count, 128), f32),
+            shape((count, 128), f32),
+            shape((count, count), f32),
+            shape((16, count), f32),
+            shape((1, 128), f32),
+            shape(block, f32),
+            shape(block, f32),
+            shape((4, 2, 8, count), f32),
+            shape((3, width, model_dim), f32),
+            shape((2, 3, width, model_dim // 2), bf16),
         ],
-        in_specs=[anywhere, anywhere, vmem, anywhere, anywhere, anywhere],
-        out_specs=[vmem, vmem, vmem, anywhere, anywhere],
+        in_specs=[vmem] * 7 + [anywhere] * 9,
+        out_specs=[anywhere] + [vmem] * 13 + [anywhere] * 2,
         scratch_shapes=[
-            pltpu.VMEM((2, 4, 2, tokens, model_dim), bf16),
-            pltpu.VMEM((4, 2, 8, tokens), f32),
-            pltpu.VMEM((4, 2, 8, tokens), f32),
-            pltpu.VMEM((4, 2, 8, tokens), f32),
+            pltpu.VMEM((8, count, HEAD_SIZE), bf16),
+            pltpu.VMEM((8, count, HEAD_SIZE), bf16),
+            pltpu.VMEM((2, 4, 2, *block), bf16),
+            *[pltpu.VMEM((4, 2, 8, count), f32)] * 4,
             pltpu.VMEM((2, 2, model_dim, width), bf16),
             pltpu.VMEM((2, 2, model_dim, width), bf16),
             pltpu.VMEM((2, 2, width, model_dim), bf16),
             pltpu.VMEM((2, 3, 2, width, model_dim), f32),
-            pltpu.VMEM((2, 4, 2, tokens, model_dim), bf16),
-            pltpu.VMEM((2, 4, tokens, model_dim), bf16),
-            pltpu.VMEM((2, 4, tokens, model_dim), bf16),
+            pltpu.VMEM((2, 4, 2, *block), bf16),
+            pltpu.VMEM((2, 4, *block), bf16),
+            pltpu.VMEM((2, 4, *block), bf16),
             *[pltpu.VMEM((2, 3, width, model_dim // 2), bf16)] * 5,
             dma((6,)),
+            dma((17,)),
             dma((2, 8)),
             dma((2, 4, 2)),
             dma((7,)),
@@ -616,10 +764,26 @@
             dma((2,)),
         ],
         compiler_params=pltpu.CompilerParams(
-            collective_id=1, has_side_effects=True, vmem_limit_bytes=62 << 20
+            collective_id=1, has_side_effects=True, vmem_limit_bytes=63 << 20
         ),
         name="expert_part",
-    )(rows, upstream, by_owner, gate_w, up_w, down_w)
+    )(
+        segment_ids,
+        live_mask,
+        routes.T,
+        rotation,
+        attn_gain[None],
+        moe_gain[None],
+        router.T,
+        tokens,
+        *attention_weights,
+        upstream,
+        gate_w,
+        up_w,
+        down_w,
+    )
+
+
 TAIL_ORDER = (
     (0, 4), (2, 1), (3, 1), (4, 1), (5, 1), (1, 4), (0, 5), (2, 2), (1, 5), (3, 2),
     (4, 2), (5, 2), (0, 6), (2, 3), (1, 6), (3, 3), (4, 3), (2, 4), (5, 3), (3, 4),
@@ -629,20 +793,11 @@
 )
 
 
-def turn(value, cosine, sine):
-    lane = lax.broadcasted_iota(jnp.int32, value.shape, 1) % HEAD_SIZE
-    swapped = jnp.where(
-        lane < HEAD_SIZE // 2, pltpu.roll(value, 128 - HEAD_SIZE // 2, 1), pltpu.roll(value, HEAD_SIZE // 2, 1)
-    )
-    return value * cosine + swapped * sine
-
-
 def tail_kernel(
     tokens,
     normed,
     query,
-    key,
-    value,
+    key_value,
     mixed,
     middle,
     moe_in,
@@ -880,13 +1035,13 @@
 
     inner = upstream_in[...].astype(jnp.float32)
     slope_rows = jnp.concatenate([slopes[e // 4, e % 2, pl.ds((e // 2) % 2, 1), :] for e in range(16)], axis=0)
-    soft_slope = slope_rows * live[...]
+    soft_slope = slope_rows * live[...].astype(jnp.float32)
     soft_t = soft[...]
     dlogits = soft_t * (soft_slope - jnp.sum(soft_t * soft_slope, axis=0, keepdims=True))
     dlogits = dlogits.astype(jnp.bfloat16)
     small_sum[0] = jnp.zeros(small_sum.shape[1:], jnp.float32)
     small_sum[0, pl.ds(0, 16), :] = contract(dlogits, moe_in[...], 1, 0)
-    small_sum[0, pl.ds(18, 1), :] = counts[...]
+    small_sum[0, pl.ds(18, 1), pl.ds(0, 128)] = counts[...]
     dmoe_in = back[...] + contract(dlogits, router[...], 0, 0)
     mid = middle[...]
     output[...] = (mid + combined[...]).astype(jnp.bfloat16)
@@ -912,8 +1067,8 @@
     loads[1].wait()
     mixed_slope[...] = contract(dattn, w_out[...], 1, 1).astype(jnp.bfloat16)
     for g in range(8):
-        keys[g] = key[:, pl.ds(g * 64, 64)]
-        values[g] = value[:, pl.ds(g * 64, 64)]
+        keys[g] = key_value[:, pl.ds(g * 64, 64)]
+        values[g] = key_value[:, pl.ds(512 + g * 64, 64)]
     scale = HEAD_SIZE ** (-0.5)
 
     def group(g, carry):
@@ -1101,96 +1256,62 @@
     experts_all = router.shape[1]
     query_per_key_head = QUERY_HEADS // KEY_VALUE_HEADS
     score_scale = HEAD_SIZE ** (-0.5)
-    special = lax.axis_size("ep") == 16 and lax.axis_size("hs") == 2
-    segment = segment_ids[0]
-    live_row = live_mask[0]
-    inputs = tokens.astype(jnp.float32)
-    normed_rows, inverse_one = rms_forward(inputs, attn_gain)
-    normed_rows_back = normed_rows.astype(jnp.bfloat16)
-    query_pre = jnp.dot(normed_rows_back, w_query, preferred_element_type=jnp.float32).reshape(
-        sequence_length, QUERY_HEADS, HEAD_SIZE
-    )
-    key_before_rotary = jnp.dot(
-        normed_rows_back, key_weight, preferred_element_type=jnp.float32
-    ).reshape(sequence_length, KEY_VALUE_HEADS, HEAD_SIZE)
-    value_b = (
-        jnp.dot(normed_rows_back, value_weight, preferred_element_type=jnp.float32)
-        .astype(jnp.bfloat16)
-        .reshape(sequence_length, KEY_VALUE_HEADS, HEAD_SIZE)
-    )
-    positions = positions_of(segment)
-    cosine_table, sine_table = rotary_tables(positions, HEAD_SIZE)
-    query_back_rows = rotary(query_pre, cosine_table, sine_table).astype(jnp.bfloat16)
-    key_b = rotary(key_before_rotary, cosine_table, sine_table).astype(jnp.bfloat16)
-    indices = jnp.arange(sequence_length)
-    allowed = (
-        (segment[:, None] == segment[None, :])
-        & (indices[None, :] <= indices[:, None])
-        & ((live_row[None, :] > 0) | (indices[None, :] == indices[:, None]))
-    )
-    grouped_rows = query_back_rows.reshape(
-        sequence_length, KEY_VALUE_HEADS, query_per_key_head, HEAD_SIZE
-    )
-    scores = (
-        jnp.einsum("qgrd,kgd->grqk", grouped_rows, key_b, preferred_element_type=jnp.float32)
-        * score_scale
-    )
-    scores = jnp.where(allowed, scores, -1e30)
-    highest = jnp.max(scores, axis=-1, keepdims=True)
-    weights_exp = jnp.exp(scores - highest)
-    denominator = jnp.sum(weights_exp, axis=-1, keepdims=True)
-    log_total = highest + jnp.log(denominator)
-    probabilities = weights_exp / denominator
-    mixed = jnp.einsum(
-        "grqk,kgd->qgrd",
-        probabilities.astype(jnp.bfloat16),
-        value_b,
-        preferred_element_type=jnp.float32,
-    )
-    mixed_b = mixed.reshape(sequence_length, QUERY_HEADS * HEAD_SIZE).astype(jnp.bfloat16)
-    middle = inputs + jnp.dot(mixed_b, w_out, preferred_element_type=jnp.float32)
-    moe_normed, inverse_two = rms_forward(middle, moe_gain)
-    moe_in = moe_normed.astype(jnp.bfloat16)
-    logits = jnp.dot(moe_in, router, preferred_element_type=jnp.float32)
-    route_hot = (routes[:, :, None] == jnp.arange(experts_all)[None, None, :]).astype(jnp.float32)
-    chosen = jnp.sum(route_hot * logits[:, None, :], axis=-1)
-    route_soft = jax.nn.softmax(chosen, axis=-1)
-    live_column = live_row.astype(jnp.float32)[:, None]
-    route_gates = route_soft * live_column
-    counts_local = jnp.sum(route_hot * live_column[:, :, None], axis=(0, 1))
-    dense_gates = jnp.sum(route_hot * route_gates[:, :, None], axis=1)
-    if special:
-        route_soft_dense = jnp.sum(route_hot * route_soft[:, :, None], axis=1)
-        combined, back, slopes, own, again = expert_part(
-            moe_in, cotangent, dense_gates, w_gate[0], w_up[0], w_down[0]
+    if lax.axis_size("ep") == 16 and lax.axis_size("hs") == 2:
+        attention_weights = (w_query, key_weight, value_weight, w_out)
+        (
+            rows,
+            normed_rows,
+            query_rows,
+            key_value,
+            mixed,
+            middle,
+            cosine,
+            sine,
+            bias,
+            soft,
+            counts,
+            combined,
+            back,
+            slopes,
+            own,
+            again,
+        ) = expert_part(
+            segment_ids,
+            live_mask,
+            routes,
+            attn_gain,
+            moe_gain,
+            router,
+            tokens,
+            attention_weights,
+            cotangent,
+            w_gate[0],
+            w_up[0],
+            w_down[0],
         )
-        sign = jnp.concatenate([-sine_table[:, 0], sine_table[:, 0]], axis=1)
         operands = (
             tokens,
-            normed_rows_back,
-            query_back_rows.reshape(sequence_length, -1),
-            key_b.reshape(sequence_length, -1),
-            value_b.reshape(sequence_length, -1),
-            mixed_b,
+            normed_rows,
+            query_rows,
+            key_value,
+            mixed,
             middle,
-            moe_in,
+            rows,
             cotangent,
             combined,
             back,
             slopes,
-            route_soft_dense.T,
-            live_row.astype(jnp.float32)[None],
-            jnp.pad(counts_local, (0, model_dim - experts_all))[None],
+            soft,
+            live_mask,
+            counts,
             router.T,
-            jnp.tile(cosine_table[:, 0], (1, 4)),
-            jnp.tile(sign, (1, 2)),
-            jnp.where(allowed, 0.0, -1e30),
+            cosine,
+            sine,
+            bias,
             attn_gain[None],
             moe_gain[None],
         )
-        output, input_grad, grads, small, tiny, expert_grads = tail_part(
-            operands, (w_query, key_weight, value_weight, w_out), again, own
-        )
+        output, input_grad, grads, small, tiny, expert_grads = tail_part(operands, attention_weights, again, own)
         return (
             output,
             input_grad,
@@ -1204,6 +1325,63 @@
             *[g[None] for g in expert_grads],
             small[18, :experts_all].astype(jnp.int32),
         )
+    segment = segment_ids[0]
+    live_row = live_mask[0]
+    inputs = tokens.astype(jnp.float32)
+    normed_rows, inverse_one = rms_forward(inputs, attn_gain)
+    normed_rows_back = normed_rows.astype(jnp.bfloat16)
+    query_pre = jnp.dot(normed_rows_back, w_query, preferred_element_type=jnp.float32).reshape(
+        sequence_length, QUERY_HEADS, HEAD_SIZE
+    )
+    key_before_rotary = jnp.dot(
+        normed_rows_back, key_weight, preferred_element_type=jnp.float32
+    ).reshape(sequence_length, KEY_VALUE_HEADS, HEAD_SIZE)
+    value_b = (
+        jnp.dot(normed_rows_back, value_weight, preferred_element_type=jnp.float32)
+        .astype(jnp.bfloat16)
+        .reshape(sequence_length, KEY_VALUE_HEADS, HEAD_SIZE)
+    )
+    positions = positions_of(segment)
+    cosine_table, sine_table = rotary_tables(positions, HEAD_SIZE)
+    query_back_rows = rotary(query_pre, cosine_table, sine_table).astype(jnp.bfloat16)
+    key_b = rotary(key_before_rotary, cosine_table, sine_table).astype(jnp.bfloat16)
+    indices = jnp.arange(sequence_length)
+    allowed = (
+        (segment[:, None] == segment[None, :])
+        & (indices[None, :] <= indices[:, None])
+        & ((live_row[None, :] > 0) | (indices[None, :] == indices[:, None]))
+    )
+    grouped_rows = query_back_rows.reshape(
+        sequence_length, KEY_VALUE_HEADS, query_per_key_head, HEAD_SIZE
+    )
+    scores = (
+        jnp.einsum("qgrd,kgd->grqk", grouped_rows, key_b, preferred_element_type=jnp.float32)
+        * score_scale
+    )
+    scores = jnp.where(allowed, scores, -1e30)
+    highest = jnp.max(scores, axis=-1, keepdims=True)
+    weights_exp = jnp.exp(scores - highest)
+    denominator = jnp.sum(weights_exp, axis=-1, keepdims=True)
+    log_total = highest + jnp.log(denominator)
+    probabilities = weights_exp / denominator
+    mixed = jnp.einsum(
+        "grqk,kgd->qgrd",
+        probabilities.astype(jnp.bfloat16),
+        value_b,
+        preferred_element_type=jnp.float32,
+    )
+    mixed_b = mixed.reshape(sequence_length, QUERY_HEADS * HEAD_SIZE).astype(jnp.bfloat16)
+    middle = inputs + jnp.dot(mixed_b, w_out, preferred_element_type=jnp.float32)
+    moe_normed, inverse_two = rms_forward(middle, moe_gain)
+    moe_in = moe_normed.astype(jnp.bfloat16)
+    logits = jnp.dot(moe_in, router, preferred_element_type=jnp.float32)
+    route_hot = (routes[:, :, None] == jnp.arange(experts_all)[None, None, :]).astype(jnp.float32)
+    chosen = jnp.sum(route_hot * logits[:, None, :], axis=-1)
+    route_soft = jax.nn.softmax(chosen, axis=-1)
+    live_column = live_row.astype(jnp.float32)[:, None]
+    route_gates = route_soft * live_column
+    counts_local = jnp.sum(route_hot * live_column[:, :, None], axis=(0, 1))
+    dense_gates = jnp.sum(route_hot * route_gates[:, :, None], axis=1)
     upstream_all = lax.all_gather(cotangent, "ep", axis=0, tiled=True)
     gate_all = lax.all_gather(w_gate, "hs", axis=0, tiled=True)
     up_all = lax.all_gather(w_up, "hs", axis=0, tiled=True)

time: 320 us -> 299 us (0.934)
  other arithmetic: 20.7 us -> 10.2 us
  matrix products: 8.42 us -> 0 us
  local copies, waits for them, and re-layouts: 15.8 us -> 8.12 us
  Pallas kernels: 274 us -> 279 us
    pallas_call x1, Pallas kernels: 159 us -> 175 us  [expert_part(): pl.pallas_call(expert_kernel, out_shape=[shape(block, bf16), shape(block,...]
    pallas_call x1, Pallas kernels: 115 us -> 104 us  [tail_part(): pl.pallas_call(tail_kernel, out_shape=[shape((tokens, model_dim), bf16),...]
    dot_general x7 -> x0, matrix products: 8.42 us -> none  [the longest x1 2.41 us: local(): jnp.dot(mixed_b, w_out, preferred_element_type=jnp.float32)]
    convert_element_type x4 -> x0, local copies, waits for them, and re-layouts: 4.64 us -> none  [the longest x1 1.79 us: local(): rotary(key_before_rotary, cosine_table, sine_table).astype(jnp.bfloat16)]
where the time goes in v6:
time: 299 us; the launch traced here: 298 us
  Pallas kernels  279 us (93%)
  other arithmetic  10.2 us (3%)
  local copies, waits for them, and re-layouts  8.12 us (3%)
    pallas_call x1, Pallas kernels, expert_part(): pl.pallas_call(expert_kernel, out_shape=[shape(block, bf16), shape(block,...  175 us
    pallas_call x1, Pallas kernels, tail_part(): pl.pallas_call(tail_kernel, out_shape=[shape((tokens, model_dim), bf16),...  104 us
    convert_element_type x2, other arithmetic, tail_part(): grads = [o.reshape(-1, o.shape[2]).astype(jnp.float32) for o in out[2:6]]  9.02 us

profile of v6, /device:TPU:0, one launch (start us, length us, event | category | flops | bytes accessed | tf_op | source)
XLA Modules:
  0.0 298.1 jit_solution(2444213756964875330)
XLA Ops:
  0.6 175.4 %expert_part.1 = (bf16[256,1024]{1,0:T(8,128)(2,1)}, bf16[256,1024]{1,0:T(8,128)(2,1)}, bf16[256,1024]{1,0:T(8,128)(2,1)}, bf16[256,1024]{1,0:T(8,128)(2,1)}, bf...) custom-call(s32[1,256]{1,0:T(1,128)} %segment.1, ...), custom_call_target="tpu_custom_call" | custom-call | tf_op jit(solution)/shard_map/expert_part/pallas_call | solution.py:714
  176.0 103.7 %tail_part.1 = (bf16[256,1024]{1,0:T(8,128)(2,1)}, f32[256,1024]{1,0:T(8,128)}, bf16[64,16,1024]{2,1,0:T(8,128)(2,1)}, bf16[64,16,1024]{2,1,0:T(8,128)(2,1)}, bf...) custom-call(bf16[256,1024]{1,0:T(8,128)(2,1)} %tokens.1, ...), custom_call_target="tpu_custom_call" | custom-call | tf_op jit(solution)/shard_map/tail_part/pallas_call | solution.py:1189
  279.7 1.2 convert_bitcast_fusion
  280.9 1.4 slice.9
  282.3 1.5 slice_bitcast_fusion
  283.8 0.0 copy-start
  283.8 0.0 copy-start.1
  283.8 4.3 %bitcast_convert_fusion.2 = (f32[1024,512]{1,0:T(8,128)}, f32[1024,512]{1,0:T(8,128)}) fusion(bf16[64,16,512]{2,1,0:T(8,128)(2,1)} %get-tuple-element.61, bf16[64,16,512]{2,1,0:T(8,128)(2,1)} %get-tuple-element.60), kind=kLoop, calls=%fused_computation.2 | loop fusion | flops 1048576 | bytes 6291456 | tf_op jit(solution)/shard_map/convert_element_type | solution.py:1233
  288.1 0.0 copy-done
  288.1 0.0 copy-done.1
  288.1 0.0 copy-start.6
  288.1 0.0 copy-start.5
  288.1 4.7 %bitcast_convert_fusion = (f32[1024,1024]{1,0:T(8,128)}, f32[1024,1024]{1,0:T(8,128)}) fusion(bf16[64,16,1024]{2,1,0:T(8,128)(2,1)S(1)} %copy-done, bf16[64,16,1024]{2,1,0:T(8,128)(2,1)S(1)} %copy-done.1), kind=kLoop, calls=%fused_computation | loop fusion | flops 2097152 | bytes 12582912 | tf_op jit(solution)/shard_map/convert_element_type | solution.py:1233
  292.8 0.0 copy-start.7
  292.8 0.0 copy-start.4
  292.8 0.0 copy-done.6
  292.8 0.8 copy.35
  293.6 0.0 copy-done.5
  293.6 0.0 copy-start.3
  293.6 1.0 copy.36
  294.6 0.0 copy-done.7
  294.6 0.6 copy.37
  295.2 0.0 copy-done.4
  295.2 0.0 copy-start.2
  295.2 1.0 copy.38
  296.1 0.0 copy-done.3
  296.1 1.0 copy.39
  297.1 0.0 copy-done.2
  297.1 1.0 copy.40
Async XLA Ops:
  283.8 4.3 %copy-start = (bf16[64,16,1024]{2,1,0:T(8,128)(2,1)S(1)}, bf16[64,16,1024]{2,1,0:T(8,128)(2,1)}, u32[]{:S(2)}) copy-start(bf16[64,16,1024]{2,1,0:T(8,128)(2,1)} %get-tuple-element.62) | copy-start | bytes 6291460
  283.8 4.3 %copy-start.1 = (bf16[64,16,1024]{2,1,0:T(8,128)(2,1)S(1)}, bf16[64,16,1024]{2,1,0:T(8,128)(2,1)}, u32[]{:S(2)}) copy-start(bf16[64,16,1024]{2,1,0:T(8,128)(2,1)} %get-tuple-element.59) | copy-start | bytes 6291460
  288.1 4.7 %copy-start.6 = (bf16[256,1024]{1,0:T(8,128)(2,1)S(1)}, bf16[256,1024]{1,0:T(8,128)(2,1)}, u32[]{:S(2)}) copy-start(bf16[256,1024]{1,0:T(8,128)(2,1)} %get-tuple-element.84) | copy-start | bytes 1572868
  288.1 5.5 %copy-start.5 = (f32[256,1024]{1,0:T(8,128)S(1)}, f32[256,1024]{1,0:T(8,128)}, u32[]{:S(2)}) copy-start(f32[256,1024]{1,0:T(8,128)} %get-tuple-element.85) | copy-start | bytes 3145732
  292.8 1.8 copy-start.7
  292.8 2.4 copy-start.4
  293.6 2.5 copy-start.3
  295.2 1.9 copy-start.2

commit v7 on v6

--- a/solution.py
+++ b/solution.py
@@ -171,22 +171,25 @@
     gate_w,
     up_w,
     down_w,
-    rows_out,
+    middle_rows,
+    input_grad,
+    out_grad,
+    query_grad,
+    side_grad,
+    small,
+    tiny,
+    own_out,
+    again_out,
+    weighted_out,
     normed,
     query,
     key_value,
     mixed,
-    middle_out,
+    back,
     cosine,
     sine,
     bias,
-    soft_out,
-    counts,
-    weighted_out,
-    back_out,
-    slope_out,
-    own_out,
-    again_out,
+    soft_rows,
     keys,
     values,
     streams,
@@ -208,6 +211,8 @@
     returned_y,
     load_sem,
     head_sem,
+    store_sem,
+    weighted_sem,
     gather_send,
     gather_recv,
     gate_send,
@@ -381,12 +386,10 @@
 
     handle(1, (1,))
     mid = start + project(mixed, lambda r: partial[1, r // 2, r % 2])
-    middle_out[...] = mid
+    middle_rows[...] = mid
     inverse = lax.rsqrt(jnp.mean(mid * mid, axis=1, keepdims=True) + EPSILON)
     streams[0, z, c] = (mid * inverse * moe_gain[...]).astype(jnp.bfloat16)
     gather_own(0)
-    rows_store = pltpu.make_async_copy(streams.at[0, z, c], rows_out, load_sem.at[1])
-    rows_store.start()
     logits = contract(router[...], streams[0, z, c], 1, 1)
     expert_id = lax.broadcasted_iota(jnp.int32, (16, 256), 0)
     routed = routes[pl.ds(0, 1), :] == expert_id
@@ -395,13 +398,14 @@
     logits = jnp.where(routed, logits, -1e30)
     raised = jnp.where(routed, jnp.exp(logits - jnp.max(logits, axis=0, keepdims=True)), 0.0)
     soft = raised / jnp.sum(raised, axis=0, keepdims=True)
-    soft_out[...] = soft
+    soft_rows[...] = soft
     held_gates = soft * live_row
     for e in range(16):
         gates_in[e // 4, e % 2, pl.ds((e // 2) % 2, 1), :] = held_gates[e : e + 1, :]
     count = jnp.sum(jnp.where(routed, live_row, 0.0), axis=1, keepdims=True)
     square = lax.broadcasted_iota(jnp.int32, (16, 128), 0) == lax.broadcasted_iota(jnp.int32, (16, 128), 1)
-    counts[...] = jnp.sum(jnp.where(square, count, 0.0), axis=0, keepdims=True)
+    small[...] = jnp.zeros((24, 1024), jnp.float32)
+    small[pl.ds(18, 1), pl.ds(0, 128)] = jnp.sum(jnp.where(square, count, 0.0), axis=0, keepdims=True)
     gate_copies = [
         remote(
             gates_in.at[a, b], gates.at[z, c], gate_send.at[n], gate_recv.at[z, c], device(a, x, b, y)
@@ -534,31 +538,31 @@
             for s in (0, 1):
                 pair_copy(s, block).start()
 
-        @pl.when((i % 2 == 1) & (again == 1) & (k > 0))
+        @pl.when((i % 2 == 1) & (again == 1))
         def _():
             for s in (0, 1):
                 pair_copy(s, block).wait_recv()
                 add_to(s, block, from_sibling.at[s, block])
 
-                @pl.when(edge & (k == 2))
-                def _():
-                    line_copy(s, block, 3, near).start()
-
-                @pl.when(edge & (k == 1))
-                def _():
-                    line_copy(s, block, 1, near).start()
-
-                @pl.when(edge & (k == 3))
-                def _():
-                    line_copy(s, block, 2, last).start()
-
-                @pl.when(middle & (k == 3))
-                def _():
-                    line_copy(s, block, 1, last).start()
-
-                @pl.when(middle & (k == 2))
-                def _():
-                    line_copy(s, block, 0, far).start()
+            @pl.when(edge & (k == 2))
+            def _():
+                line_copy(0, block, 2, near).start()
+
+            @pl.when(edge & (k == 1))
+            def _():
+                line_copy(0, block, 1, near).start()
+
+            @pl.when(edge & (k == 3))
+            def _():
+                line_copy(0, block, 2, last).start()
+
+            @pl.when(middle & (k == 3))
+            def _():
+                line_copy(0, block, 1, last).start()
+
+            @pl.when(middle & (k == 2))
+            def _():
+                line_copy(0, block, 0, far).start()
 
         return carry
 
@@ -596,71 +600,19 @@
         copy.start()
     slopes_in[z, c] = slopes[z, c]
 
+
+    weighted_stores = [
+        pltpu.make_async_copy(partial.at[1, k, c], weighted_out.at[k], weighted_sem.at[k]) for k in range(4)
+    ]
+    for copy in weighted_stores:
+        copy.start()
+
     @pl.when(middle)
     def _():
-        for s in (0, 1):
-            line_wait(s, 3)
-            add_to(s, near, from_line.at[s, 3])
-            line_copy(s, near, 0, near).start()
-
-    grad_copy(0, staged_x, returned_x, beside).wait_recv()
-
-    def second_low(a, at):
-        value = sums[x, a, 1 - y, at, low] + returned_x[1 - y, a, at, :].astype(jnp.float32)
-        staged_again[0, a, at, :] = value.astype(jnp.bfloat16)
-
-    each(second_low)
-    again_stores = [pltpu.make_async_copy(staged_again.at[0], again_out.at[0], load_sem.at[3])]
-    again_stores[0].start()
-    grad_copy(1, staged_y, returned_y, across).wait_recv()
-
-    def second_high(a, at):
-        value = sums[1 - x, a, y, at, high] + returned_y[0, a, at, :].astype(jnp.float32)
-        staged_again[1, a, at, :] = value.astype(jnp.bfloat16)
-
-    each(second_high)
-    again_stores.append(pltpu.make_async_copy(staged_again.at[1], again_out.at[1], load_sem.at[4]))
-    again_stores[1].start()
-
-    def own_grad(a, at):
-        sums[x, a, y, at, low] += returned_x[y, a, at, :].astype(jnp.float32)
-        sums[x, a, y, at, high] += returned_y[1, a, at, :].astype(jnp.float32)
-
-    each(own_grad)
-    stores = [pltpu.make_async_copy(sums.at[x, a, y], own_out.at[a], load_sem.at[a]) for a in range(3)]
-    for copy in stores:
-        copy.start()
-
-    def finish(slots):
-        for s in (0, 1):
-            for slot in slots:
-                line_wait(s, slot)
-
-            def body(u, carry):
-                at = pl.ds(pl.multiple_of(u * 32, 32), 32)
-                value = partial[s, z, c, at, :].astype(jnp.float32)
-                value = value + from_sibling[s, z, at, :].astype(jnp.float32)
-                for slot in slots:
-                    value = value + from_line[s, slot, at, :].astype(jnp.float32)
-                (back_out, weighted_out)[s][at, :] = value
-                return carry
-
-            lax.fori_loop(0, 8, body, 0)
-
-    for s in (0, 1):
-        pair_copy(s, z).wait_recv()
-
-    @pl.when(middle)
-    def _():
-        finish((0, 1))
-
-    @pl.when(edge)
-    def _():
-        finish((0, 1, 2))
-
-    for a, b in line:
-        pltpu.make_async_copy(slopes_in.at[a, b], slopes_in.at[a, b], slope_recv.at[a, b]).wait()
-    slope_out[...] = slopes_in[...]
+        line_wait(0, 2)
+        add_to(0, near, from_line.at[0, 2])
+        line_copy(0, near, 0, near).start()
+
     gather(1, z, 0, device(near, x, c, y)).wait_send()
 
     @pl.when(middle)
@@ -672,20 +624,187 @@
         gather(s, z, 2, sibling).wait_send()
         for k in (1, 2, 3):
             gather(s, chip(k), 4 + k, sibling).wait_send()
-            line_copy(s, chip(k), 0, near).wait_send()
 
         @pl.when(middle)
         def _():
             for k in (1, 3):
                 gather(s, chip(k), 2 + (k + 1) // 2, device(far, x, c, y)).wait_send()
 
+    for copy in (*gate_copies, *weight_copies):
+        copy.wait_send()
+
+    def query_weight(r):
+        return streams.at[0, chip(1 + r // 2), r % 2]
+
+    reloads = []
+    for r in range(4):
+        rows = pl.ds(r * 256, 256)
+        for n, (source, target) in enumerate(
+            (
+                (w_out_in, from_sibling.at[1, r]),
+                (w_query_in, query_weight(r)),
+                (w_key_in, from_sibling.at[0, r, :, pl.ds(0, 512)]),
+                (w_value_in, from_sibling.at[0, r, :, pl.ds(512, 512)]),
+            )
+        ):
+            reloads.append(pltpu.make_async_copy(source.at[rows, :], target, head_sem.at[1 + r * 4 + n]))
+    for copy in reloads:
+        copy.start()
+
+    def combined(s, slots, body_of):
+        for slot in slots:
+            line_wait(s, slot)
+
+        def body(u, carry):
+            at = pl.ds(pl.multiple_of(u * 32, 32), 32)
+            value = partial[s, z, c, at, :].astype(jnp.float32)
+            for slot in slots:
+                value = value + from_line[s, slot, at, :].astype(jnp.float32)
+            body_of(at, value)
+            return carry
+
+        lax.fori_loop(0, 8, body, 0)
+
+    def finish(s, body_of):
+        @pl.when(middle)
+        def _():
+            combined(s, (0, 1), body_of)
+
+        @pl.when(edge)
+        def _():
+            combined(s, (0, 1, 2), body_of)
+
+    def store_back(at, value):
+        back[at, :] = value
+
+    finish(0, store_back)
+    for a, b in line:
+        pltpu.make_async_copy(slopes_in.at[a, b], slopes_in.at[a, b], slope_recv.at[a, b]).wait()
+    upstream = streams[1, z, c].astype(jnp.float32)
+    slope_rows = jnp.concatenate([slopes_in[e // 4, e % 2, pl.ds((e // 2) % 2, 1), :] for e in range(16)], axis=0)
+    soft_slope = slope_rows * live[...].astype(jnp.float32)
+    soft_t = soft_rows[...]
+    dlogits = soft_t * (soft_slope - jnp.sum(soft_t * soft_slope, axis=0, keepdims=True))
+    dlogits = dlogits.astype(jnp.bfloat16)
+    small[pl.ds(0, 16), :] = contract(dlogits, streams[0, z, c], 1, 0)
+    dmoe_in = back[...] + contract(dlogits, router[...], 0, 0)
+    mid = middle_rows[...]
+    inverse = lax.rsqrt(jnp.mean(mid * mid, axis=1, keepdims=True) + EPSILON)
+    small[pl.ds(17, 1), :] = jnp.sum(dmoe_in * mid * inverse, axis=0, keepdims=True)
+    scaled = dmoe_in * moe_gain[...]
+    dmiddle = upstream + inverse * (
+        scaled - mid * inverse * inverse * jnp.mean(scaled * mid, axis=1, keepdims=True)
+    )
+    input_grad[...] = dmiddle
+    dattn = dmiddle.astype(jnp.bfloat16)
+    outgoing = []
+
+    def send_out(source, target):
+        copy = pltpu.make_async_copy(source, target, store_sem.at[len(outgoing)])
+        copy.start()
+        outgoing.append(copy)
+
+    def column_grad(left, right, held, target):
+        for r in range(4):
+            rows = contract(left[:, pl.ds(r * 256, 256)], right, 0, 0).astype(jnp.bfloat16)
+            for n in range(4):
+                held[n // 2, n % 2, pl.ds(r * 256, 256), :] = rows[:, n * 256 : n * 256 + 256]
+        for n in range(4):
+            send_out(held.at[n // 2, n % 2], target.at[:, pl.ds(n * 256, 256)])
+
+    column_grad(mixed, dattn, w_gate, out_grad)
+    for copy in reloads:
+        copy.wait()
+    mixed_slope, query_slope, side_slope = w_down.at[0, 0], w_down.at[0, 1], w_down.at[1, 0]
+    for r in range(4):
+        mixed_slope[:, pl.ds(r * 256, 256)] = contract(dattn, from_sibling[1, r], 1, 1).astype(jnp.bfloat16)
+    scale = HEAD_SIZE ** (-0.5)
+
+    def attend_back(p, carry):
+        wide = pl.ds(pl.multiple_of(p * 256, 256), 256)
+        queries, slopes_here = query[:, wide], mixed_slope[:, wide]
+        key_slopes, value_slopes, query_slopes = [], [], []
+        for n in (0, 1):
+            key_g, value_g = keys[2 * p + n], values[2 * p + n]
+            key_slope = jnp.zeros((256, 64), jnp.float32)
+            value_slope = jnp.zeros((256, 64), jnp.float32)
+            for r in (0, 1):
+                cut = slice(n * 128 + r * 64, n * 128 + r * 64 + 64)
+                query_h, slope_h = queries[:, cut], slopes_here[:, cut]
+                scores = contract(query_h, key_g, 1, 1) * scale + bias[...]
+                weights = jnp.exp(scores - jnp.max(scores, axis=1, keepdims=True))
+                probs = weights / jnp.sum(weights, axis=1, keepdims=True)
+                prob_slope = contract(slope_h, value_g, 1, 1)
+                value_slope = value_slope + contract(probs.astype(jnp.bfloat16), slope_h, 0, 0)
+                delta = jnp.sum(probs * prob_slope, axis=1, keepdims=True)
+                score_slope = (probs * (prob_slope - delta)).astype(jnp.bfloat16)
+                query_slopes.append(contract(score_slope, key_g, 1, 0) * scale)
+                key_slope = key_slope + contract(score_slope, query_h, 0, 0) * scale
+            key_slopes.append(key_slope)
+            value_slopes.append(value_slope)
+        for n in (0, 1):
+            pair = turn(jnp.concatenate(query_slopes[2 * n : 2 * n + 2], axis=1), cosine[...], -sine[...])
+            query_slope[:, pl.ds(pl.multiple_of(p * 256 + n * 128, 128), 128)] = pair.astype(jnp.bfloat16)
+        pair = turn(jnp.concatenate(key_slopes, axis=1), cosine[...], -sine[...])
+        side_slope[:, pl.ds(pl.multiple_of(p * 128, 128), 128)] = pair.astype(jnp.bfloat16)
+        pair = jnp.concatenate(value_slopes, axis=1)
+        side_slope[:, pl.ds(pl.multiple_of(512 + p * 128, 128), 128)] = pair.astype(jnp.bfloat16)
+        return carry
+
+    lax.fori_loop(0, 4, attend_back, 0)
+
+    column_grad(normed, query_slope[...], w_up, query_grad)
+    for r in range(4):
+        rows = contract(normed[:, pl.ds(r * 256, 256)], side_slope[...], 0, 0).astype(jnp.bfloat16)
+        streams[1, chip(1 + r // 2), r % 2] = rows
+        send_out(streams.at[1, chip(1 + r // 2), r % 2], side_grad.at[pl.ds(r * 256, 256), :])
+    dnormed = jnp.concatenate(
+        [
+            contract(query_slope[...], query_weight(r)[...], 1, 1)
+            + contract(side_slope[...], from_sibling[0, r], 1, 1)
+            for r in range(4)
+        ],
+        axis=1,
+    )
+    tokens_again = pltpu.make_async_copy(tokens_in, w_down.at[1, 1], head_sem.at[0])
+    tokens_again.start()
+    tokens_again.wait()
+    start = w_down[1, 1].astype(jnp.float32)
+    inverse = lax.rsqrt(jnp.mean(start * start, axis=1, keepdims=True) + EPSILON)
+    gain_slope = jnp.sum(dnormed * start * inverse, axis=0, keepdims=True)
+    for r in range(8):
+        tiny[pl.ds(r, 1), :] = gain_slope[:, r * 128 : r * 128 + 128]
+    scaled = dnormed * attn_gain[...]
+    input_grad[...] += inverse * (
+        scaled - start * inverse * inverse * jnp.mean(scaled * start, axis=1, keepdims=True)
+    )
+
+    grad_copy(0, staged_x, returned_x, beside).wait_recv()
+    grad_copy(1, staged_y, returned_y, across).wait_recv()
+
+    def stage_again(a, at):
+        value = sums[x, a, 1 - y, at, low] + returned_x[1 - y, a, at, :].astype(jnp.float32)
+        staged_again[0, a, at, :] = value.astype(jnp.bfloat16)
+        value = sums[1 - x, a, y, at, high] + returned_y[0, a, at, :].astype(jnp.float32)
+        staged_again[1, a, at, :] = value.astype(jnp.bfloat16)
+        sums[x, a, y, at, low] += returned_x[y, a, at, :].astype(jnp.float32)
+        sums[x, a, y, at, high] += returned_y[1, a, at, :].astype(jnp.float32)
+
+    each(stage_again)
+    send_out(staged_again, again_out)
+    for a in range(3):
+        send_out(sums.at[x, a, y], own_out.at[a])
+
+    for k in (1, 2, 3):
+        line_copy(0, chip(k), 0, near).wait_send()
+    for s in (0, 1):
         for k in range(4):
             pair_copy(s, chip(k)).wait_send()
-    for copy in (*gate_copies, *weight_copies, *slope_copies):
+    for copy in slope_copies:
         copy.wait_send()
     grad_copy(0, staged_x, returned_x, beside).wait_send()
     grad_copy(1, staged_y, returned_y, across).wait_send()
-    for copy in (rows_store, *stores, *again_stores):
+    for copy in (*outgoing, *weighted_stores):
         copy.wait()
 
 
@@ -714,26 +833,25 @@
     return pl.pallas_call(
         expert_kernel,
         out_shape=[
-            shape(block, bf16),
-            shape(block, bf16),
-            shape(block, bf16),
-            shape(block, bf16),
-            shape(block, bf16),
-            shape(block, f32),
-            shape((count, 128), f32),
-            shape((count, 128), f32),
-            shape((count, count), f32),
-            shape((16, count), f32),
-            shape((1, 128), f32),
             shape(block, f32),
             shape(block, f32),
-            shape((4, 2, 8, count), f32),
+            shape((model_dim, model_dim), bf16),
+            shape((model_dim, model_dim), bf16),
+            shape((model_dim, model_dim), bf16),
+            shape((24, model_dim), f32),
+            shape((8, 128), f32),
             shape((3, width, model_dim), f32),
             shape((2, 3, width, model_dim // 2), bf16),
+            shape((4, *block), bf16),
         ],
         in_specs=[vmem] * 7 + [anywhere] * 9,
-        out_specs=[anywhere] + [vmem] * 13 + [anywhere] * 2,
+        out_specs=[vmem] * 2 + [anywhere] * 3 + [vmem] * 2 + [anywhere] * 3,
         scratch_shapes=[
+            *[pltpu.VMEM(block, bf16)] * 4,
+            pltpu.VMEM(block, f32),
+            *[pltpu.VMEM((count, 128), f32)] * 2,
+            pltpu.VMEM((count, count), f32),
+            pltpu.VMEM((16, count), f32),
             pltpu.VMEM((8, count, HEAD_SIZE), bf16),
             pltpu.VMEM((8, count, HEAD_SIZE), bf16),
             pltpu.VMEM((2, 4, 2, *block), bf16),
@@ -744,10 +862,12 @@
             pltpu.VMEM((2, 3, 2, width, model_dim), f32),
             pltpu.VMEM((2, 4, 2, *block), bf16),
             pltpu.VMEM((2, 4, *block), bf16),
-            pltpu.VMEM((2, 4, *block), bf16),
+            pltpu.VMEM((1, 3, *block), bf16),
             *[pltpu.VMEM((2, 3, width, model_dim // 2), bf16)] * 5,
             dma((6,)),
             dma((17,)),
+            dma((16,)),
+            dma((4,)),
             dma((2, 8)),
             dma((2, 4, 2)),
             dma((7,)),
@@ -784,106 +904,108 @@
     )
 
 
-TAIL_ORDER = (
-    (0, 4), (2, 1), (3, 1), (4, 1), (5, 1), (1, 4), (0, 5), (2, 2), (1, 5), (3, 2),
-    (4, 2), (5, 2), (0, 6), (2, 3), (1, 6), (3, 3), (4, 3), (2, 4), (5, 3), (3, 4),
-    (0, 7), (4, 4), (0, 8), (1, 7), (2, 5), (1, 8), (5, 4), (2, 6), (3, 5), (2, 7),
-    (4, 5), (3, 6), (2, 8), (5, 5), (4, 6), (3, 7), (5, 6), (3, 8), (4, 7), (4, 8),
-    (5, 7), (5, 8),
-)
-
-
-def tail_kernel(
-    tokens,
-    normed,
-    query,
-    key_value,
-    mixed,
-    middle,
-    moe_in,
-    upstream_in,
-    combined,
-    back,
-    slopes,
-    soft,
-    live,
-    counts,
-    router,
-    cosine,
-    sine,
-    bias,
-    attn_gain,
-    moe_gain,
-    w_query_in,
-    w_key_in,
-    w_value_in,
-    w_out_in,
+AGAIN_AT = (0, 4, 8)
+COMBINE_AT = 6
+SMALL_AT = 9
+
+
+def sum_kernel(
+    small,
+    tiny,
+    out_in,
+    query_in,
+    side_in,
     again_in,
     own_in,
+    weighted_in,
+    middle_rows,
     output,
-    input_grad,
     out_sum,
     query_sum,
-    key_sum,
-    value_sum,
+    side_sum,
     small_out,
     tiny_out,
     gate_grad,
     up_grad,
     down_grad,
-    w_query,
-    w_key,
-    w_value,
-    w_out,
-    keys,
-    values,
-    key_slopes,
-    value_slopes,
-    mixed_slope,
-    query_slope,
     again,
     returned_again,
     own,
+    weighted,
+    from_line,
     *rest,
 ):
     count = 6
     grads, halves, totals, fulls, firsts, seconds, lines = [rest[n * count : (n + 1) * count] for n in range(7)]
-    small_sum, small_in, tiny_sum, tiny_in, send, recv, small_send, small_recv, local_sem, load_sem, again_send, again_recv = rest[7 * count :]
-    outs = [ref.at[:, :, pl.ds(n * 512, 512)] for ref in (out_sum, query_sum) for n in (0, 1)]
-    outs += [key_sum, value_sum]
+    small_sum, small_in, tiny_sum, tiny_in, send, recv, small_send, small_recv, local_sem, load_sem, again_send, again_recv, line_send, line_recv = rest[7 * count :]
+    windows = [(ref, pl.ds(n * 512, 512)) for ref in range(3) for n in (0, 1)]
+    outs = [(out_sum, query_sum, side_sum)[ref].at[:, :, columns] for ref, columns in windows]
     z, x, c, y = place()
     sibling, beside, across = device(z, x, 1 - c, y), device(z, 1 - x, c, y), device(z, x, c, 1 - y)
     along = [device((z + k) % 4, x, c, y) for k in (1, 2, 3)]
     loads = [
-        pltpu.make_async_copy(source, target, load_sem.at[n])
-        for n, (source, target) in enumerate(
-            (
-                (again_in, again),
-                (w_out_in, w_out),
-                (w_query_in, w_query),
-                (w_key_in, w_key),
-                (w_value_in, w_value),
-                (own_in, own),
-            )
-        )
+        pltpu.make_async_copy((out_in, query_in, side_in)[ref].at[:, :, columns], grads[i], load_sem.at[i])
+        for i, (ref, columns) in enumerate(windows)
     ]
+    loads.append(pltpu.make_async_copy(again_in, again, load_sem.at[6]))
+    loads.append(pltpu.make_async_copy(own_in, own, load_sem.at[7]))
+    loads.append(pltpu.make_async_copy(weighted_in, weighted, load_sem.at[8]))
     for copy in loads:
         copy.start()
+    small_sum[0] = small[...]
+    tiny_sum[0] = tiny[...]
     greet([sibling, beside, across] + along)
-    loads[0].wait()
     again_copies = [
         pltpu.make_async_remote_copy(
-            src_ref=again.at[n],
-            dst_ref=returned_again.at[n],
-            send_sem=again_send.at[n],
-            recv_sem=again_recv.at[n],
+            src_ref=again.at[n, a],
+            dst_ref=returned_again.at[n, a],
+            send_sem=again_send.at[n, a],
+            recv_sem=again_recv.at[n, a],
             device_id=peer,
             device_id_type=MESH,
         )
+        for a in range(3)
         for n, peer in enumerate((across, beside))
     ]
-    for copy in again_copies:
-        copy.start()
+    near, far, last = 1 + z % 2, (2 + 3 * z) % 5, 3 - 3 * (z // 2)
+    middle, edge = (z == 1) | (z == 2), (z == 0) | (z == 3)
+
+    def line_copy(block, piece, slot, peer):
+        rows = pl.ds(piece * 64, 64)
+        return pltpu.make_async_remote_copy(
+            src_ref=weighted.at[block, rows, :],
+            dst_ref=from_line.at[slot, rows, :],
+            send_sem=line_send.at[block, piece],
+            recv_sem=line_recv.at[slot, piece],
+            device_id=device(peer, x, c, y),
+            device_id_type=MESH,
+        )
+
+    def line_wait(slot, piece):
+        part = from_line.at[slot, pl.ds(piece * 64, 64), :]
+        pltpu.make_async_copy(part, part, line_recv.at[slot, piece]).wait()
+
+    def line_stage(tick):
+        @pl.when(edge)
+        def _():
+            for block, slot, peer, first in ((far, 2, near, 0), (near, 1, near, 4), (last, 2, last, 4)):
+                if 0 <= tick - first < 4:
+                    line_copy(block, tick - first, slot, peer).start()
+
+        @pl.when(middle)
+        def _():
+            for block, slot, peer, first in ((last, 1, last, 0), (far, 0, far, 1)):
+                if 0 <= tick - first < 4:
+                    line_copy(block, tick - first, slot, peer).start()
+            if 0 <= tick - COMBINE_AT < 4:
+                piece = tick - COMBINE_AT
+                line_wait(2, piece)
+                for r in (0, 32):
+                    at = pl.ds(piece * 64 + r, 32)
+                    value = weighted[near, at, :].astype(jnp.float32) + from_line[2, at, :].astype(jnp.float32)
+                    weighted[near, at, :] = value.astype(jnp.bfloat16)
+                line_copy(near, piece, 0, near).start()
+
     bits = ((x, y), (y, x))
     partners = ((beside, across), (across, beside))
 
@@ -1033,125 +1155,24 @@
                 copy.wait_recv()
             (small_out, tiny_out)[n][...] = (arrived[3] + arrived[4]) + (arrived[5] + arrived[6])
 
-    inner = upstream_in[...].astype(jnp.float32)
-    slope_rows = jnp.concatenate([slopes[e // 4, e % 2, pl.ds((e // 2) % 2, 1), :] for e in range(16)], axis=0)
-    soft_slope = slope_rows * live[...].astype(jnp.float32)
-    soft_t = soft[...]
-    dlogits = soft_t * (soft_slope - jnp.sum(soft_t * soft_slope, axis=0, keepdims=True))
-    dlogits = dlogits.astype(jnp.bfloat16)
-    small_sum[0] = jnp.zeros(small_sum.shape[1:], jnp.float32)
-    small_sum[0, pl.ds(0, 16), :] = contract(dlogits, moe_in[...], 1, 0)
-    small_sum[0, pl.ds(18, 1), pl.ds(0, 128)] = counts[...]
-    dmoe_in = back[...] + contract(dlogits, router[...], 0, 0)
-    mid = middle[...]
-    output[...] = (mid + combined[...]).astype(jnp.bfloat16)
-    inverse = lax.rsqrt(jnp.mean(mid * mid, axis=1, keepdims=True) + EPSILON)
-    small_sum[0, pl.ds(17, 1), :] = jnp.sum(dmoe_in * mid * inverse, axis=0, keepdims=True)
-    scaled = dmoe_in * moe_gain[...]
-    dmiddle = inner + inverse * (
-        scaled - mid * inverse * inverse * jnp.mean(scaled * mid, axis=1, keepdims=True)
-    )
-    input_grad[...] = dmiddle
-    dattn = dmiddle.astype(jnp.bfloat16)
-
-    def weight_grad(i, left, right):
-        for r in range(4):
-            rows = contract(left[:, pl.ds(r * 256, 256)], right, 0, 0).astype(jnp.bfloat16)
-            grads[i][pl.ds(r * 16, 16)] = rows.reshape(16, 16, 512)
-
-    small_stage(0, 0)
-    weight_grad(0, mixed, dattn[:, :512])
-    stage(0, 0)
-    weight_grad(1, mixed, dattn[:, 512:])
-    stage(1, 0)
-    loads[1].wait()
-    mixed_slope[...] = contract(dattn, w_out[...], 1, 1).astype(jnp.bfloat16)
-    for g in range(8):
-        keys[g] = key_value[:, pl.ds(g * 64, 64)]
-        values[g] = key_value[:, pl.ds(512 + g * 64, 64)]
-    scale = HEAD_SIZE ** (-0.5)
-
-    def group(g, carry):
-        columns = pl.ds(pl.multiple_of(g * 128, 128), 128)
-        key_g, value_g = keys[g], values[g]
-        query_pair, slope_pair = query[:, columns], mixed_slope[:, columns]
-        key_slope = jnp.zeros((256, 64), jnp.float32)
-        value_slope = jnp.zeros((256, 64), jnp.float32)
-        query_slopes = []
-        for r in (0, 1):
-            query_h, slope_h = query_pair[:, r * 64 : r * 64 + 64], slope_pair[:, r * 64 : r * 64 + 64]
-            scores = contract(query_h, key_g, 1, 1) * scale + bias[...]
-            weights = jnp.exp(scores - jnp.max(scores, axis=1, keepdims=True))
-            probs = weights / jnp.sum(weights, axis=1, keepdims=True)
-            prob_slope = contract(slope_h, value_g, 1, 1)
-            value_slope = value_slope + contract(probs.astype(jnp.bfloat16), slope_h, 0, 0)
-            delta = jnp.sum(probs * prob_slope, axis=1, keepdims=True)
-            score_slope = (probs * (prob_slope - delta)).astype(jnp.bfloat16)
-            query_slopes.append(contract(score_slope, key_g, 1, 0) * scale)
-            key_slope = key_slope + contract(score_slope, query_h, 0, 0) * scale
-        pair = turn(jnp.concatenate(query_slopes, axis=1), cosine[...], -sine[...])
-        query_slope[:, columns] = pair.astype(jnp.bfloat16)
-        key_slopes[g] = key_slope
-        value_slopes[g] = value_slope
-        return carry
-
-    stage(0, 1)
-    stage(1, 1)
-    small_stage(0, 1)
-    lax.fori_loop(0, 5, group, 0)
-    small_stage(0, 2)
-    stage(0, 2)
-    stage(1, 2)
-    lax.fori_loop(5, 8, group, 0)
-    small_stage(0, 3)
-    stage(0, 3)
-    stage(1, 3)
-    loads[2].wait()
-    loads[3].wait()
-    loads[4].wait()
-    for n in (0, 1):
-        weight_grad(2 + n, normed, query_slope[:, n * 512 : n * 512 + 512])
-        stage(2 + n, 0)
-    key_slope = jnp.concatenate(
-        [
-            turn(jnp.concatenate([key_slopes[2 * p], key_slopes[2 * p + 1]], axis=1), cosine[...], -sine[...])
-            for p in range(4)
-        ],
-        axis=1,
-    ).astype(jnp.bfloat16)
-    weight_grad(4, normed, key_slope)
-    stage(4, 0)
-    value_slope = jnp.concatenate(
-        [jnp.concatenate([value_slopes[2 * p], value_slopes[2 * p + 1]], axis=1) for p in range(4)], axis=1
-    ).astype(jnp.bfloat16)
-    weight_grad(5, normed, value_slope)
-    stage(5, 0)
-    todo = list(TAIL_ORDER)
-
-    def proceed(steps):
-        for _ in range(min(steps, len(todo))):
-            stage(*todo.pop(0))
-
-    proceed(6)
-    dnormed = contract(query_slope[...], w_query[...], 1, 1)
-    dnormed = dnormed + contract(key_slope, w_key[...], 1, 1)
-    dnormed = dnormed + contract(value_slope, w_value[...], 1, 1)
-    start = tokens[...].astype(jnp.float32)
-    inverse = lax.rsqrt(jnp.mean(start * start, axis=1, keepdims=True) + EPSILON)
-    gain_slope = jnp.sum(dnormed * start * inverse, axis=0, keepdims=True)
-    for r in range(8):
-        tiny_sum[0, pl.ds(r, 1), :] = gain_slope[:, r * 128 : r * 128 + 128]
-    scaled = dnormed * attn_gain[...]
-    input_grad[...] += inverse * (
-        scaled - start * inverse * inverse * jnp.mean(scaled * start, axis=1, keepdims=True)
-    )
-    small_stage(1, 0)
-    proceed(4)
-    small_stage(1, 1)
-    proceed(4)
-    small_stage(1, 2)
-    small_stage(0, 4)
-    loads[5].wait()
+    for tick in range(count + 8):
+        for i in range(count):
+            if tick == i:
+                loads[i].wait()
+            if 0 <= tick - i <= 8:
+                stage(i, tick - i)
+        if tick == 0:
+            loads[6].wait()
+            loads[8].wait()
+        if tick in AGAIN_AT:
+            part = 2 * AGAIN_AT.index(tick)
+            again_copies[part].start()
+            again_copies[part + 1].start()
+        line_stage(tick)
+        if SMALL_AT <= tick <= SMALL_AT + 4:
+            small_stage(0, tick - SMALL_AT)
+            small_stage(1, tick - SMALL_AT)
+    loads[7].wait()
     for copy in again_copies:
         copy.wait_recv()
     for a, target in enumerate((gate_grad, up_grad, down_grad)):
@@ -1162,11 +1183,33 @@
                 target[columns, :] = summed.T
             else:
                 target[:, columns] = summed
-    proceed(4)
-    small_stage(1, 3)
-    proceed(4)
-    small_stage(1, 4)
-    proceed(len(todo))
+
+    def finish(slots):
+        for slot in slots:
+            for piece in range(4):
+                line_wait(slot, piece)
+
+        def body(u, carry):
+            at = pl.ds(pl.multiple_of(u * 32, 32), 32)
+            value = weighted[z, at, :].astype(jnp.float32)
+            for slot in slots:
+                value = value + from_line[slot, at, :].astype(jnp.float32)
+            output[at, :] = (middle_rows[at, :] + value).astype(jnp.bfloat16)
+            return carry
+
+        lax.fori_loop(0, 8, body, 0)
+
+    @pl.when(middle)
+    def _():
+        finish((0, 1))
+
+    @pl.when(edge)
+    def _():
+        finish((0, 1, 2))
+
+    for block in (near, far, last):
+        for piece in range(4):
+            line_copy(block, piece, 0, near).wait_send()
     for key_of, made in copies.items():
         for copy in made:
             if key_of[1] == 8:
@@ -1177,61 +1220,55 @@
         copy.wait_send()
 
 
-def tail_part(operands, weights, again, own):
-    tokens, model_dim = operands[0].shape
-    narrow = weights[1].shape[1]
+def sum_part(wide, small, tiny, again, own, weighted, middle):
+    model_dim = small.shape[1]
     vmem, anywhere = pl.BlockSpec(memory_space=pltpu.VMEM), pl.BlockSpec(memory_space=pl.ANY)
     f32, bf16, dma = jnp.float32, jnp.bfloat16, pltpu.SemaphoreType.DMA
-    widths = (model_dim, model_dim, narrow, narrow)
     leads = ((64,), (32,), (32,), (64,), (2, 8), (2, 4), (2, 3))
     shape = jax.ShapeDtypeStruct
     width = own.shape[1]
+    units = [g.reshape(64, UNIT, model_dim) for g in wide]
     out = pl.pallas_call(
-        tail_kernel,
+        sum_kernel,
         out_shape=[
-            shape((tokens, model_dim), bf16),
-            shape((tokens, model_dim), f32),
-            *[shape((64, UNIT, w), bf16) for w in widths],
-            shape((24, model_dim), f32),
-            shape((8, 128), f32),
+            shape(middle.shape, bf16),
+            *[shape(u.shape, bf16) for u in units],
+            shape(small.shape, f32),
+            shape(tiny.shape, f32),
             shape((model_dim, width), f32),
             shape((model_dim, width), f32),
             shape((width, model_dim), f32),
         ],
-        in_specs=[vmem] * len(operands) + [anywhere] * 6,
-        out_specs=[vmem, vmem] + [anywhere] * 4 + [vmem] * 5,
+        in_specs=[vmem] * 2 + [anywhere] * 6 + [vmem],
+        out_specs=[vmem] + [anywhere] * 3 + [vmem] * 5,
         scratch_shapes=[
-            *[pltpu.VMEM(w.shape, bf16) for w in weights],
-            pltpu.VMEM((8, tokens, HEAD_SIZE), bf16),
-            pltpu.VMEM((8, tokens, HEAD_SIZE), bf16),
-            pltpu.VMEM((8, tokens, HEAD_SIZE), f32),
-            pltpu.VMEM((8, tokens, HEAD_SIZE), f32),
-            pltpu.VMEM((tokens, model_dim), bf16),
-            pltpu.VMEM((tokens, model_dim), bf16),
             pltpu.VMEM(again.shape, bf16),
             pltpu.VMEM(again.shape, bf16),
             pltpu.VMEM(own.shape, f32),
+            pltpu.VMEM(weighted.shape, bf16),
+            pltpu.VMEM((3, *middle.shape), bf16),
             *[pltpu.VMEM((*lead, UNIT, 512), bf16) for lead in leads for _ in range(6)],
-            pltpu.VMEM((4, 24, model_dim), f32),
-            pltpu.VMEM((7, 24, model_dim), f32),
-            pltpu.VMEM((4, 8, 128), f32),
-            pltpu.VMEM((7, 8, 128), f32),
+            pltpu.VMEM((4, *small.shape), f32),
+            pltpu.VMEM((7, *small.shape), f32),
+            pltpu.VMEM((4, *tiny.shape), f32),
+            pltpu.VMEM((7, *tiny.shape), f32),
             dma((6, 22)),
             dma((6, 22)),
             dma((2, 6)),
             dma((2, 6)),
             dma((6,)),
-            dma((6,)),
-            dma((2,)),
-            dma((2,)),
+            dma((9,)),
+            dma((2, 3)),
+            dma((2, 3)),
+            dma((4, 4)),
+            dma((3, 4)),
         ],
         compiler_params=pltpu.CompilerParams(
             collective_id=0, has_side_effects=True, vmem_limit_bytes=60 << 20
         ),
-        name="tail_part",
-    )(*operands, *weights, again, own)
-    grads = [o.reshape(-1, o.shape[2]).astype(jnp.float32) for o in out[2:6]]
-    return (out[0], out[1], grads, out[6], out[7], out[8:11])
+        name="sum_part",
+    )(small, tiny, *units, again, own, weighted, middle)
+    return out[0], [o.reshape(model_dim, model_dim) for o in out[1:4]], out[4], out[5], out[6:9]
 
 
 def local(
@@ -1257,25 +1294,7 @@
     query_per_key_head = QUERY_HEADS // KEY_VALUE_HEADS
     score_scale = HEAD_SIZE ** (-0.5)
     if lax.axis_size("ep") == 16 and lax.axis_size("hs") == 2:
-        attention_weights = (w_query, key_weight, value_weight, w_out)
-        (
-            rows,
-            normed_rows,
-            query_rows,
-            key_value,
-            mixed,
-            middle,
-            cosine,
-            sine,
-            bias,
-            soft,
-            counts,
-            combined,
-            back,
-            slopes,
-            own,
-            again,
-        ) = expert_part(
+        middle, input_grad, out_w_grad, query_w_grad, side_grad, small, tiny, own, again, weighted = expert_part(
             segment_ids,
             live_mask,
             routes,
@@ -1283,43 +1302,24 @@
             moe_gain,
             router,
             tokens,
-            attention_weights,
+            (w_query, key_weight, value_weight, w_out),
             cotangent,
             w_gate[0],
             w_up[0],
             w_down[0],
         )
-        operands = (
-            tokens,
-            normed_rows,
-            query_rows,
-            key_value,
-            mixed,
-            middle,
-            rows,
-            cotangent,
-            combined,
-            back,
-            slopes,
-            soft,
-            live_mask,
-            counts,
-            router.T,
-            cosine,
-            sine,
-            bias,
-            attn_gain[None],
-            moe_gain[None],
+        output, wide, small, tiny, expert_grads = sum_part(
+            (out_w_grad, query_w_grad, side_grad), small, tiny, again, own, weighted, middle
         )
-        output, input_grad, grads, small, tiny, expert_grads = tail_part(operands, attention_weights, again, own)
+        narrow = key_weight.shape[1]
         return (
             output,
             input_grad,
             tiny.reshape(model_dim),
-            grads[1],
-            grads[2],
-            grads[3],
-            grads[0],
+            wide[1].astype(jnp.float32),
+            wide[2][:, :narrow].astype(jnp.float32),
+            wide[2][:, narrow:].astype(jnp.float32),
+            wide[0].astype(jnp.float32),
             small[17],
             small[:experts_all].T,
             *[g[None] for g in expert_grads],

time: 299 us -> 286 us (0.957)
  Pallas kernels: 279 us -> 267 us
    pallas_call x2, Pallas kernels: 279 us -> 267 us  [the longest x1 163 us: expert_part(): pl.pallas_call(expert_kernel, out_shape=[shape(block, f32), shape(block,...]
where the time goes in v7:
time: 286 us
  Pallas kernels  267 us (93%)
  other arithmetic  10.2 us (4%)
  local copies, waits for them, and re-layouts  8.12 us (3%)
    pallas_call x1, Pallas kernels, expert_part(): pl.pallas_call(expert_kernel, out_shape=[shape(block, f32), shape(block,...  163 us
    pallas_call x1, Pallas kernels, sum_part(): pl.pallas_call(sum_kernel, out_shape=[shape(middle.shape, bf16), *[shape(...  103 us

profile of v7, /device:TPU:0, one launch (start us, length us, event | category | flops | bytes accessed | tf_op | source)
XLA Modules:
  0.0 285.5 jit_solution(14449797508986582073)
XLA Ops:
  0.7 163.4 %expert_part.1 = (f32[256,1024]{1,0:T(8,128)}, f32[256,1024]{1,0:T(8,128)}, bf16[1024,1024]{1,0:T(8,128)(2,1)}, bf16[1024,1024]{1,0:T(8,128)(2,1)}, bf16[1024,10...) custom-call(s32[1,256]{1,0:T(1,128)} %segment.1, ...), custom_call_target="tpu_custom_call" | custom-call | tf_op jit(solution)/shard_map/expert_part/pallas_call | solution.py:833
  164.1 103.1 %sum_part.1 = (bf16[256,1024]{1,0:T(8,128)(2,1)}, bf16[64,16,1024]{2,1,0:T(8,128)(2,1)}, bf16[64,16,1024]{2,1,0:T(8,128)(2,1)}, bf16[64,16,1024]{2,1,0:T(8,128)(...) custom-call(f32[24,1024]{1,0:T(8,128)} %get-tuple-element.32.small, ...), custom_call_target="tpu_custom_call" | custom-call | tf_op jit(solution)/shard_map/sum_part/pallas_call | solution.py:1231
  267.2 1.2 convert_bitcast_fusion
  268.4 1.4 slice.17
  269.7 1.5 slice_bitcast_fusion
  271.2 0.0 copy-start
  271.2 0.0 copy-start.1
  271.2 4.3 %slice_convert_fusion = (f32[1024,512]{1,0:T(8,128)}, f32[1024,512]{1,0:T(8,128)}) fusion(bf16[1024,1024]{1,0:T(8,128)(2,1)} %bitcast.26), kind=kLoop, calls=%fused_computation.2 | loop fusion | flops 1048576 | bytes 6291456 | tf_op jit(solution)/shard_map/convert_element_type | solution.py:1321
  275.5 0.0 copy-done
  275.5 0.0 copy-done.1
  275.5 0.0 copy-start.6
  275.5 0.0 copy-start.2
  275.5 4.7 %bitcast_convert_fusion = (f32[1024,1024]{1,0:T(8,128)}, f32[1024,1024]{1,0:T(8,128)}) fusion(bf16[64,16,1024]{2,1,0:T(8,128)(2,1)S(1)} %copy-done, bf16[64,16,1024]{2,1,0:T(8,128)(2,1)S(1)} %copy-done.1), kind=kLoop, calls=%fused_computation | loop fusion | flops 2097152 | bytes 12582912 | tf_op jit(solution)/shard_map/convert_element_type | solution.py:1322
  280.2 0.0 copy-start.7
  280.2 0.0 copy-start.5
  280.2 0.0 copy-done.6
  280.2 0.8 copy.35
  281.0 0.0 copy-done.2
  281.0 0.0 copy-start.4
  281.0 1.0 copy.36
  282.0 0.0 copy-done.7
  282.0 0.6 copy.37
  282.6 0.0 copy-done.5
  282.6 0.0 copy-start.3
  282.6 1.0 copy.38
  283.6 0.0 copy-done.4
  283.6 1.0 copy.39
  284.6 0.0 copy-done.3
  284.6 1.0 copy.40
Async XLA Ops:
  271.2 4.3 %copy-start = (bf16[64,16,1024]{2,1,0:T(8,128)(2,1)S(1)}, bf16[64,16,1024]{2,1,0:T(8,128)(2,1)}, u32[]{:S(2)}) copy-start(bf16[64,16,1024]{2,1,0:T(8,128)(2,1)} %get-tuple-element.46) | copy-start | bytes 6291460
  271.2 4.3 %copy-start.1 = (bf16[64,16,1024]{2,1,0:T(8,128)(2,1)S(1)}, bf16[64,16,1024]{2,1,0:T(8,128)(2,1)}, u32[]{:S(2)}) copy-start(bf16[64,16,1024]{2,1,0:T(8,128)(2,1)} %get-tuple-element.44) | copy-start | bytes 6291460
  275.5 4.7 %copy-start.6 = (bf16[256,1024]{1,0:T(8,128)(2,1)S(1)}, bf16[256,1024]{1,0:T(8,128)(2,1)}, u32[]{:S(2)}) copy-start(bf16[256,1024]{1,0:T(8,128)(2,1)} %get-tuple-element.68) | copy-start | bytes 1572868
  275.5 5.5 %copy-start.2 = (f32[256,1024]{1,0:T(8,128)S(1)}, f32[256,1024]{1,0:T(8,128)}, u32[]{:S(2)}) copy-start(f32[256,1024]{1,0:T(8,128)} %get-tuple-element.69) | copy-start | bytes 3145732
  280.2 1.8 copy-start.7
  280.2 2.4 copy-start.5
  281.0 2.5 copy-start.4
  282.6 1.9 copy-start.3

commit v8 on v7

--- a/solution.py
+++ b/solution.py
@@ -233,7 +233,6 @@
     middle = (z == 1) | (z == 2)
     edge = (z == 0) | (z == 3)
     sibling, beside, across = device(z, x, 1 - c, y), device(z, 1 - x, c, y), device(z, x, c, 1 - y)
-    corner = device(z, 1 - x, c, 1 - y)
     line = [((z + k) % 4, (c + d) % 2) for k in range(4) for d in range(2) if k or d]
 
     def chip(k):
@@ -267,7 +266,7 @@
             head_loads.append(pltpu.make_async_copy(source.at[rows, :], target, head_sem.at[1 + r * 4 + n]))
     for copy in (own, *weights_own, *head_loads):
         copy.start()
-    greet([device(a, x, b, y) for a, b in line] + [beside, across, corner])
+    greet([device(a, x, b, y) for a, b in line] + [beside, across])
 
     def gather(s, block, slot, peer):
         piece = streams.at[s, block, c]
@@ -290,14 +289,25 @@
     weight_copies = []
     for a, held in enumerate((w_gate, w_up, w_down)):
         weights_own[a].wait()
-        for n, peer in enumerate((across, beside, corner)):
+        for n, peer in enumerate((across, beside)):
             piece = held.at[x, y]
             weight_copies.append(
                 remote(piece, piece, weight_send.at[n, a], weight_recv.at[x, y, a], peer)
             )
-    for n in range(3):
-        for a in range(3):
-            weight_copies[a * 3 + n].start()
+    for copy in weight_copies:
+        copy.start()
+    upper, lower = pl.ds(0, 128), pl.ds(128, 128)
+
+    def relay(n, expert, group, peer):
+        if n < 2:
+            piece = (w_gate, w_up)[n].at[expert, group]
+        else:
+            piece = w_down.at[expert, group, (upper, lower)[n - 2], :]
+        return remote(piece, piece, weight_send.at[2, n], weight_recv.at[expert, group, n], peer)
+
+    def corner_here():
+        for n in range(4):
+            relay(n, 1 - x, 1 - y, beside).wait_recv()
 
     def weights_here(expert, group):
         for a, held in enumerate((w_gate, w_up, w_down)):
@@ -422,10 +432,19 @@
         gather(0, z, 0, device(near, x, c, y)).wait_send()
         gather(0, z, 1, device(far, x, c, y)).start()
 
+    @pl.when(middle)
+    def _():
+        handle(2, (1,))
+        handle(3, (1,))
+
     handle(1, (0,))
     for a, b in line:
         pltpu.make_async_copy(gates.at[a, b], gates.at[a, b], gate_recv.at[a, b]).wait()
     weights_here(x, 1 - y)
+    weights_here(1 - x, y)
+    relays = [relay(n, x, 1 - y, beside) for n in (0, 2)] + [relay(n, 1 - x, y, across) for n in (1, 3)]
+    for copy in relays:
+        copy.start()
 
     def compute(expert, block, core):
         diagonal = lax.broadcasted_iota(jnp.int32, (256, 256), 0) == lax.broadcasted_iota(jnp.int32, (256, 256), 1)
@@ -513,18 +532,25 @@
         expert = x + (code // 4) * (1 - 2 * x)
         block, core = chip(k), (c + i + again) % 2
 
-        @pl.when((i == 2) & middle | (i == 4) & edge)
+        @pl.when((i == 2) & middle)
+        def _():
+            handle(2, (0,))
+
+        @pl.when((i == 4) & middle)
+        def _():
+            handle(3, (0,))
+
+        @pl.when((i == 4) & edge)
         def _():
             handle(2)
 
-        @pl.when((i == 4) & middle | (i == 12) & edge)
+        @pl.when((i == 12) & edge)
         def _():
             handle(3)
 
         @pl.when((i == 8) & middle | (i == 6) & edge)
         def _():
-            weights_here(1 - x, y)
-            weights_here(1 - x, 1 - y)
+            corner_here()
 
         @pl.when((i % 2 == 1) & (again == 0))
         def _():
@@ -630,7 +656,7 @@
             for k in (1, 3):
                 gather(s, chip(k), 2 + (k + 1) // 2, device(far, x, c, y)).wait_send()
 
-    for copy in (*gate_copies, *weight_copies):
+    for copy in (*gate_copies, *weight_copies, *relays):
         copy.wait_send()
 
     def query_weight(r):
@@ -874,8 +900,8 @@
             dma((4, 2)),
             dma((7,)),
             dma((4, 2)),
-            dma((3, 3)),
-            dma((2, 2, 3)),
+            dma((3, 4)),
+            dma((2, 2, 4)),
             dma((2, 4)),
             dma((2, 4)),
             dma((2, 4)),
@@ -904,6 +930,7 @@
     )
 
 
+ROWS_AT_ONCE = 256
 AGAIN_AT = (0, 4, 8)
 COMBINE_AT = 6
 SMALL_AT = 9
@@ -1271,6 +1298,90 @@
     return out[0], [o.reshape(model_dim, model_dim) for o in out[1:4]], out[4], out[5], out[6:9]
 
 
+def finish_kernel(
+    out_in,
+    query_in,
+    side_in,
+    small,
+    output_in,
+    input_grad_in,
+    gate_in,
+    up_in,
+    down_in,
+    tiny_in,
+    out_grad,
+    query_grad,
+    key_grad,
+    value_grad,
+    router_grad,
+    gain_grad,
+    counts,
+    output,
+    input_grad,
+    gate_grad,
+    up_grad,
+    down_grad,
+    tiny,
+):
+    for source, target in (
+        (input_grad_in, input_grad),
+        (gate_in, gate_grad),
+        (up_in, up_grad),
+        (down_in, down_grad),
+        (output_in, output),
+    ):
+        target[...] = source[...]
+
+    @pl.when(pl.program_id(0) == 0)
+    def _():
+        tiny[...] = tiny_in[...]
+        router_grad[...] = small[pl.ds(0, 16), :]
+        for r in range(8):
+            gain_grad[pl.ds(r, 1), :] = small[pl.ds(17, 1), pl.ds(r * 128, 128)]
+        counts[...] = small[pl.ds(18, 1), pl.ds(0, 16)].astype(jnp.int32)
+
+    out_grad[...] = out_in[...].astype(jnp.float32)
+    query_grad[...] = query_in[...].astype(jnp.float32)
+    key_grad[...] = side_in[:, :512].astype(jnp.float32)
+    value_grad[...] = side_in[:, 512:].astype(jnp.float32)
+
+
+def finish_part(wide, small, output, input_grad, expert_grads, tiny):
+    model_dim = small.shape[1]
+    narrow = model_dim // 2
+    f32, shape = jnp.float32, jax.ShapeDtypeStruct
+    steps = model_dim // ROWS_AT_ONCE
+    full = pl.BlockSpec((ROWS_AT_ONCE, model_dim), lambda i: (i, 0))
+    part = pl.BlockSpec((ROWS_AT_ONCE, narrow), lambda i: (i, 0))
+
+    def fixed(*dims):
+        return pl.BlockSpec(dims, lambda i: (0, 0))
+
+    def rows_of(array):
+        return pl.BlockSpec((array.shape[0] // steps, array.shape[1]), lambda i: (i, 0))
+
+    raw = (output, input_grad, *expert_grads, tiny)
+    raw_specs = [rows_of(r) for r in raw[:5]] + [fixed(8, 128)]
+    return pl.pallas_call(
+        finish_kernel,
+        grid=(steps,),
+        out_shape=[
+            shape((model_dim, model_dim), f32),
+            shape((model_dim, model_dim), f32),
+            shape((model_dim, narrow), f32),
+            shape((model_dim, narrow), f32),
+            shape((16, model_dim), f32),
+            shape((8, 128), f32),
+            shape((1, 16), jnp.int32),
+            *[shape(r.shape, r.dtype) for r in raw],
+        ],
+        in_specs=[full] * 3 + [fixed(*small.shape)] + raw_specs,
+        out_specs=[full, full, part, part, fixed(16, model_dim), fixed(8, 128), fixed(1, 16)] + raw_specs,
+        compiler_params=pltpu.CompilerParams(vmem_limit_bytes=62 << 20),
+        name="finish_part",
+    )(*wide, small, *raw)
+
+
 def local(
     tokens,
     segment_ids,
@@ -1311,19 +1422,31 @@
         output, wide, small, tiny, expert_grads = sum_part(
             (out_w_grad, query_w_grad, side_grad), small, tiny, again, own, weighted, middle
         )
-        narrow = key_weight.shape[1]
+        (
+            out_w_grad,
+            query_w_grad,
+            key_w_grad,
+            value_w_grad,
+            router_w_grad,
+            moe_gain_grad,
+            counts,
+            output,
+            input_grad,
+            *expert_grads,
+            tiny,
+        ) = finish_part(wide, small, output, input_grad, expert_grads, tiny)
         return (
             output,
             input_grad,
             tiny.reshape(model_dim),
-            wide[1].astype(jnp.float32),
-            wide[2][:, :narrow].astype(jnp.float32),
-            wide[2][:, narrow:].astype(jnp.float32),
-            wide[0].astype(jnp.float32),
-            small[17],
-            small[:experts_all].T,
+            query_w_grad,
+            key_w_grad,
+            value_w_grad,
+            out_w_grad,
+            moe_gain_grad.reshape(model_dim),
+            router_w_grad.T,
             *[g[None] for g in expert_grads],
-            small[18, :experts_all].astype(jnp.int32),
+            counts.reshape(experts_all),
         )
     segment = segment_ids[0]
     live_row = live_mask[0]

time: 286 us -> 279 us (0.976)
  Pallas kernels: 267 us -> 278 us
  other arithmetic: 10.2 us -> 0 us
  local copies, waits for them, and re-layouts: 8.12 us -> 0 us
    pallas_call x0 -> x1, Pallas kernels: none -> 11.3 us  [finish_part(): pl.pallas_call(finish_kernel, grid=(steps,), out_shape=[shape((model_dim,...]
    convert_element_type x3 -> x0, other arithmetic: 10.2 us -> none  [the longest x1 4.72 us: local(): wide[0].astype(jnp.float32)]
    pallas_call x1, Pallas kernels: 163 us -> 158 us  [expert_part(): pl.pallas_call(expert_kernel, out_shape=[shape(block, f32), shape(block,...]
    unnamed x22 -> x0, local copies, waits for them, and re-layouts: 5.3 us -> none
    pallas_call x1, Pallas kernels: 103 us -> 108 us  [sum_part(): pl.pallas_call(sum_kernel, out_shape=[shape(middle.shape, bf16), *[shape(...]
where the time goes in v8:
time: 279 us; the launch traced here: 278 us
  Pallas kernels  278 us (100%)
    pallas_call x1, Pallas kernels, expert_part(): pl.pallas_call(expert_kernel, out_shape=[shape(block, f32), shape(block,...  158 us
    pallas_call x1, Pallas kernels, sum_part(): pl.pallas_call(sum_kernel, out_shape=[shape(middle.shape, bf16), *[shape(...  108 us
    pallas_call x1, Pallas kernels, finish_part(): pl.pallas_call(finish_kernel, grid=(steps,), out_shape=[shape((model_dim,...  11.3 us

profile of v8, /device:TPU:0, one launch (start us, length us, event | category | flops | bytes accessed | tf_op | source)
XLA Modules:
  0.0 278.4 jit_solution(8169292617381151404)
XLA Ops:
  0.7 158.1 %expert_part.1 = (f32[256,1024]{1,0:T(8,128)}, f32[256,1024]{1,0:T(8,128)}, bf16[1024,1024]{1,0:T(8,128)(2,1)}, bf16[1024,1024]{1,0:T(8,128)(2,1)}, bf16[1024,10...) custom-call(s32[1,256]{1,0:T(1,128)} %segment.1, ...), custom_call_target="tpu_custom_call" | custom-call | tf_op jit(solution)/shard_map/expert_part/pallas_call | solution.py:859
  158.7 108.2 %sum_part.1 = (bf16[256,1024]{1,0:T(8,128)(2,1)}, bf16[64,16,1024]{2,1,0:T(8,128)(2,1)}, bf16[64,16,1024]{2,1,0:T(8,128)(2,1)}, bf16[64,16,1024]{2,1,0:T(8,128)(...) custom-call(f32[24,1024]{1,0:T(8,128)} %get-tuple-element.45.small, ...), custom_call_target="tpu_custom_call" | custom-call | tf_op jit(solution)/shard_map/sum_part/pallas_call | solution.py:1258
  267.0 11.3 %finish_part.1 = (f32[1024,1024]{1,0:T(8,128)}, f32[1024,1024]{1,0:T(8,128)}, f32[1024,512]{1,0:T(8,128)}, f32[1024,512]{1,0:T(8,128)}, f32[16,1024]{1,0:T(8,128...) custom-call(bf16[1024,1024]{1,0:T(8,128)(2,1)} %bitcast.20, ...), custom_call_target="tpu_custom_call" | custom-call | tf_op jit(solution)/shard_map/finish_part/pallas_call | solution.py:1365

commit v9 on v8

--- a/solution.py
+++ b/solution.py
@@ -415,7 +415,8 @@
     count = jnp.sum(jnp.where(routed, live_row, 0.0), axis=1, keepdims=True)
     square = lax.broadcasted_iota(jnp.int32, (16, 128), 0) == lax.broadcasted_iota(jnp.int32, (16, 128), 1)
     small[...] = jnp.zeros((24, 1024), jnp.float32)
-    small[pl.ds(18, 1), pl.ds(0, 128)] = jnp.sum(jnp.where(square, count, 0.0), axis=0, keepdims=True)
+    tiny[pl.ds(8, 8), :] = jnp.zeros((8, 128), jnp.float32)
+    tiny[pl.ds(8, 1), :] = jnp.sum(jnp.where(square, count, 0.0), axis=0, keepdims=True)
     gate_copies = [
         remote(
             gates_in.at[a, b], gates.at[z, c], gate_send.at[n], gate_recv.at[z, c], device(a, x, b, y)
@@ -865,7 +866,7 @@
             shape((model_dim, model_dim), bf16),
             shape((model_dim, model_dim), bf16),
             shape((24, model_dim), f32),
-            shape((8, 128), f32),
+            shape((16, 128), f32),
             shape((3, width, model_dim), f32),
             shape((2, 3, width, model_dim // 2), bf16),
             shape((4, *block), bf16),
@@ -979,7 +980,7 @@
     loads.append(pltpu.make_async_copy(weighted_in, weighted, load_sem.at[8]))
     for copy in loads:
         copy.start()
-    small_sum[0] = small[...]
+    small_sum[0] = small[...].astype(jnp.bfloat16)
     tiny_sum[0] = tiny[...]
     greet([sibling, beside, across] + along)
     again_copies = [
@@ -1170,7 +1171,8 @@
             small_push(0, sibling, 0, 0)
         if step in (1, 2, 3):
             copies[n, "s", step - 1][0].wait_recv()
-            total[step] = total[step - 1] + arrived[step - 1]
+            value = total[step - 1].astype(jnp.float32) + arrived[step - 1].astype(jnp.float32)
+            total[step] = value.astype(total.dtype)
         if step in (1, 2):
             small_push(step, (beside, across)[step - 1], step, step)
         if step == 3:
@@ -1180,7 +1182,8 @@
         if step == 4:
             for copy in copies[n, "s", 3]:
                 copy.wait_recv()
-            (small_out, tiny_out)[n][...] = (arrived[3] + arrived[4]) + (arrived[5] + arrived[6])
+            parts = [arrived[3 + k].astype(jnp.float32) for k in range(4)]
+            (small_out, tiny_out)[n][...] = (parts[0] + parts[1]) + (parts[2] + parts[3])
 
     for tick in range(count + 8):
         for i in range(count):
@@ -1275,8 +1278,8 @@
             pltpu.VMEM(weighted.shape, bf16),
             pltpu.VMEM((3, *middle.shape), bf16),
             *[pltpu.VMEM((*lead, UNIT, 512), bf16) for lead in leads for _ in range(6)],
-            pltpu.VMEM((4, *small.shape), f32),
-            pltpu.VMEM((7, *small.shape), f32),
+            pltpu.VMEM((4, *small.shape), bf16),
+            pltpu.VMEM((7, *small.shape), bf16),
             pltpu.VMEM((4, *tiny.shape), f32),
             pltpu.VMEM((7, *tiny.shape), f32),
             dma((6, 22)),
@@ -1334,11 +1337,11 @@
 
     @pl.when(pl.program_id(0) == 0)
     def _():
-        tiny[...] = tiny_in[...]
+        tiny[...] = tiny_in[pl.ds(0, 8), :]
         router_grad[...] = small[pl.ds(0, 16), :]
         for r in range(8):
             gain_grad[pl.ds(r, 1), :] = small[pl.ds(17, 1), pl.ds(r * 128, 128)]
-        counts[...] = small[pl.ds(18, 1), pl.ds(0, 16)].astype(jnp.int32)
+        counts[...] = tiny_in[pl.ds(8, 1), pl.ds(0, 16)].astype(jnp.int32)
 
     out_grad[...] = out_in[...].astype(jnp.float32)
     query_grad[...] = query_in[...].astype(jnp.float32)
@@ -1361,7 +1364,7 @@
         return pl.BlockSpec((array.shape[0] // steps, array.shape[1]), lambda i: (i, 0))
 
     raw = (output, input_grad, *expert_grads, tiny)
-    raw_specs = [rows_of(r) for r in raw[:5]] + [fixed(8, 128)]
+    raw_specs = [rows_of(r) for r in raw[:5]]
     return pl.pallas_call(
         finish_kernel,
         grid=(steps,),
@@ -1373,10 +1376,11 @@
             shape((16, model_dim), f32),
             shape((8, 128), f32),
             shape((1, 16), jnp.int32),
-            *[shape(r.shape, r.dtype) for r in raw],
+            *[shape(r.shape, r.dtype) for r in raw[:5]],
+            shape((8, 128), f32),
         ],
-        in_specs=[full] * 3 + [fixed(*small.shape)] + raw_specs,
-        out_specs=[full, full, part, part, fixed(16, model_dim), fixed(8, 128), fixed(1, 16)] + raw_specs,
+        in_specs=[full] * 3 + [fixed(*small.shape)] + raw_specs + [fixed(16, 128)],
+        out_specs=[full, full, part, part, fixed(16, model_dim), fixed(8, 128), fixed(1, 16)] + raw_specs + [fixed(8, 128)],
         compiler_params=pltpu.CompilerParams(vmem_limit_bytes=62 << 20),
         name="finish_part",
     )(*wide, small, *raw)

time: 279 us -> 276 us (0.989)
  Pallas kernels: 278 us -> 275 us
where the time goes in v9:
time: 276 us
  Pallas kernels  275 us (100%)
    pallas_call x1, Pallas kernels, expert_part(): pl.pallas_call(expert_kernel, out_shape=[shape(block, f32), shape(block,...  158 us
    pallas_call x1, Pallas kernels, sum_part(): pl.pallas_call(sum_kernel, out_shape=[shape(middle.shape, bf16), *[shape(...  106 us
    pallas_call x1, Pallas kernels, finish_part(): pl.pallas_call(finish_kernel, grid=(steps,), out_shape=[shape((model_dim,...  11.3 us

profile of v9, /device:TPU:0, one launch (start us, length us, event | category | flops | bytes accessed | tf_op | source)
XLA Modules:
  0.0 276.0 jit_solution(15377388937037353435)
XLA Ops:
  0.7 157.8 %expert_part.1 = (f32[256,1024]{1,0:T(8,128)}, f32[256,1024]{1,0:T(8,128)}, bf16[1024,1024]{1,0:T(8,128)(2,1)}, bf16[1024,1024]{1,0:T(8,128)(2,1)}, bf16[1024,10...) custom-call(s32[1,256]{1,0:T(1,128)} %segment.1, ...), custom_call_target="tpu_custom_call" | custom-call | tf_op jit(solution)/shard_map/expert_part/pallas_call | solution.py:860
  158.4 106.1 %sum_part.1 = (bf16[256,1024]{1,0:T(8,128)(2,1)}, bf16[64,16,1024]{2,1,0:T(8,128)(2,1)}, bf16[64,16,1024]{2,1,0:T(8,128)(2,1)}, bf16[64,16,1024]{2,1,0:T(8,128)(...) custom-call(f32[24,1024]{1,0:T(8,128)} %get-tuple-element.45.small, ...), custom_call_target="tpu_custom_call" | custom-call | tf_op jit(solution)/shard_map/sum_part/pallas_call | solution.py:1261
  264.5 11.3 %finish_part.1 = (f32[1024,1024]{1,0:T(8,128)}, f32[1024,1024]{1,0:T(8,128)}, f32[1024,512]{1,0:T(8,128)}, f32[1024,512]{1,0:T(8,128)}, f32[16,1024]{1,0:T(8,128...) custom-call(bf16[1024,1024]{1,0:T(8,128)(2,1)} %bitcast.23, ...), custom_call_target="tpu_custom_call" | custom-call | tf_op jit(solution)/shard_map/finish_part/pallas_call | solution.py:1368

commit v10 on v9

--- a/solution.py
+++ b/solution.py
@@ -933,8 +933,8 @@
 
 ROWS_AT_ONCE = 256
 AGAIN_AT = (0, 4, 8)
-COMBINE_AT = 6
-SMALL_AT = 9
+COMBINE_AT = 9
+SMALL_AT = 6
 
 
 def sum_kernel(

time: 276 us -> 274 us (level)
  Pallas kernels: 275 us -> 271 us
    pallas_call x1, Pallas kernels: 106 us -> 102 us  [sum_part(): pl.pallas_call(sum_kernel, out_shape=[shape(middle.shape, bf16), *[shape(...]
where the time goes in v10:
time: 274 us; the launch traced here: 272 us
  Pallas kernels  271 us (99%)
    pallas_call x1, Pallas kernels, expert_part(): pl.pallas_call(expert_kernel, out_shape=[shape(block, f32), shape(block,...  158 us
    pallas_call x1, Pallas kernels, sum_part(): pl.pallas_call(sum_kernel, out_shape=[shape(middle.shape, bf16), *[shape(...  102 us
    pallas_call x1, Pallas kernels, finish_part(): pl.pallas_call(finish_kernel, grid=(steps,), out_shape=[shape((model_dim,...  11.3 us

profile of v10, /device:TPU:0, one launch (start us, length us, event | category | flops | bytes accessed | tf_op | source)
XLA Modules:
  0.0 271.9 jit_solution(4425633924998165011)
XLA Ops:
  0.7 157.8 %expert_part.1 = (f32[256,1024]{1,0:T(8,128)}, f32[256,1024]{1,0:T(8,128)}, bf16[1024,1024]{1,0:T(8,128)(2,1)}, bf16[1024,1024]{1,0:T(8,128)(2,1)}, bf16[1024,10...) custom-call(s32[1,256]{1,0:T(1,128)} %segment.1, ...), custom_call_target="tpu_custom_call" | custom-call | tf_op jit(solution)/shard_map/expert_part/pallas_call | solution.py:860
  158.4 102.1 %sum_part.1 = (bf16[256,1024]{1,0:T(8,128)(2,1)}, bf16[64,16,1024]{2,1,0:T(8,128)(2,1)}, bf16[64,16,1024]{2,1,0:T(8,128)(2,1)}, bf16[64,16,1024]{2,1,0:T(8,128)(...) custom-call(f32[24,1024]{1,0:T(8,128)} %get-tuple-element.45.small, ...), custom_call_target="tpu_custom_call" | custom-call | tf_op jit(solution)/shard_map/sum_part/pallas_call | solution.py:1261
  260.5 11.3 %finish_part.1 = (f32[1024,1024]{1,0:T(8,128)}, f32[1024,1024]{1,0:T(8,128)}, f32[1024,512]{1,0:T(8,128)}, f32[1024,512]{1,0:T(8,128)}, f32[16,1024]{1,0:T(8,128...) custom-call(bf16[1024,1024]{1,0:T(8,128)(2,1)} %bitcast.23, ...), custom_call_target="tpu_custom_call" | custom-call | tf_op jit(solution)/shard_map/finish_part/pallas_call | solution.py:1368
